TPU v7x, 32 devices: a whole 2x2x4 slice. The times are simulated.
32 devices in a mesh: gx: 8 (over y, x, core), gy: 4 (over z).
Axes of the slice: x: 2, y: 2, z: 4, core: 2. Of those that a mesh axis runs over, the one named last changes fastest.
Arguments:
- slab_tokens: bfloat16 [16, 8, 16, 512], P('gx', None, 'gy'), may hold values from -6 to 6
- cotangent: bfloat16 [16, 8, 16, 512], P('gx', 'gy'), may hold values from -6 to 6
- w_qkv: bfloat16 [1536, 512], replicated, may hold values from -1 to 1
- w_out: bfloat16 [512, 512], replicated, may hold values from -0.75 to 0.75
- logit_scale: float32 [8], replicated, may hold values from 1 to 400
Outputs:
- output: bfloat16 [16, 8, 16, 512], P('gx', 'gy')
- grad_input: bfloat16 [16, 8, 16, 512], P('gx', None, 'gy')
- grad_weights: float32 [2048, 512], P(('gx', 'gy'))
All inputs are finite; a program needn't handle non-finite values.
Results may differ from a plain program's by a relative error of at most 0.011.
The roundings to bfloat16 on the way count: a program that leaves them out, or rounds other values in their place, can miss the bound.
Values may be sent and summed in bfloat16 or wider, within the bound.
No kernel may reach another device: no remote copies, remote signals or barrier semaphores. Data moves between devices by JAX's collectives and lax.ppermute only.
A program may use at most 128 MiB of HBM per device.

v0:
```python
import math

import jax
import jax.numpy as jnp
from jax import lax
from jax.experimental import pallas as pl
from jax.experimental.pallas import tpu as pltpu
from jax.sharding import PartitionSpec as P

D = 512
HEADS = 8
HEAD_DIM = 64
EPSILON = 1e-06
NEGATIVE = -1e30
F32 = jnp.float32
BF16 = jnp.bfloat16

NN = (((1,), (0,)), ((), ()))
NT = (((1,), (1,)), ((), ()))
TN = (((0,), (0,)), ((), ()))


def mm(a, b, dims=NN):
    return lax.dot_general(a, b, dims, preferred_element_type=F32)


def iota(shape, dim):
    return lax.broadcasted_iota(jnp.int32, shape, dim)


def head_sums(values, ones):
    high = values.astype(BF16)
    low = (values - high.astype(F32)).astype(BF16)
    return mm(high, ones) + mm(low, ones)


def select_rows(count, source_of):
    rows = iota((count, 1), 0)
    cols = iota((1, count), 1)
    return (source_of(rows) == cols).astype(F32).astype(BF16)


def main_kernel(
    pos_ref, own_ref, xl_ref, xh_ref, zl_ref, zh_ref, cot_ref, wqkv_ref, wout_ref, scale_ref,
    send_ref, out_ref, gin_ref,
    e_ref, dq_ref, dk_ref, dv_ref, att_ref,
    *, ny, n_gx, n_gy, total_x, total_z,
):
    plane = 8 * ny
    inner = 4 * ny
    qplane = 6 * ny
    tokens = 2 * inner
    yb = ny // n_gy
    for p in range(2):
        e_ref[p, 2 * ny : 6 * ny] = xl_ref[p * inner : (p + 1) * inner]
        e_ref[p + 2, 2 * ny : 6 * ny] = own_ref[p * inner : (p + 1) * inner]
        e_ref[p + 4, 2 * ny : 6 * ny] = xh_ref[p * inner : (p + 1) * inner]
    for p in range(6):
        e_ref[p, 0 : 2 * ny] = zl_ref[p * 2 * ny : (p + 1) * 2 * ny]
        e_ref[p, 6 * ny : 8 * ny] = zh_ref[p * 2 * ny : (p + 1) * 2 * ny]
    x = e_ref[...].reshape(6 * plane, D).astype(F32)
    r = lax.rsqrt(jnp.mean(x * x, axis=-1, keepdims=True) + EPSILON)
    normed = (x * r).astype(BF16)
    ones = (iota((D, 1), 0) // HEAD_DIM == iota((1, D), 1) // HEAD_DIM).astype(F32).astype(BF16)

    k = mm(normed, wqkv_ref[D : 2 * D], NT)
    v = mm(normed, wqkv_ref[2 * D : 3 * D], NT)
    q = mm(normed[plane : 5 * plane], wqkv_ref[0:D], NT)
    scale = scale_ref[...]
    rk = lax.rsqrt(head_sums(k * k, ones) * (1.0 / HEAD_DIM) + EPSILON)
    rq = lax.rsqrt(head_sums(q * q, ones) * (1.0 / HEAD_DIM) + EPSILON)
    kb = (k * rk).astype(BF16)
    vb = v.astype(BF16)
    qf = q * rq * scale

    def cot_source(i):
        px = i // qplane
        rest = i - px * qplane
        pz = rest // ny
        py = rest - pz * ny
        src = py // yb
        return ((src * 4 + px) * yb + (py - src * yb)) * 6 + pz

    cot = mm(select_rows(4 * qplane, cot_source), cot_ref[...])
    upf = mm(cot.astype(BF16), wout_ref[...])

    gx_pos = pos_ref[0]
    gy_pos = pos_ref[1]
    qi = iota((2 * qplane, 1), 0)
    qx = jnp.where(qi >= qplane, 1, 0)
    qr = qi - qx * qplane
    qz = qr // ny
    qy = qr - qz * ny
    kj = iota((1, 4 * plane), 1)
    kx = kj // plane
    kr = kj - kx * plane
    kz = kr // ny
    ky = kr - kz * ny
    dx = kx - qx
    dz = kz - qz
    dy = ky - qy
    near = (dx >= 0) & (dx <= 2) & (dz >= 0) & (dz <= 2) & (dy >= -1) & (dy <= 1)
    gz = gy_pos * 4 - 2 + kz
    z_ok = (gz >= 0) & (gz < total_z)

    for b in range(2):
        gxk = gx_pos * 2 - 2 + 2 * b + kx
        ok = near & (z_ok & (gxk >= 0) & (gxk < total_x))
        bias = jnp.where(ok, 0.0, NEGATIVE)
        q0 = 2 * b * plane + ny
        qblk = jnp.concatenate(
            [qf[q0 : q0 + qplane], qf[q0 + plane : q0 + plane + qplane]], axis=0
        ).astype(BF16)
        kblk = kb[2 * b * plane : (2 * b + 4) * plane]
        vblk = vb[2 * b * plane : (2 * b + 4) * plane]
        ublk = upf[2 * b * qplane : (2 * b + 2) * qplane].astype(BF16)
        own0 = (qplane if b == 0 else 0) + ny
        col0 = 2 * plane if b == 0 else 0
        for h in range(HEADS):
            lanes = slice(h * HEAD_DIM, (h + 1) * HEAD_DIM)
            qh, kh, vh, uh = qblk[:, lanes], kblk[:, lanes], vblk[:, lanes], ublk[:, lanes]
            s = mm(qh, kh, NT) + bias
            w = jnp.exp(s - jnp.max(s, axis=-1, keepdims=True))
            w = w * (1.0 / jnp.sum(w, axis=-1, keepdims=True))
            dp = mm(uh, vh, NT)
            ds = w * (dp - jnp.sum(w * dp, axis=-1, keepdims=True))
            att_ref[b * inner : (b + 1) * inner, lanes] = mm(
                w[own0 : own0 + inner].astype(BF16), vh
            )
            dq_ref[b * inner : (b + 1) * inner, lanes] = mm(
                ds[own0 : own0 + inner].astype(BF16), kh
            )
            dk = mm(ds[:, col0 : col0 + 2 * plane].astype(BF16), qh, TN)
            dv = mm(w[:, col0 : col0 + 2 * plane].astype(BF16), uh, TN)
            if b == 0:
                dk_ref[:, lanes] = dk
                dv_ref[:, lanes] = dv
            else:
                dk_ref[:, lanes] += dk
                dv_ref[:, lanes] += dv

    def own_rows(values, planes, start, first):
        return jnp.concatenate(
            [values[(first + p) * planes + start : (first + p) * planes + start + inner] for p in range(2)],
            axis=0,
        )

    q_o = own_rows(q, plane, 2 * ny, 1)
    rq_o = own_rows(rq, plane, 2 * ny, 1)
    k_o = own_rows(k, plane, 2 * ny, 2)
    rk_o = own_rows(rk, plane, 2 * ny, 2)
    x_o = own_rows(x, plane, 2 * ny, 2)
    r_o = own_rows(r, plane, 2 * ny, 2)
    cot_o = own_rows(cot, qplane, ny, 1)
    dk_o = own_rows(dk_ref[...], plane, 2 * ny, 0)
    dv_o = own_rows(dv_ref[...], plane, 2 * ny, 0)
    gq = dq_ref[...] * scale
    inv = 1.0 / HEAD_DIM
    gq_b = (rq_o * gq - q_o * (rq_o * rq_o * rq_o) * (head_sums(q_o * gq, ones) * inv)).astype(BF16)
    gk_b = (rk_o * dk_o - k_o * (rk_o * rk_o * rk_o) * (head_sums(k_o * dk_o, ones) * inv)).astype(BF16)
    gv_b = dv_o.astype(BF16)
    att_b = att_ref[...].astype(BF16)
    cot_b = cot_o.astype(BF16)
    normed_b = (x_o * r_o).astype(BF16)

    width = 4 * D // n_gx
    per = D // width
    for d in range(n_gx):
        part = (gq_b, gk_b, gv_b, cot_b)[d // per]
        off = (d % per) * width
        send_ref[d, :, 0:width] = part[:, off : off + width]
        send_ref[d, :, width : width + D] = normed_b if d < 3 * per else att_b

    g_norm = mm(gq_b, wqkv_ref[0:D]) + mm(gk_b, wqkv_ref[D : 2 * D]) + mm(gv_b, wqkv_ref[2 * D : 3 * D])
    g_in = r_o * g_norm - x_o * (r_o * r_o * r_o) * jnp.mean(x_o * g_norm, axis=-1, keepdims=True)
    gin = (cot_o + g_in).astype(BF16)

    def gin_source(i):
        px = i // inner
        rest = i - px * inner
        py = rest // 4
        return px * inner + (rest - py * 4) * ny + py

    gin_ref[...] = mm(select_rows(tokens, gin_source), gin).astype(BF16)

    out = (x_o + mm(att_b, wout_ref[...], NT)).astype(BF16)

    def out_source(i):
        dst = i // (2 * yb * 4)
        rest = i - dst * (2 * yb * 4)
        px = rest // (yb * 4)
        rest = rest - px * (yb * 4)
        py = rest // 4
        return px * inner + (rest - py * 4) * ny + dst * yb + py

    out_ref[...] = mm(select_rows(tokens, out_source), out).astype(BF16)


def partial_kernel(recv_ref, out_ref, send_ref, *, width, n_gy, extra):
    n_gx, tokens, _ = recv_ref.shape
    both = recv_ref[...].reshape(n_gx * tokens, width + D)
    partial = mm(both[:, 0:width], both[:, width : width + D], TN).astype(BF16)
    rows = width // n_gy
    for d in range(n_gy):
        send_ref[d, 0:rows] = partial[d * rows : (d + 1) * rows]
        send_ref[d, rows : rows + extra] = out_ref[d * extra : (d + 1) * extra]


def final_kernel(recv_ref, gw_ref, out_ref, *, rows, extra, factor):
    n_gy = recv_ref.shape[0]
    total = recv_ref[0, 0:rows].astype(F32)
    for s in range(1, n_gy):
        total = total + recv_ref[s, 0:rows].astype(F32)
    gw_ref[...] = total * factor
    got = jnp.concatenate([recv_ref[s, rows : rows + extra].astype(F32) for s in range(n_gy)], axis=0)

    def source(i):
        xy = i // (4 * n_gy)
        rest = i - xy * (4 * n_gy)
        src = rest // 4
        return src * extra + xy * 4 + rest - src * 4

    out_ref[...] = mm(select_rows(n_gy * extra, source), got.astype(BF16)).astype(BF16)


def on_device(slab_tokens, cotangent, w_qkv, w_out, logit_scale):
    size_x, ny, size_z, _ = slab_tokens.shape
    n_gx = lax.axis_size("gx")
    n_gy = lax.axis_size("gy")
    yb = cotangent.shape[1]
    total_x, total_z = size_x * n_gx, size_z * n_gy
    assert size_x == 2 and size_z == 4 and cotangent.shape[0] == 2
    assert cotangent.shape[2] == total_z and yb * n_gy == ny
    tokens = size_x * ny * size_z
    up_x = [(i, i + 1) for i in range(n_gx - 1)]
    down_x = [(t, s) for s, t in up_x]
    up_y = [(i, i + 1) for i in range(n_gy - 1)]
    down_y = [(t, s) for s, t in up_y]

    own = jnp.transpose(slab_tokens, (0, 2, 1, 3))
    own_rows = own.reshape(tokens, D)
    from_low = lax.ppermute(
        jnp.concatenate([own_rows, cotangent[1].reshape(-1, D)], axis=0), "gx", up_x
    )
    from_high = lax.ppermute(
        jnp.concatenate([own_rows, cotangent[0].reshape(-1, D)], axis=0), "gx", down_x
    )
    low_slab = from_low[:tokens].reshape(2, 4, ny, D)
    high_slab = from_high[:tokens].reshape(2, 4, ny, D)

    def z_edge(start):
        return jnp.concatenate(
            [a[:, start : start + 2] for a in (low_slab, own, high_slab)], axis=0
        ).reshape(-1, D)

    z_low = lax.ppermute(z_edge(2), "gy", up_y)
    z_high = lax.ppermute(z_edge(0), "gy", down_y)
    cot4 = jnp.concatenate(
        [
            from_low[tokens:].reshape(1, yb, total_z, D),
            cotangent,
            from_high[tokens:].reshape(1, yb, total_z, D),
        ],
        axis=0,
    )
    padded = jnp.pad(cot4, ((0, 0), (0, 0), (1, 1), (0, 0)))
    windows = jnp.stack([padded[:, :, 4 * d : 4 * d + 6] for d in range(n_gy)])
    cot_rows = lax.all_to_all(windows, "gy", 0, 0, tiled=True).reshape(-1, D)

    scale = jnp.repeat(logit_scale / HEAD_DIM, HEAD_DIM)[None]
    pos = jnp.stack([lax.axis_index("gx"), lax.axis_index("gy")]).astype(jnp.int32)
    width = 4 * D // n_gx
    vmem = pl.BlockSpec(memory_space=pltpu.VMEM)
    send, out_rows, gin = pl.pallas_call(
        lambda *refs: main_kernel(
            *refs, ny=ny, n_gx=n_gx, n_gy=n_gy, total_x=total_x, total_z=total_z
        ),
        name="layer",
        out_shape=(
            jax.ShapeDtypeStruct((n_gx, tokens, width + D), BF16),
            jax.ShapeDtypeStruct((tokens, D), BF16),
            jax.ShapeDtypeStruct((tokens, D), BF16),
        ),
        in_specs=[pl.BlockSpec(memory_space=pltpu.SMEM)] + [vmem] * 9,
        out_specs=(vmem, vmem, vmem),
        scratch_shapes=[
            pltpu.VMEM((6, 8 * ny, D), BF16),
            pltpu.VMEM((tokens, D), F32),
            pltpu.VMEM((16 * ny, D), F32),
            pltpu.VMEM((16 * ny, D), F32),
            pltpu.VMEM((tokens, D), F32),
        ],
    )(pos, own_rows, from_low, from_high, z_low, z_high, cot_rows, w_qkv, w_out, scale)

    recv = lax.all_to_all(send, "gx", 0, 0, tiled=True)
    extra = tokens // n_gy
    rows = width // n_gy
    send2 = pl.pallas_call(
        lambda *refs: partial_kernel(*refs, width=width, n_gy=n_gy, extra=extra),
        name="partial",
        out_shape=jax.ShapeDtypeStruct((n_gy, rows + extra, D), BF16),
        in_specs=[vmem, vmem],
        out_specs=vmem,
    )(recv, out_rows)
    recv2 = lax.all_to_all(send2, "gy", 0, 0, tiled=True)
    factor = 1.0 / math.sqrt(total_x * ny * total_z)
    grad_weights, output = pl.pallas_call(
        lambda *refs: final_kernel(*refs, rows=rows, extra=extra, factor=factor),
        name="final",
        out_shape=(
            jax.ShapeDtypeStruct((rows, D), F32),
            jax.ShapeDtypeStruct((n_gy * extra, D), BF16),
        ),
        in_specs=[vmem],
        out_specs=(vmem, vmem),
    )(recv2)
    return (
        output.reshape(2, yb, total_z, D),
        gin.reshape(2, ny, 4, D),
        grad_weights,
    )


def solution(mesh):
    return jax.shard_map(
        on_device,
        mesh=mesh,
        in_specs=(P("gx", None, "gy", None), P("gx", "gy", None, None), P(), P(), P()),
        out_specs=(P("gx", "gy", None, None), P("gx", None, "gy", None), P(("gx", "gy"), None)),
        check_vma=False,
    )
```

profile of v0, /device:TPU:0, one launch (start us, length us, event | category | flops | bytes accessed | tf_op | source)
XLA Modules:
  0.0 77.9 jit_solution(2030430600480100649)
XLA Ops:
  0.6 0.9 %copy.22 = bf16[2,4,8,512]{3,2,1,0:T(8,128)(2,1)S(1)} copy(bf16[2,4,8,512]{3,1,2,0:T(4,128)(2,1)} %bitcast.23) | data formatting | bytes 131072 | tf_op jit(solution)/shard_map/transpose | solution.py:240
  1.5 0.0 copy-start.1
  1.5 0.8 %fusion.5 = (bf16[1,2,16,512]{3,2,1,0:T(8,128)(2,1)S(1)}, bf16[1,2,16,512]{3,2,1,0:T(8,128)(2,1)S(1)}) fusion(bf16[2,2,16,512]{3,2,1,0:T(8,128)(2,1)} %param.6), kind=kLoop, calls=%fused_computation.17 | loop fusion | bytes 131072 | tf_op jit(solution)/shard_map/slice | solution.py:246
  2.3 1.3 %collective-permute-start.1 = (bf16[96,512]{1,0:T(8,128)(2,1)S(1)}, bf16[96,512]{1,0:T(8,128)(2,1)S(1)}, u32[]{:S(2)}, u32[]{:S(2)}) collective-permute-start(bf16[96,512]{1,0:T(8,128)(2,1)S(1)} %get-tuple-element.23), channel_id=1, source_target_pairs={{4,0},{8,4},{12,8},{16,12},{20,16},{24,20},{28,24},{5,1},{9,5},{13... | collective-permute-start | bytes 294920 | tf_op jit(solution)/shard_map/ppermute | solution.py:245
  3.6 3.0 %collective-permute-start = (bf16[96,512]{1,0:T(8,128)(2,1)S(1)}, bf16[96,512]{1,0:T(8,128)(2,1)S(1)}, u32[]{:S(2)}, u32[]{:S(2)}) collective-permute-start(bf16[96,512]{1,0:T(8,128)(2,1)S(1)} %get-tuple-element.24), channel_id=1, source_target_pairs={{0,4},{4,8},{8,12},{12,16},{16,20},{20,24},{24,28},{1,5},{5,9},{9,... | collective-permute-start | bytes 294920 | tf_op jit(solution)/shard_map/ppermute | solution.py:242
  6.7 1.0 %fusion.3 = (bf16[2,2,8,512]{3,1,2,0:T(2,128)(2,1)S(1)}, bf16[2,2,8,512]{3,1,2,0:T(2,128)(2,1)S(1)}) fusion(bf16[2,4,8,512]{3,1,2,0:T(4,128)(2,1)} %bitcast.24), kind=kLoop, calls=%fused_computation.15 | loop fusion | bytes 131072 | tf_op jit(solution)/shard_map/slice | solution.py:253
  7.6 0.7 broadcast_multiply_fusion
  8.3 0.9 %copy.30 = bf16[2,2,16,512]{3,0,2,1:T(2,128)(2,1)S(1)} copy(bf16[2,2,16,512]{3,2,1,0:T(8,128)(2,1)} %param.6) | data formatting | bytes 131072 | tf_op args[1]
  9.2 0.1 broadcast_in_dim.3
  9.3 0.7 broadcast_in_dim_reshape.3.refs_9_
  10.0 0.0 collective-permute-done.1.refs_3_
  10.0 0.0 copy-start.2
  10.0 0.1 copy.31
  10.1 0.0 collective-permute-done.refs_2_
  10.1 0.0 copy-start.3
  10.1 0.1 copy.29
  10.2 0.2 pad_maximum_fusion.1
  10.4 0.1 fusion
  10.5 0.8 %pad_maximum_fusion = bf16[4,4,2,6,512]{4,1,3,2,0:T(4,128)(2,1)} fusion(bf16[1,4,2,6,512]{4,1,3,2,0:T(4,128)(2,1)S(1)} %get-tuple-element.14, bf16[1,4,2,6,512]{4,1,3,2,0:T(4,128)(2,1)S(1)} %get-tuple-element.15, bf16[1,4,2,6,512]{4,1,3,2,0:T(4,128)(2,1)S(1)} %get-tuple-element.16, bf16[1,4,2,6,512]{4,1,3,2,0:T(4,128)(2,1)S(1)} %get-tuple-element.13), kind=kLoop, calls=%fused_computation | loop fusion | flops 294912 | bytes 393216 | tf_op jit(solution)/shard_map/stack | solution.py:267
  11.3 6.3 %all-to-all-start = ((bf16[4,4,2,6,512]{4,1,3,2,0:T(4,128)(2,1)}), bf16[4,4,2,6,512]{4,1,3,2,0:T(4,128)(2,1)S(1)}, u32[]{:S(2)}, u32[]{:S(2)}) async-start(bf16[4,4,2,6,512]{4,1,3,2,0:T(4,128)(2,1)} %pad_maximum_fusion), calls=%async_computation | async-start | bytes 393216 | tf_op jit(solution)/shard_map/all_to_all | solution.py:268
  17.7 0.0 copy-done.1
  17.8 0.3 pad_maximum_fusion.4
  18.1 0.0 copy-done.2
  18.2 1.3 %collective-permute-start.3 = (bf16[96,512]{1,0:T(8,128)(2,1)S(1)}, bf16[96,512]{1,0:T(8,128)(2,1)S(1)}, u32[]{:S(2)}, u32[]{:S(2)}) collective-permute-start(bf16[96,512]{1,0:T(8,128)(2,1)S(1)} %bitcast.32), channel_id=1, source_target_pairs={{1,0},{2,1},{3,2},{5,4},{6,5},{7,6},{9,8},{10,9},{11,10},{13,12},{... | collective-permute-start | bytes 294920 | tf_op jit(solution)/shard_map/ppermute | solution.py:257
  19.5 4.6 %collective-permute-start.2 = (bf16[96,512]{1,0:T(8,128)(2,1)S(1)}, bf16[96,512]{1,0:T(8,128)(2,1)S(1)}, u32[]{:S(2)}, u32[]{:S(2)}) collective-permute-start(bf16[96,512]{1,0:T(8,128)(2,1)S(1)} %bitcast.31), channel_id=1, source_target_pairs={{0,1},{1,2},{2,3},{4,5},{5,6},{6,7},{8,9},{9,10},{10,11},{12,13},{... | collective-permute-start | bytes 294920 | tf_op jit(solution)/shard_map/ppermute | solution.py:256
  24.0 0.7 pad_add_fusion.refs_0_
  24.7 1.9 %all-to-all-done = bf16[4,4,2,6,512]{4,1,3,2,0:T(4,128)(2,1)S(1)} async-done(((bf16[4,4,2,6,512]{4,1,3,2,0:T(4,128)(2,1)}), bf16[4,4,2,6,512]{4,1,3,2,0:T(4,128)(2,1)S(1)}, u32[]{:S(2)}, u32[]{:S(2)}) %all-to-all-start) | async-done | bytes 196640 | tf_op jit(solution)/shard_map/all_to_all | solution.py:268
  26.6 0.0 copy-done.3
  26.6 0.7 reshape.43.refs_6_
  27.3 0.0 collective-permute-done.3.refs_5_
  27.4 0.0 copy-start.4
  27.4 0.0 collective-permute-done.2.refs_4_
  27.4 0.6 copy-done.4
  28.0 0.0 copy-start.5
  28.0 0.6 copy-done.5
  28.6 13.3 %layer.1 = (bf16[8,64,768]{2,1,0:T(8,128)(2,1)}, bf16[64,512]{1,0:T(8,128)(2,1)}, bf16[64,512]{1,0:T(8,128)(2,1)}) custom-call(s32[2]{0:T(128)} %pad_add_fusion.refs_0_, bf16[64,512]{1,0:T(8,128)(2,1)} %bitcast.22, bf16[96,512]{1,0:T(8,128)(2,1)} %copy-done.3, bf16[96,512]{1,0:T(8,128)(2,1)} %copy-done.2, bf16[96,512]{1,0:T(8,128)(2,1)} %copy-done.5, ...), custom_call_target="tpu_custom_call" | custom-call | tf_op jit(solution)/shard_map/layer/pallas_call | solution.py:274
  41.9 0.0 copy-start.6
  41.9 16.9 %all_to_all.15.refs_0_ = bf16[8,64,768]{2,1,0:T(8,128)(2,1)} all-to-all(bf16[8,64,768]{2,1,0:T(8,128)(2,1)} %get-tuple-element.8), channel_id=1, replica_groups=mesh['gx'=8,'gy'=4] {'gx'}, dimensions={0} | all-to-all | bytes 1572864 | tf_op jit(solution)/shard_map/all_to_all | solution.py:295
  58.7 2.2 %partial.1 = bf16[4,80,512]{2,1,0:T(8,128)(2,1)} custom-call(bf16[8,64,768]{2,1,0:T(8,128)(2,1)} %all_to_all.15.refs_0_, bf16[64,512]{1,0:T(8,128)(2,1)} %get-tuple-element.9.refs_1_), custom_call_target="tpu_custom_call" | custom-call | tf_op jit(solution)/shard_map/partial/pallas_call | solution.py:298
  60.9 4.8 %all-to-all-start.2 = ((bf16[4,80,512]{2,1,0:T(8,128)(2,1)}), bf16[4,80,512]{2,1,0:T(8,128)(2,1)S(1)}, u32[]{:S(2)}, u32[]{:S(2)}) async-start(bf16[4,80,512]{2,1,0:T(8,128)(2,1)} %partial.1), calls=%async_computation.2 | async-start | bytes 655360 | tf_op jit(solution)/shard_map/all_to_all | solution.py:305
  65.7 0.0 copy-done.6
  65.7 0.6 reshape.45
  66.4 9.1 %all-to-all-done.2.refs_0_ = bf16[4,80,512]{2,1,0:T(8,128)(2,1)S(1)} async-done(((bf16[4,80,512]{2,1,0:T(8,128)(2,1)}), bf16[4,80,512]{2,1,0:T(8,128)(2,1)S(1)}, u32[]{:S(2)}, u32[]{:S(2)}) %all-to-all-start.2) | async-done | bytes 327712 | tf_op jit(solution)/shard_map/all_to_all | solution.py:305
  75.5 0.0 copy-start
  75.5 0.7 copy-done
  76.2 1.8 %final.1 = (f32[64,512]{1,0:T(8,128)}, bf16[64,512]{1,0:T(8,128)(2,1)}) custom-call(bf16[4,80,512]{2,1,0:T(8,128)(2,1)} %copy-done), custom_call_target="tpu_custom_call" | custom-call | tf_op jit(solution)/shard_map/final/pallas_call | solution.py:307
  (14 shorter events, 0.2 us)
Async XLA Ops:
  1.5 16.2 %copy-start.1 = (bf16[2,4,8,512]{3,2,1,0:T(8,128)(2,1)}, bf16[2,4,8,512]{3,2,1,0:T(8,128)(2,1)S(1)}, u32[]{:S(2)}) copy-start(bf16[2,4,8,512]{3,2,1,0:T(8,128)(2,1)S(1)} %copy.22) | copy-start | bytes 196612
  2.3 7.6 %collective-permute-start.1 = (bf16[96,512]{1,0:T(8,128)(2,1)S(1)}, bf16[96,512]{1,0:T(8,128)(2,1)S(1)}, u32[]{:S(2)}, u32[]{:S(2)}) collective-permute-start(bf16[96,512]{1,0:T(8,128)(2,1)S(1)} %get-tuple-element.23), channel_id=1, source_target_pairs={{4,0},{8,4},{12,8},{16,12},{20,16},{24,20},{28,24},{5,1},{9,5},{13... | collective-permute-start | bytes 294920 | tf_op jit(solution)/shard_map/ppermute | solution.py:245
  3.6 6.4 %collective-permute-start = (bf16[96,512]{1,0:T(8,128)(2,1)S(1)}, bf16[96,512]{1,0:T(8,128)(2,1)S(1)}, u32[]{:S(2)}, u32[]{:S(2)}) collective-permute-start(bf16[96,512]{1,0:T(8,128)(2,1)S(1)} %get-tuple-element.24), channel_id=1, source_target_pairs={{0,4},{4,8},{8,12},{12,16},{16,20},{20,24},{24,28},{1,5},{5,9},{9,... | collective-permute-start | bytes 294920 | tf_op jit(solution)/shard_map/ppermute | solution.py:242
  10.0 8.2 %copy-start.2 = (bf16[96,512]{1,0:T(8,128)(2,1)}, bf16[96,512]{1,0:T(8,128)(2,1)S(1)}, u32[]{:S(2)}) copy-start(bf16[96,512]{1,0:T(8,128)(2,1)S(1)} %collective-permute-done.1.refs_3_) | copy-start | bytes 294916
  10.1 16.5 %copy-start.3 = (bf16[96,512]{1,0:T(8,128)(2,1)}, bf16[96,512]{1,0:T(8,128)(2,1)S(1)}, u32[]{:S(2)}) copy-start(bf16[96,512]{1,0:T(8,128)(2,1)S(1)} %collective-permute-done.refs_2_) | copy-start | bytes 294916
  11.3 15.2 %all-to-all-start = ((bf16[4,4,2,6,512]{4,1,3,2,0:T(4,128)(2,1)}), bf16[4,4,2,6,512]{4,1,3,2,0:T(4,128)(2,1)S(1)}, u32[]{:S(2)}, u32[]{:S(2)}) async-start(bf16[4,4,2,6,512]{4,1,3,2,0:T(4,128)(2,1)} %pad_maximum_fusion), calls=%async_computation | async-start | bytes 393216 | tf_op jit(solution)/shard_map/all_to_all | solution.py:268
  18.2 9.2 %collective-permute-start.3 = (bf16[96,512]{1,0:T(8,128)(2,1)S(1)}, bf16[96,512]{1,0:T(8,128)(2,1)S(1)}, u32[]{:S(2)}, u32[]{:S(2)}) collective-permute-start(bf16[96,512]{1,0:T(8,128)(2,1)S(1)} %bitcast.32), channel_id=1, source_target_pairs={{1,0},{2,1},{3,2},{5,4},{6,5},{7,6},{9,8},{10,9},{11,10},{13,12},{... | collective-permute-start | bytes 294920 | tf_op jit(solution)/shard_map/ppermute | solution.py:257
  19.5 7.9 %collective-permute-start.2 = (bf16[96,512]{1,0:T(8,128)(2,1)S(1)}, bf16[96,512]{1,0:T(8,128)(2,1)S(1)}, u32[]{:S(2)}, u32[]{:S(2)}) collective-permute-start(bf16[96,512]{1,0:T(8,128)(2,1)S(1)} %bitcast.31), channel_id=1, source_target_pairs={{0,1},{1,2},{2,3},{4,5},{5,6},{6,7},{8,9},{9,10},{10,11},{12,13},{... | collective-permute-start | bytes 294920 | tf_op jit(solution)/shard_map/ppermute | solution.py:256
  27.4 0.6 copy-start.4
  28.0 0.6 copy-start.5
  41.9 23.8 %copy-start.6 = (bf16[64,512]{1,0:T(8,128)(2,1)S(1)}, bf16[64,512]{1,0:T(8,128)(2,1)}, u32[]{:S(2)}) copy-start(bf16[64,512]{1,0:T(8,128)(2,1)} %get-tuple-element.11) | copy-start | bytes 196612
  60.9 14.5 %all-to-all-start.2 = ((bf16[4,80,512]{2,1,0:T(8,128)(2,1)}), bf16[4,80,512]{2,1,0:T(8,128)(2,1)S(1)}, u32[]{:S(2)}, u32[]{:S(2)}) async-start(bf16[4,80,512]{2,1,0:T(8,128)(2,1)} %partial.1), calls=%async_computation.2 | async-start | bytes 655360 | tf_op jit(solution)/shard_map/all_to_all | solution.py:305
  75.5 0.7 copy-start
where the time goes:
time: 78.7 us; the launch traced here: 77.9 us
  starting transfers between devices  21.3 us (27%)
  Pallas kernels  17.2 us (22%)
  blocking collectives  16.9 us (21%)
  waiting for transfers between devices  10.9 us (14%)
  local copies, waits for them, and re-layouts  8.06 us (10%)
  other arithmetic  2.67 us (3%)
  between operations  0.87 us (1%)
    all_to_all x1, blocking collectives, on_device(): recv = lax.all_to_all(send, 'gx', 0, 0, tiled=True)  16.9 us
    pallas_call x1, Pallas kernels, on_device(): pl.pallas_call(lambda *refs: main_kernel(*refs, ny=ny, n_gx=n_gx, n_gy=n_...  13.3 us
    all_to_all x1, waiting for transfers between devices, on_device(): recv2 = lax.all_to_all(send2, 'gy', 0, 0, tiled=True)  9.07 us
    all_to_all x1, starting transfers between devices, on_device(): cot_rows = lax.all_to_all(windows, 'gy', 0, 0, tiled=True).reshape(-1, D)  6.35 us
    all_to_all x1, starting transfers between devices, on_device(): recv2 = lax.all_to_all(send2, 'gy', 0, 0, tiled=True)  4.81 us
    ppermute x1, starting transfers between devices, on_device(): z_low = lax.ppermute(z_edge(2), 'gy', up_y)  4.55 us
    ppermute x1, starting transfers between devices, on_device(): lax.ppermute(jnp.concatenate([own_rows, cotangent[1].reshape(-1, D)], axi...  3.04 us
    unnamed x19, local copies, waits for them, and re-layouts  3.01 us
  transfers between devices with their start and end apart: 6, of which 2 were waited for; matrix products, arithmetic and copies ran while one was open for 8% of the time, Pallas kernels for 0%

commit v1 on v0

v1 whole, which is shorter than its diff:
```python
import math

import jax
import jax.numpy as jnp
from jax import lax
from jax.experimental import pallas as pl
from jax.experimental.pallas import tpu as pltpu
from jax.sharding import PartitionSpec as P

D = 512
HEADS = 8
HEAD_DIM = 64
QUAD = 4
LANES = QUAD * HEAD_DIM
EPSILON = 1e-06
NEGATIVE = -1e30
F32 = jnp.float32
BF16 = jnp.bfloat16

NN = (((1,), (0,)), ((), ()))
NT = (((1,), (1,)), ((), ()))
TN = (((0,), (0,)), ((), ()))


def mm(a, b, dims=NN):
    return lax.dot_general(a, b, dims, preferred_element_type=F32)


def iota(shape, dim):
    return lax.broadcasted_iota(jnp.int32, shape, dim)


def head_sums(values, ones):
    high = values.astype(BF16)
    low = (values - high.astype(F32)).astype(BF16)
    return jnp.concatenate(
        [
            mm(high[:, g : g + LANES], ones) + mm(low[:, g : g + LANES], ones)
            for g in range(0, D, LANES)
        ],
        axis=1,
    )


def one_hot_rows(count, columns, source_of):
    return jnp.where(source_of(iota((count, 1), 0)) == iota((1, columns), 1), 1.0, 0.0).astype(BF16)


def pack_x_kernel(own_ref, cot_ref, m1_ref, m2_ref):
    tokens = own_ref.shape[0]
    odd = lax.axis_index("gx") % 2
    own = own_ref[...]
    m1_ref[0:tokens] = own
    m2_ref[0:tokens] = own
    m1_ref[tokens:] = cot_ref[1 - odd]
    m2_ref[tokens:] = cot_ref[odd]


def pack_z_kernel(own_ref, m1_ref, m2_ref, cot_ref, z1_ref, z2_ref, win_ref, *, ny, n_gx, n_gy):
    inner = 4 * ny
    tokens = 2 * inner
    edge = 2 * ny
    yb = ny // n_gy
    total_z = 4 * n_gy
    gx = lax.axis_index("gx")
    odd = gx % 2
    odd_z = lax.axis_index("gy") % 2
    for ref, off in ((z1_ref, (1 - odd_z) * edge), (z2_ref, odd_z * edge)):
        for i, src in enumerate((m1_ref, own_ref, m2_ref)):
            for p in range(2):
                start = pl.multiple_of(p * inner + off, edge)
                ref[(2 * i + p) * edge : (2 * i + p + 1) * edge] = src[pl.ds(start, edge)]
    planes = jnp.concatenate([m1_ref[tokens:], cot_ref[0], cot_ref[1], m2_ref[tokens:]], axis=0)

    def source(i):
        dst = i // (24 * yb)
        rest = i - dst * (24 * yb)
        px = rest // (6 * yb)
        rest = rest - px * (6 * yb)
        pz = rest // yb
        y = rest - pz * yb
        z = 4 * dst - 1 + pz
        outer = jnp.where(px == 0, jnp.where(odd == 0, 3, 0), jnp.where(odd == 0, 0, 3))
        slot = jnp.where((px == 0) | (px == 3), outer, px)
        x = gx * 2 - 1 + px
        ok = (z >= 0) & (z < total_z) & (x >= 0) & (x < 2 * n_gx)
        return jnp.where(ok, (slot * yb + y) * total_z + z, -1)

    rows = n_gy * 24 * yb
    win = mm(one_hot_rows(rows, 4 * yb * total_z, source), planes).astype(BF16)
    for d in range(n_gy):
        win_ref[d] = win[d * 24 * yb : (d + 1) * 24 * yb]


def main_kernel(
    ls_ref, own_ref, m1_ref, m2_ref, z1_ref, z2_ref, cot_ref, wqkv_ref, wout_ref,
    send_ref, out_ref, gin_ref,
    e_ref, bias_ref, dq_ref, dk_ref, dv_ref, att_ref,
    *, ny, n_gx, n_gy,
):
    plane = 8 * ny
    inner = 4 * ny
    edge = 2 * ny
    block = 12 * ny
    tokens = 2 * inner
    yb = ny // n_gy
    total_x, total_z = 2 * n_gx, 4 * n_gy
    gx = lax.axis_index("gx")
    gy = lax.axis_index("gy")
    odd = gx % 2
    odd_z = gy % 2
    base1 = 4 - 4 * odd
    base2 = 4 * odd
    for i, (src, base) in enumerate(((m1_ref, base1), (own_ref, 2), (m2_ref, base2))):
        for p in range(2):
            e_ref[base + p, edge : edge + inner] = src[p * inner : (p + 1) * inner]
            for ref, at in ((z1_ref, (1 - odd_z) * 6 * ny), (z2_ref, odd_z * 6 * ny)):
                at = pl.multiple_of(at, edge)
                e_ref[base + p, pl.ds(at, edge)] = ref[(2 * i + p) * edge : (2 * i + p + 1) * edge]

    x = e_ref[...].reshape(6 * plane, D).astype(F32)
    r = lax.rsqrt(jnp.mean(x * x, axis=-1, keepdims=True) + EPSILON)
    normed_f = x * r
    normed = normed_f.astype(BF16)

    def query_rows(values):
        parts = []
        for own_plane, other in ((2, 1), (3, 4)):
            a, o = own_plane * plane, other * plane
            parts += [
                values[a + 2 * ny : a + 6 * ny],
                values[a + ny : a + 2 * ny],
                values[a + 6 * ny : a + 7 * ny],
                values[o + ny : o + 7 * ny],
            ]
        return jnp.concatenate(parts, axis=0)

    def cot_source(i):
        b = i // block
        t = i - b * block
        own_x = 1 + b
        other_x = 3 * b
        t4 = t - 6 * ny
        zo = t4 // ny
        z_own = jnp.where(t < 4 * ny, 1 + t // ny, jnp.where(t < 5 * ny, 0, 5))
        is_own = t < 6 * ny
        px = jnp.where(is_own, own_x, other_x)
        pz = jnp.where(is_own, z_own, zo)
        y = t % ny
        src = y // yb
        return ((src * 4 + px) * 6 + pz) * yb + (y - src * yb)

    ones = (iota((LANES, 1), 0) // HEAD_DIM == iota((1, LANES), 1) // HEAD_DIM)
    ones = jnp.where(ones, 1.0, 0.0).astype(BF16)
    head = iota((1, D), 1) // HEAD_DIM
    scale = jnp.zeros((1, D), F32)
    for h in range(HEADS):
        scale = jnp.where(head == h, ls_ref[h] * (1.0 / HEAD_DIM), scale)

    k = mm(normed, wqkv_ref[D : 2 * D], NT)
    v = mm(normed, wqkv_ref[2 * D : 3 * D], NT)
    q = mm(query_rows(normed_f).astype(BF16), wqkv_ref[0:D], NT)
    rk = lax.rsqrt(head_sums(k * k, ones) * (1.0 / HEAD_DIM) + EPSILON)
    rq = lax.rsqrt(head_sums(q * q, ones) * (1.0 / HEAD_DIM) + EPSILON)
    kb = (k * rk).astype(BF16)
    vb = v.astype(BF16)
    qb = (q * rq * scale).astype(BF16)
    cot = mm(one_hot_rows(2 * block, 2 * block, cot_source), cot_ref[...])
    ub = mm(cot.astype(BF16), wout_ref[...]).astype(BF16)

    lane = iota((1, QUAD * block), 1)
    is_own = lane < QUAD * inner
    t_own = lane % inner
    t_oth = (lane - QUAD * inner) % (8 * ny)
    in_edge = t_oth < 2 * ny
    qz = jnp.where(
        is_own,
        2 + t_own // ny,
        jnp.where(in_edge, jnp.where(t_oth < ny, 1, 6), 1 + (t_oth - 2 * ny) // ny),
    )
    qy = lane % ny
    own_plane = is_own | in_edge
    kj = iota((4 * plane, 1), 0)
    kx = kj // plane
    kr = kj - kx * plane
    kz = kr // ny
    ky = kr - kz * ny
    gz = gy * 4 - 2 + kz
    z_ok = (gz >= 0) & (gz < total_z)
    near_zy = (jnp.abs(kz - qz) <= 1) & (jnp.abs(ky - qy) <= 1)

    mask = [
        jnp.where(iota((1, LANES), 1) // HEAD_DIM == j, 1.0, 0.0).astype(BF16) for j in range(QUAD)
    ]
    for b in range(2):
        qx = jnp.where(own_plane, 2 - b, 1 + b)
        gxk = gx * 2 - 2 + 2 * b + kx
        k_ok = z_ok & (gxk >= 0) & (gxk < total_x)
        ok = near_zy & (jnp.abs(kx - qx) <= 1) & k_ok
        bias_ref[...] = jnp.where(ok, 0.0, NEGATIVE)
        first = 2 * plane if b == 0 else 0
        for g in range(0, D, LANES):
            lanes = slice(g, g + LANES)
            kq = kb[2 * b * plane : (2 * b + 4) * plane, lanes]
            vq = vb[2 * b * plane : (2 * b + 4) * plane, lanes]

            def stacked(values):
                own_part = values[b * block : b * block + inner, lanes]
                other = values[b * block + inner : (b + 1) * block, lanes]
                return jnp.concatenate(
                    [own_part * m for m in mask] + [other * m for m in mask], axis=0
                )

            qs = stacked(qb)
            us = stacked(ub)
            s = mm(kq, qs, NT) + bias_ref[...]
            w = jnp.exp(s - jnp.max(s, axis=0, keepdims=True))
            w = w * (1.0 / jnp.sum(w, axis=0, keepdims=True))
            dp = mm(vq, us, NT)
            ds = w * (dp - jnp.sum(w * dp, axis=0, keepdims=True))
            wb = w.astype(BF16)
            dsb = ds.astype(BF16)
            o_all = mm(wb[:, 0 : QUAD * inner], vq, TN)
            dq_all = mm(dsb[:, 0 : QUAD * inner], kq, TN)
            lane_head = iota((1, LANES), 1) // HEAD_DIM
            att = o_all[0:inner]
            dq = dq_all[0:inner]
            for j in range(1, QUAD):
                att = jnp.where(lane_head == j, o_all[j * inner : (j + 1) * inner], att)
                dq = jnp.where(lane_head == j, dq_all[j * inner : (j + 1) * inner], dq)
            att_ref[b * inner : (b + 1) * inner, lanes] = att
            dq_ref[b * inner : (b + 1) * inner, lanes] = dq

            def own_keys(values):
                return jnp.concatenate(
                    [values[first + p * plane + edge : first + p * plane + edge + inner] for p in range(2)],
                    axis=0,
                )

            dk = mm(own_keys(dsb), qs)
            dv = mm(own_keys(wb), us)
            if b == 0:
                dk_ref[:, lanes] = dk
                dv_ref[:, lanes] = dv
            else:
                dk_ref[:, lanes] += dk
                dv_ref[:, lanes] += dv

    def own_queries(values):
        return jnp.concatenate([values[0:inner], values[block : block + inner]], axis=0)

    def own_rows(values):
        return jnp.concatenate(
            [values[(2 + p) * plane + edge : (2 + p) * plane + edge + inner] for p in range(2)],
            axis=0,
        )

    q_o, rq_o, cot_o = own_queries(q), own_queries(rq), own_queries(cot)
    k_o, rk_o, x_o, r_o = own_rows(k), own_rows(rk), own_rows(x), own_rows(r)
    dk_o = dk_ref[...]
    gq = dq_ref[...] * scale
    inv = 1.0 / HEAD_DIM
    gq_b = (rq_o * gq - q_o * (rq_o * rq_o * rq_o) * (head_sums(q_o * gq, ones) * inv)).astype(BF16)
    gk_b = (rk_o * dk_o - k_o * (rk_o * rk_o * rk_o) * (head_sums(k_o * dk_o, ones) * inv)).astype(BF16)
    gv_b = dv_ref[...].astype(BF16)
    att_b = att_ref[...].astype(BF16)
    cot_b = cot_o.astype(BF16)
    normed_b = (x_o * r_o).astype(BF16)

    width = 4 * D // n_gx
    per = D // width
    for d in range(n_gx):
        part = (gq_b, gk_b, gv_b, cot_b)[d // per]
        off = (d % per) * width
        send_ref[d, :, 0:width] = part[:, off : off + width]
        send_ref[d, :, width : width + D] = normed_b if d < 3 * per else att_b

    g_norm = mm(gq_b, wqkv_ref[0:D]) + mm(gk_b, wqkv_ref[D : 2 * D]) + mm(gv_b, wqkv_ref[2 * D : 3 * D])
    g_in = r_o * g_norm - x_o * (r_o * r_o * r_o) * jnp.mean(x_o * g_norm, axis=-1, keepdims=True)
    gin = (cot_o + g_in).astype(BF16)

    def gin_source(i):
        px = i // inner
        rest = i - px * inner
        py = rest // 4
        return px * inner + (rest - py * 4) * ny + py

    gin_ref[...] = mm(one_hot_rows(tokens, tokens, gin_source), gin).astype(BF16)

    out = (x_o + mm(att_b, wout_ref[...], NT)).astype(BF16)

    def out_source(i):
        dst = i // (8 * yb)
        rest = i - dst * (8 * yb)
        px = rest // (4 * yb)
        rest = rest - px * (4 * yb)
        py = rest // 4
        return px * inner + (rest - py * 4) * ny + dst * yb + py

    out_ref[...] = mm(one_hot_rows(tokens, tokens, out_source), out).astype(BF16)


def partial_kernel(recv_ref, out_ref, send_ref, *, width, n_gy, extra):
    n_gx, tokens, _ = recv_ref.shape
    both = recv_ref[...].reshape(n_gx * tokens, width + D)
    partial = mm(both[:, 0:width], both[:, width : width + D], TN).astype(BF16)
    rows = width // n_gy
    for d in range(n_gy):
        send_ref[d, 0:rows] = partial[d * rows : (d + 1) * rows]
        send_ref[d, rows : rows + extra] = out_ref[d * extra : (d + 1) * extra]


def final_kernel(recv_ref, gw_ref, out_ref, *, rows, extra, factor):
    n_gy = recv_ref.shape[0]
    total = recv_ref[0, 0:rows].astype(F32)
    for s in range(1, n_gy):
        total = total + recv_ref[s, 0:rows].astype(F32)
    gw_ref[...] = total * factor
    got = jnp.concatenate([recv_ref[s, rows : rows + extra] for s in range(n_gy)], axis=0)

    def source(i):
        xy = i // (4 * n_gy)
        rest = i - xy * (4 * n_gy)
        src = rest // 4
        return src * extra + xy * 4 + rest - src * 4

    out_ref[...] = mm(one_hot_rows(n_gy * extra, n_gy * extra, source), got).astype(BF16)


def matchings(count, wrap):
    first = [(i, i ^ 1) for i in range(count)]
    ends = [(0, count - 1), (count - 1, 0)] if wrap else [(0, 0), (count - 1, count - 1)]
    second = ends + [(i, i + 1) for i in range(1, count - 1, 2)]
    second += [(i + 1, i) for i in range(1, count - 1, 2)]
    return first, second


def call(kernel, name, args, outs, scratch=(), smem=0):
    vmem = pl.BlockSpec(memory_space=pltpu.VMEM)
    args = list(args[:smem]) + [
        pltpu.with_memory_space_constraint(a, pltpu.VMEM) for a in args[smem:]
    ]
    return pl.pallas_call(
        kernel,
        name=name,
        out_shape=tuple(jax.ShapeDtypeStruct(s, t) for s, t in outs),
        in_specs=[pl.BlockSpec(memory_space=pltpu.SMEM)] * smem + [vmem] * (len(args) - smem),
        out_specs=(vmem,) * len(outs),
        scratch_shapes=[pltpu.VMEM(s, t) for s, t in scratch],
    )(*args)


def on_device(slab_tokens, cotangent, w_qkv, w_out, logit_scale):
    size_x, ny, size_z, _ = slab_tokens.shape
    n_gx = lax.axis_size("gx")
    n_gy = lax.axis_size("gy")
    yb = cotangent.shape[1]
    total_x, total_z = size_x * n_gx, size_z * n_gy
    assert size_x == 2 and size_z == 4 and cotangent.shape[0] == 2
    assert cotangent.shape[2] == total_z and yb * n_gy == ny
    tokens = size_x * ny * size_z
    gx1, gx2 = matchings(n_gx, True)
    gy1, gy2 = matchings(n_gy, False)

    own = jnp.transpose(slab_tokens, (0, 2, 1, 3)).reshape(tokens, D)
    cot = cotangent.reshape(2, yb * total_z, D)
    x_payload = ((tokens + yb * total_z, D), BF16)
    p1, p2 = call(pack_x_kernel, "pack_x", (own, cot), (x_payload, x_payload))
    m1 = lax.ppermute(p1, "gx", gx1)
    m2 = lax.ppermute(p2, "gx", gx2)

    z_payload = ((12 * ny, D), BF16)
    s1, s2, windows = call(
        lambda *refs: pack_z_kernel(*refs, ny=ny, n_gx=n_gx, n_gy=n_gy),
        "pack_z",
        (own, m1, m2, cot),
        (z_payload, z_payload, ((n_gy, 24 * yb, D), BF16)),
    )
    z1 = lax.ppermute(s1, "gy", gy1)
    z2 = lax.ppermute(s2, "gy", gy2)
    cot_rows = lax.all_to_all(windows, "gy", 0, 0, tiled=True).reshape(24 * ny, D)

    width = 4 * D // n_gx
    send, out_rows, gin = call(
        lambda *refs: main_kernel(*refs, ny=ny, n_gx=n_gx, n_gy=n_gy),
        "layer",
        (logit_scale, own, m1, m2, z1, z2, cot_rows, w_qkv, w_out),
        (((n_gx, tokens, width + D), BF16), ((tokens, D), BF16), ((tokens, D), BF16)),
        scratch=(
            ((6, 8 * ny, D), BF16),
            ((32 * ny, QUAD * 12 * ny), F32),
            ((tokens, D), F32),
            ((tokens, D), F32),
            ((tokens, D), F32),
            ((tokens, D), F32),
        ),
        smem=1,
    )

    recv = lax.all_to_all(send, "gx", 0, 0, tiled=True)
    extra = tokens // n_gy
    rows = width // n_gy
    (send2,) = call(
        lambda *refs: partial_kernel(*refs, width=width, n_gy=n_gy, extra=extra),
        "partial",
        (recv, out_rows),
        (((n_gy, rows + extra, D), BF16),),
    )
    recv2 = lax.all_to_all(send2, "gy", 0, 0, tiled=True)
    factor = 1.0 / math.sqrt(total_x * ny * total_z)
    grad_weights, output = call(
        lambda *refs: final_kernel(*refs, rows=rows, extra=extra, factor=factor),
        "final",
        (recv2,),
        (((rows, D), F32), ((n_gy * extra, D), BF16)),
    )
    return (
        output.reshape(2, yb, total_z, D),
        gin.reshape(2, ny, 4, D),
        grad_weights,
    )


def solution(mesh):
    return jax.shard_map(
        on_device,
        mesh=mesh,
        in_specs=(P("gx", None, "gy", None), P("gx", "gy", None, None), P(), P(), P()),
        out_specs=(P("gx", "gy", None, None), P("gx", None, "gy", None), P(("gx", "gy"), None)),
        check_vma=False,
    )
```

time: 78.7 us -> 65.1 us (0.83)
  Pallas kernels: 17.2 us -> 9.75 us
  waiting for transfers between devices: 10.9 us -> 16.4 us
  starting transfers between devices: 21.3 us -> 16.6 us
  local copies, waits for them, and re-layouts: 8.06 us -> 4.8 us
  other arithmetic: 2.67 us -> 0 us
    pallas_call x3 -> x5, Pallas kernels: 17.2 us -> 9.75 us  [call(): pl.pallas_call(kernel, name=name, out_shape=tuple((jax.ShapeDtypeStruct(s...]
    ppermute x4, waiting for transfers between devices: 0.02 us -> 7 us  [the longest x1 4.26 us: on_device(): z1 = lax.ppermute(s1, 'gy', gy1)]
    ppermute x4, starting transfers between devices: 10.2 us -> 7.6 us  [the longest x1 3.54 us: on_device(): m2 = lax.ppermute(p2, 'gx', gx2)]
    slice x8 -> x0, local copies, waits for them, and re-layouts: 1.81 us -> none  [the longest x3 0.99 us: z_edge(): a[:, start:start + 2]]
    all_to_all x1, waiting for transfers between devices: 1.85 us -> 0.3 us  [on_device(): lax.all_to_all(windows, 'gy', 0, 0, tiled=True).reshape(24 * ny, D)]
    another operation x2 -> x0, other arithmetic: 1.5 us -> none  [the longest x1 0.84 us: on_device(): windows = jnp.stack([padded[:, :, 4 * d:4 * d + 6] for d in range(n_gy)])]
    all_to_all x1, starting transfers between devices: 6.35 us -> 5.04 us  [on_device(): lax.all_to_all(windows, 'gy', 0, 0, tiled=True).reshape(24 * ny, D)]
    reshape x3 -> x0, local copies, waits for them, and re-layouts: 0.85 us -> none  [the longest x1 0.74 us: on_device(): cot_rows = lax.all_to_all(windows, 'gy', 0, 0, tiled=True).reshape(-1, D)]
  transfers between devices with their start and end apart: 6 -> 6, of which waited for: 2 -> 4; matrix products, arithmetic and copies ran while one was open for 8% -> 1% of each run, Pallas kernels for 0% -> 0%
where the time goes in v1:
time: 65.1 us; the launch traced here: 64.5 us
  starting transfers between devices  16.6 us (25%)
  waiting for transfers between devices  16.4 us (25%)
  blocking collectives  16.3 us (25%)
  Pallas kernels  9.75 us (15%)
  local copies, waits for them, and re-layouts  4.8 us (7%)
    all_to_all x1, blocking collectives, on_device(): recv = lax.all_to_all(send, 'gx', 0, 0, tiled=True)  16.3 us
    pallas_call x5, Pallas kernels, call(): pl.pallas_call(kernel, name=name, out_shape=tuple((jax.ShapeDtypeStruct(s...  9.75 us
    all_to_all x1, waiting for transfers between devices, on_device(): recv2 = lax.all_to_all(send2, 'gy', 0, 0, tiled=True)  9.07 us
    all_to_all x1, starting transfers between devices, on_device(): lax.all_to_all(windows, 'gy', 0, 0, tiled=True).reshape(24 * ny, D)  5.04 us
    ppermute x1, waiting for transfers between devices, on_device(): z1 = lax.ppermute(s1, 'gy', gy1)  4.26 us
    all_to_all x1, starting transfers between devices, on_device(): recv2 = lax.all_to_all(send2, 'gy', 0, 0, tiled=True)  4.01 us
    ppermute x1, starting transfers between devices, on_device(): m2 = lax.ppermute(p2, 'gx', gx2)  3.54 us
    unnamed x10, local copies, waits for them, and re-layouts  3.29 us
  transfers between devices with their start and end apart: 6, of which 4 were waited for; matrix products, arithmetic and copies ran while one was open for 1% of the time, Pallas kernels for 0%

profile of v1, /device:TPU:0, one launch (start us, length us, event | category | flops | bytes accessed | tf_op | source)
XLA Modules:
  0.0 64.5 jit_solution(7074061943865684482)
XLA Ops:
  0.6 0.9 %copy.8 = bf16[2,4,8,512]{3,2,1,0:T(8,128)(2,1)S(1)} copy(bf16[2,4,8,512]{3,1,2,0:T(4,128)(2,1)} %bitcast.11) | data formatting | bytes 131072 | tf_op jit(solution)/shard_map/transpose | solution.py:365
  1.5 0.0 copy-start.2
  1.5 0.8 %copy-done.2 = bf16[2,2,16,512]{3,2,1,0:T(8,128)(2,1)S(1)} copy-done((bf16[2,2,16,512]{3,2,1,0:T(8,128)(2,1)S(1)}, bf16[2,2,16,512]{3,2,1,0:T(8,128)(2,1)}, u32[]{:S(2)}) %copy-start.2) | copy-done | bytes 65560
  2.3 0.7 %pack_x.1 = (bf16[96,512]{1,0:T(8,128)(2,1)}, bf16[96,512]{1,0:T(8,128)(2,1)}) custom-call(bf16[64,512]{1,0:T(8,128)(2,1)S(1)} %bitcast.5, bf16[2,32,512]{2,1,0:T(8,128)(2,1)S(1)} %bitcast.9), custom_call_target="tpu_custom_call" | custom-call | tf_op jit(solution)/shard_map/pack_x/pallas_call | solution.py:343
  3.0 0.5 collective-permute-start
  3.5 3.5 %collective-permute-start.1 = (bf16[96,512]{1,0:T(8,128)(2,1)}, bf16[96,512]{1,0:T(8,128)(2,1)S(1)}, u32[]{:S(2)}, u32[]{:S(2)}) collective-permute-start(bf16[96,512]{1,0:T(8,128)(2,1)} %get-tuple-element.14), channel_id=1, source_target_pairs={{0,28},{28,0},{4,8},{12,16},{20,24},{8,4},{16,12},{24,20},{1,29},{... | collective-permute-start | bytes 294920 | tf_op jit(solution)/shard_map/ppermute | solution.py:370
  7.1 0.0 collective-permute-done.refs_1_.refs_2_
  7.1 2.7 %collective-permute-done.1.refs_2_.refs_3_ = bf16[96,512]{1,0:T(8,128)(2,1)S(1)} collective-permute-done((bf16[96,512]{1,0:T(8,128)(2,1)}, bf16[96,512]{1,0:T(8,128)(2,1)S(1)}, u32[]{:S(2)}, u32[]{:S(2)}) %collective-permute-start.1) | collective-permute-done | bytes 98336 | tf_op jit(solution)/shard_map/ppermute | solution.py:370
  9.8 1.0 %pack_z.1 = (bf16[96,512]{1,0:T(8,128)(2,1)}, bf16[96,512]{1,0:T(8,128)(2,1)}, bf16[4,48,512]{2,1,0:T(8,128)(2,1)}) custom-call(bf16[64,512]{1,0:T(8,128)(2,1)S(1)} %bitcast.6, bf16[96,512]{1,0:T(8,128)(2,1)S(1)} %collective-permute-done.refs_1_.refs_2_, bf16[96,512]{1,0:T(8,128)(2,1)S(1)} %collective-permute-done.1.refs_2_.refs_3_, ...), custom_call_target="tpu_custom_call" | custom-call | tf_op jit(solution)/shard_map/pack_z/pallas_call | solution.py:343
  10.8 5.0 %all-to-all-start = ((bf16[4,48,512]{2,1,0:T(8,128)(2,1)}), bf16[4,48,512]{2,1,0:T(8,128)(2,1)S(1)}, u32[]{:S(2)}, u32[]{:S(2)}) async-start(bf16[4,48,512]{2,1,0:T(8,128)(2,1)} %get-tuple-element.17), calls=%async_computation | async-start | bytes 393216 | tf_op jit(solution)/shard_map/all_to_all | solution.py:381
  15.9 2.0 %collective-permute-start.2 = (bf16[96,512]{1,0:T(8,128)(2,1)}, bf16[96,512]{1,0:T(8,128)(2,1)S(1)}, u32[]{:S(2)}, u32[]{:S(2)}) collective-permute-start(bf16[96,512]{1,0:T(8,128)(2,1)} %get-tuple-element.15), channel_id=1, source_target_pairs={{0,1},{1,0},{2,3},{3,2},{4,5},{5,4},{6,7},{7,6},{8,9},{9,8},{10,11... | collective-permute-start | bytes 294920 | tf_op jit(solution)/shard_map/ppermute | solution.py:379
  17.9 1.5 %collective-permute-start.3 = (bf16[96,512]{1,0:T(8,128)(2,1)}, bf16[96,512]{1,0:T(8,128)(2,1)S(1)}, u32[]{:S(2)}, u32[]{:S(2)}) collective-permute-start(bf16[96,512]{1,0:T(8,128)(2,1)} %get-tuple-element.16), channel_id=1, source_target_pairs={{0,0},{3,3},{1,2},{2,1},{4,4},{7,7},{5,6},{6,5},{8,8},{11,11},{9,1... | collective-permute-start | bytes 294920 | tf_op jit(solution)/shard_map/ppermute | solution.py:380
  19.4 4.3 %collective-permute-done.2.refs_4_ = bf16[96,512]{1,0:T(8,128)(2,1)S(1)} collective-permute-done((bf16[96,512]{1,0:T(8,128)(2,1)}, bf16[96,512]{1,0:T(8,128)(2,1)S(1)}, u32[]{:S(2)}, u32[]{:S(2)}) %collective-permute-start.2) | collective-permute-done | bytes 98336 | tf_op jit(solution)/shard_map/ppermute | solution.py:379
  23.7 0.0 collective-permute-done.3.refs_5_
  23.7 0.3 all-to-all-done
  24.0 0.0 copy-start
  24.0 1.4 %copy-done = bf16[1536,512]{1,0:T(8,128)(2,1)S(1)} copy-done((bf16[1536,512]{1,0:T(8,128)(2,1)S(1)}, bf16[1536,512]{1,0:T(8,128)(2,1)}, u32[]{:S(2)}) %copy-start) | copy-done | bytes 1572888
  25.4 0.0 copy-start.1
  25.4 1.0 %copy-done.1 = bf16[512,512]{1,0:T(8,128)(2,1)S(1)} copy-done((bf16[512,512]{1,0:T(8,128)(2,1)S(1)}, bf16[512,512]{1,0:T(8,128)(2,1)}, u32[]{:S(2)}) %copy-start.1) | copy-done | bytes 524312
  26.4 6.2 %layer.1 = (bf16[8,64,768]{2,1,0:T(8,128)(2,1)}, bf16[64,512]{1,0:T(8,128)(2,1)}, bf16[64,512]{1,0:T(8,128)(2,1)}) custom-call(f32[8]{0:T(128)} %refs_0_.1, bf16[64,512]{1,0:T(8,128)(2,1)S(1)} %bitcast.7, bf16[96,512]{1,0:T(8,128)(2,1)S(1)} %collective-permute-done.refs_1_.refs_2_, bf16[96,512]{1,0:T(8,128)(2,1)S(1)} %collective-permute-done.1.refs_2_.refs_3_, ...), custom_call_target="tpu_custom_call" | custom-call | tf_op jit(solution)/shard_map/layer/pallas_call | solution.py:343
  32.6 0.0 copy-start.3
  32.6 0.0 copy-start.4
  32.6 16.3 %all_to_all.15.refs_0_ = bf16[8,64,768]{2,1,0:T(8,128)(2,1)S(1)} all-to-all(bf16[8,64,768]{2,1,0:T(8,128)(2,1)} %get-tuple-element.18), channel_id=1, replica_groups=mesh['gx'=8,'gy'=4] {'gx'}, dimensions={0} | all-to-all | bytes 1572864 | tf_op jit(solution)/shard_map/all_to_all | solution.py:400
  49.0 0.0 copy-done.3
  49.0 1.0 %partial.1 = bf16[4,80,512]{2,1,0:T(8,128)(2,1)} custom-call(bf16[8,64,768]{2,1,0:T(8,128)(2,1)S(1)} %all_to_all.15.refs_0_, bf16[64,512]{1,0:T(8,128)(2,1)S(1)} %copy-done.3), custom_call_target="tpu_custom_call" | custom-call | tf_op jit(solution)/shard_map/partial/pallas_call | solution.py:343
  50.0 4.0 %all-to-all-start.2 = ((bf16[4,80,512]{2,1,0:T(8,128)(2,1)}), bf16[4,80,512]{2,1,0:T(8,128)(2,1)S(1)}, u32[]{:S(2)}, u32[]{:S(2)}) async-start(bf16[4,80,512]{2,1,0:T(8,128)(2,1)} %partial.1), calls=%async_computation.2 | async-start | bytes 655360 | tf_op jit(solution)/shard_map/all_to_all | solution.py:409
  54.0 0.0 copy-done.4
  54.0 0.6 %reshape.25 = bf16[2,8,4,512]{3,2,1,0:T(4,128)(2,1)} reshape(bf16[64,512]{1,0:T(8,128)(2,1)S(1)} %copy-done.4) | data formatting | bytes 131072 | tf_op jit(solution)/shard_map/reshape | solution.py:419
  54.7 9.1 %all-to-all-done.2.refs_0_ = bf16[4,80,512]{2,1,0:T(8,128)(2,1)S(1)} async-done(((bf16[4,80,512]{2,1,0:T(8,128)(2,1)}), bf16[4,80,512]{2,1,0:T(8,128)(2,1)S(1)}, u32[]{:S(2)}, u32[]{:S(2)}) %all-to-all-start.2) | async-done | bytes 327712 | tf_op jit(solution)/shard_map/all_to_all | solution.py:409
  63.7 0.8 %final.1 = (f32[64,512]{1,0:T(8,128)}, bf16[64,512]{1,0:T(8,128)(2,1)}) custom-call(bf16[4,80,512]{2,1,0:T(8,128)(2,1)S(1)} %all-to-all-done.2.refs_0_), custom_call_target="tpu_custom_call" | custom-call | tf_op jit(solution)/shard_map/final/pallas_call | solution.py:343
Async XLA Ops:
  1.5 0.8 %copy-start.2 = (bf16[2,2,16,512]{3,2,1,0:T(8,128)(2,1)S(1)}, bf16[2,2,16,512]{3,2,1,0:T(8,128)(2,1)}, u32[]{:S(2)}) copy-start(bf16[2,2,16,512]{3,2,1,0:T(8,128)(2,1)} %param.6) | copy-start | bytes 196612
  3.0 4.0 %collective-permute-start = (bf16[96,512]{1,0:T(8,128)(2,1)}, bf16[96,512]{1,0:T(8,128)(2,1)S(1)}, u32[]{:S(2)}, u32[]{:S(2)}) collective-permute-start(bf16[96,512]{1,0:T(8,128)(2,1)} %get-tuple-element.13), channel_id=1, source_target_pairs={{0,4},{4,0},{8,12},{12,8},{16,20},{20,16},{24,28},{28,24},{1,5},{5... | collective-permute-start | bytes 294920 | tf_op jit(solution)/shard_map/ppermute | solution.py:369
  3.5 6.3 %collective-permute-start.1 = (bf16[96,512]{1,0:T(8,128)(2,1)}, bf16[96,512]{1,0:T(8,128)(2,1)S(1)}, u32[]{:S(2)}, u32[]{:S(2)}) collective-permute-start(bf16[96,512]{1,0:T(8,128)(2,1)} %get-tuple-element.14), channel_id=1, source_target_pairs={{0,28},{28,0},{4,8},{12,16},{20,24},{8,4},{16,12},{24,20},{1,29},{... | collective-permute-start | bytes 294920 | tf_op jit(solution)/shard_map/ppermute | solution.py:370
  10.8 13.2 %all-to-all-start = ((bf16[4,48,512]{2,1,0:T(8,128)(2,1)}), bf16[4,48,512]{2,1,0:T(8,128)(2,1)S(1)}, u32[]{:S(2)}, u32[]{:S(2)}) async-start(bf16[4,48,512]{2,1,0:T(8,128)(2,1)} %get-tuple-element.17), calls=%async_computation | async-start | bytes 393216 | tf_op jit(solution)/shard_map/all_to_all | solution.py:381
  15.9 7.8 %collective-permute-start.2 = (bf16[96,512]{1,0:T(8,128)(2,1)}, bf16[96,512]{1,0:T(8,128)(2,1)S(1)}, u32[]{:S(2)}, u32[]{:S(2)}) collective-permute-start(bf16[96,512]{1,0:T(8,128)(2,1)} %get-tuple-element.15), channel_id=1, source_target_pairs={{0,1},{1,0},{2,3},{3,2},{4,5},{5,4},{6,7},{7,6},{8,9},{9,8},{10,11... | collective-permute-start | bytes 294920 | tf_op jit(solution)/shard_map/ppermute | solution.py:379
  17.9 5.8 %collective-permute-start.3 = (bf16[96,512]{1,0:T(8,128)(2,1)}, bf16[96,512]{1,0:T(8,128)(2,1)S(1)}, u32[]{:S(2)}, u32[]{:S(2)}) collective-permute-start(bf16[96,512]{1,0:T(8,128)(2,1)} %get-tuple-element.16), channel_id=1, source_target_pairs={{0,0},{3,3},{1,2},{2,1},{4,4},{7,7},{5,6},{6,5},{8,8},{11,11},{9,1... | collective-permute-start | bytes 294920 | tf_op jit(solution)/shard_map/ppermute | solution.py:380
  24.0 1.4 %copy-start = (bf16[1536,512]{1,0:T(8,128)(2,1)S(1)}, bf16[1536,512]{1,0:T(8,128)(2,1)}, u32[]{:S(2)}) copy-start(bf16[1536,512]{1,0:T(8,128)(2,1)} %refs_7_.1) | copy-start | bytes 4718596
  25.4 1.0 %copy-start.1 = (bf16[512,512]{1,0:T(8,128)(2,1)S(1)}, bf16[512,512]{1,0:T(8,128)(2,1)}, u32[]{:S(2)}) copy-start(bf16[512,512]{1,0:T(8,128)(2,1)} %refs_8_.1) | copy-start | bytes 1572868
  32.6 16.3 %copy-start.3 = (bf16[64,512]{1,0:T(8,128)(2,1)S(1)}, bf16[64,512]{1,0:T(8,128)(2,1)}, u32[]{:S(2)}) copy-start(bf16[64,512]{1,0:T(8,128)(2,1)} %get-tuple-element.19.refs_1_) | copy-start | bytes 196612
  32.6 21.4 %copy-start.4 = (bf16[64,512]{1,0:T(8,128)(2,1)S(1)}, bf16[64,512]{1,0:T(8,128)(2,1)}, u32[]{:S(2)}) copy-start(bf16[64,512]{1,0:T(8,128)(2,1)} %get-tuple-element.21) | copy-start | bytes 196612
  50.0 13.7 %all-to-all-start.2 = ((bf16[4,80,512]{2,1,0:T(8,128)(2,1)}), bf16[4,80,512]{2,1,0:T(8,128)(2,1)S(1)}, u32[]{:S(2)}, u32[]{:S(2)}) async-start(bf16[4,80,512]{2,1,0:T(8,128)(2,1)} %partial.1), calls=%async_computation.2 | async-start | bytes 655360 | tf_op jit(solution)/shard_map/all_to_all | solution.py:409

commit v2 on v1

--- a/solution.py
+++ b/solution.py
@@ -46,60 +46,78 @@
     return jnp.where(source_of(iota((count, 1), 0)) == iota((1, columns), 1), 1.0, 0.0).astype(BF16)
 
 
-def pack_x_kernel(own_ref, cot_ref, m1_ref, m2_ref):
-    tokens = own_ref.shape[0]
-    odd = lax.axis_index("gx") % 2
-    own = own_ref[...]
-    m1_ref[0:tokens] = own
-    m2_ref[0:tokens] = own
-    m1_ref[tokens:] = cot_ref[1 - odd]
-    m2_ref[tokens:] = cot_ref[odd]
-
-
-def pack_z_kernel(own_ref, m1_ref, m2_ref, cot_ref, z1_ref, z2_ref, win_ref, *, ny, n_gx, n_gy):
+def pack_z_kernel(own_ref, cot_ref, *outs, ny, n_gy):
     inner = 4 * ny
-    tokens = 2 * inner
     edge = 2 * ny
     yb = ny // n_gy
     total_z = 4 * n_gy
-    gx = lax.axis_index("gx")
-    odd = gx % 2
-    odd_z = lax.axis_index("gy") % 2
-    for ref, off in ((z1_ref, (1 - odd_z) * edge), (z2_ref, odd_z * edge)):
-        for i, src in enumerate((m1_ref, own_ref, m2_ref)):
-            for p in range(2):
-                start = pl.multiple_of(p * inner + off, edge)
-                ref[(2 * i + p) * edge : (2 * i + p + 1) * edge] = src[pl.ds(start, edge)]
-    planes = jnp.concatenate([m1_ref[tokens:], cot_ref[0], cot_ref[1], m2_ref[tokens:]], axis=0)
+    window = 12 * yb
+    gy = lax.axis_index("gy")
+    odd = gy % 2
 
     def source(i):
-        dst = i // (24 * yb)
-        rest = i - dst * (24 * yb)
+        k = i // window
+        rest = i - k * window
         px = rest // (6 * yb)
         rest = rest - px * (6 * yb)
         pz = rest // yb
-        y = rest - pz * yb
-        z = 4 * dst - 1 + pz
-        outer = jnp.where(px == 0, jnp.where(odd == 0, 3, 0), jnp.where(odd == 0, 0, 3))
-        slot = jnp.where((px == 0) | (px == 3), outer, px)
-        x = gx * 2 - 1 + px
-        ok = (z >= 0) & (z < total_z) & (x >= 0) & (x < 2 * n_gx)
-        return jnp.where(ok, (slot * yb + y) * total_z + z, -1)
-
-    rows = n_gy * 24 * yb
-    win = mm(one_hot_rows(rows, 4 * yb * total_z, source), planes).astype(BF16)
-    for d in range(n_gy):
-        win_ref[d] = win[d * 24 * yb : (d + 1) * 24 * yb]
-
-
-def main_kernel(
-    ls_ref, own_ref, m1_ref, m2_ref, z1_ref, z2_ref, cot_ref, wqkv_ref, wout_ref,
-    send_ref, out_ref, gin_ref,
-    e_ref, bias_ref, dq_ref, dk_ref, dv_ref, att_ref,
-    *, ny, n_gx, n_gy,
-):
+        z = 4 * (gy ^ k) - 1 + pz
+        return jnp.where((z >= 0) & (z < total_z), (px * yb + rest - pz * yb) * total_z + z, -1)
+
+    win = mm(one_hot_rows(n_gy * window, 2 * yb * total_z, source), cot_ref[...]).astype(BF16)
+    for k in range(n_gy):
+        outs[k][0:window] = win[k * window : (k + 1) * window]
+    last = 3 if n_gy == 4 else n_gy
+    base = window if n_gy == 4 else 0
+    for ref, start, off in ((outs[1], window, 1 - odd), (outs[last], base, odd)):
+        for p in range(2):
+            at = pl.multiple_of(p * inner + off * edge, edge)
+            ref[start + p * edge : start + (p + 1) * edge] = own_ref[pl.ds(at, edge)]
+
+
+def pack_x_kernel(own_ref, *refs, ny, n_gy):
+    ins, (w1_ref, w2_ref, m1_ref, m2_ref, ext_ref, cot_ref) = refs[:-6], refs[-6:]
+    inner = 4 * ny
+    plane = 8 * ny
+    edge = 2 * ny
+    qplane = 6 * ny
+    yb = ny // n_gy
+    window = 12 * yb
+    gx = lax.axis_index("gx")
+    gy = lax.axis_index("gy")
+    odd = gx % 2
+    odd_z = gy % 2
+    last = 3 if n_gy == 4 else n_gy
+    base = window if n_gy == 4 else 0
+    for p in range(2):
+        ext_ref[p * plane + edge : p * plane + edge + inner] = own_ref[p * inner : (p + 1) * inner]
+        for ref, start, top in ((ins[1], window, 1 - odd_z), (ins[last], base, odd_z)):
+            at = pl.multiple_of(p * plane + top * qplane, edge)
+            ext_ref[pl.ds(at, edge)] = ref[start + p * edge : start + (p + 1) * edge]
+    got = jnp.concatenate([ins[k][0:window].astype(F32) for k in range(n_gy)], axis=0).astype(BF16)
+
+    def source(i):
+        row = i // ny
+        y = i - row * ny
+        src = y // yb
+        return ((src ^ gy) * 12 + row) * yb + y - src * yb
+
+    cot = mm(one_hot_rows(2 * qplane, n_gy * window, source), got).astype(BF16)
+    cot_ref[0] = cot[0:qplane]
+    cot_ref[1] = cot[qplane : 2 * qplane]
+    for ref, p in ((m1_ref, 1 - odd), (m2_ref, odd)):
+        ref[0 : 2 * plane] = ext_ref[...]
+        ref[2 * plane :] = cot_ref[p]
+
+
+def main_kernel(*refs, ny, n_gx, n_gy):
+    ls_ref, ext_ref, m1_ref, m2_ref, cot_ref, wqkv_ref, wout_ref = refs[:7]
+    pairs = n_gx // 2
+    send_refs = refs[7 : 7 + pairs]
+    out_ref, gin_ref, e_ref, c_ref, full_ref, bias_ref, dq_ref, dk_ref, dv_ref, att_ref = refs[7 + pairs :]
     plane = 8 * ny
     inner = 4 * ny
+    qplane = 6 * ny
     edge = 2 * ny
     block = 12 * ny
     tokens = 2 * inner
@@ -108,47 +126,32 @@
     gx = lax.axis_index("gx")
     gy = lax.axis_index("gy")
     odd = gx % 2
-    odd_z = gy % 2
-    base1 = 4 - 4 * odd
-    base2 = 4 * odd
-    for i, (src, base) in enumerate(((m1_ref, base1), (own_ref, 2), (m2_ref, base2))):
+    for src, base in ((m1_ref, 4 - 4 * odd), (ext_ref, 2), (m2_ref, 4 * odd)):
         for p in range(2):
-            e_ref[base + p, edge : edge + inner] = src[p * inner : (p + 1) * inner]
-            for ref, at in ((z1_ref, (1 - odd_z) * 6 * ny), (z2_ref, odd_z * 6 * ny)):
-                at = pl.multiple_of(at, edge)
-                e_ref[base + p, pl.ds(at, edge)] = ref[(2 * i + p) * edge : (2 * i + p + 1) * edge]
+            e_ref[base + p] = src[p * plane : (p + 1) * plane]
+    inside = jnp.where((gx > 0) & (gx < n_gx - 1), 1.0, 0.0)
+    c_ref[1] = cot_ref[0]
+    c_ref[2] = cot_ref[1]
+    c_ref[3 - 3 * odd] = m1_ref[2 * plane :]
+    c_ref[3 * odd] = (m2_ref[2 * plane :].astype(F32) * inside).astype(BF16)
 
     x = e_ref[...].reshape(6 * plane, D).astype(F32)
     r = lax.rsqrt(jnp.mean(x * x, axis=-1, keepdims=True) + EPSILON)
     normed_f = x * r
     normed = normed_f.astype(BF16)
 
-    def query_rows(values):
+    def query_rows(values, rows, halo):
         parts = []
         for own_plane, other in ((2, 1), (3, 4)):
-            a, o = own_plane * plane, other * plane
+            a, o = own_plane * rows - halo[0], other * rows - halo[0]
+            first = halo[1]
             parts += [
-                values[a + 2 * ny : a + 6 * ny],
-                values[a + ny : a + 2 * ny],
-                values[a + 6 * ny : a + 7 * ny],
-                values[o + ny : o + 7 * ny],
+                values[a + first + ny : a + first + 5 * ny],
+                values[a + first : a + first + ny],
+                values[a + first + 5 * ny : a + first + 6 * ny],
+                values[o + first : o + first + 6 * ny],
             ]
         return jnp.concatenate(parts, axis=0)
-
-    def cot_source(i):
-        b = i // block
-        t = i - b * block
-        own_x = 1 + b
-        other_x = 3 * b
-        t4 = t - 6 * ny
-        zo = t4 // ny
-        z_own = jnp.where(t < 4 * ny, 1 + t // ny, jnp.where(t < 5 * ny, 0, 5))
-        is_own = t < 6 * ny
-        px = jnp.where(is_own, own_x, other_x)
-        pz = jnp.where(is_own, z_own, zo)
-        y = t % ny
-        src = y // yb
-        return ((src * 4 + px) * 6 + pz) * yb + (y - src * yb)
 
     ones = (iota((LANES, 1), 0) // HEAD_DIM == iota((1, LANES), 1) // HEAD_DIM)
     ones = jnp.where(ones, 1.0, 0.0).astype(BF16)
@@ -159,14 +162,14 @@
 
     k = mm(normed, wqkv_ref[D : 2 * D], NT)
     v = mm(normed, wqkv_ref[2 * D : 3 * D], NT)
-    q = mm(query_rows(normed_f).astype(BF16), wqkv_ref[0:D], NT)
+    q = mm(query_rows(normed_f, plane, (0, ny)).astype(BF16), wqkv_ref[0:D], NT)
     rk = lax.rsqrt(head_sums(k * k, ones) * (1.0 / HEAD_DIM) + EPSILON)
     rq = lax.rsqrt(head_sums(q * q, ones) * (1.0 / HEAD_DIM) + EPSILON)
     kb = (k * rk).astype(BF16)
     vb = v.astype(BF16)
     qb = (q * rq * scale).astype(BF16)
-    cot = mm(one_hot_rows(2 * block, 2 * block, cot_source), cot_ref[...])
-    ub = mm(cot.astype(BF16), wout_ref[...]).astype(BF16)
+    up = mm(c_ref[...].reshape(4 * qplane, D), wout_ref[...])
+    ub = query_rows(up, qplane, (qplane, 0)).astype(BF16)
 
     lane = iota((1, QUAD * block), 1)
     is_own = lane < QUAD * inner
@@ -255,7 +258,8 @@
             axis=0,
         )
 
-    q_o, rq_o, cot_o = own_queries(q), own_queries(rq), own_queries(cot)
+    q_o, rq_o = own_queries(q), own_queries(rq)
+    cot_o = jnp.concatenate([c_ref[1 + p].astype(F32)[ny : 5 * ny] for p in range(2)], axis=0)
     k_o, rk_o, x_o, r_o = own_rows(k), own_rows(rk), own_rows(x), own_rows(r)
     dk_o = dk_ref[...]
     gq = dq_ref[...] * scale
@@ -267,13 +271,15 @@
     cot_b = cot_o.astype(BF16)
     normed_b = (x_o * r_o).astype(BF16)
 
-    width = 4 * D // n_gx
+    width = 8 * D // n_gx
     per = D // width
-    for d in range(n_gx):
+    for d in range(pairs):
         part = (gq_b, gk_b, gv_b, cot_b)[d // per]
         off = (d % per) * width
-        send_ref[d, :, 0:width] = part[:, off : off + width]
-        send_ref[d, :, width : width + D] = normed_b if d < 3 * per else att_b
+        full_ref[d, :, 0:width] = part[:, off : off + width]
+        full_ref[d, :, width : width + D] = normed_b if d < 3 * per else att_b
+    for k in range(pairs):
+        send_refs[k][...] = full_ref[(gx // 2) ^ k]
 
     g_norm = mm(gq_b, wqkv_ref[0:D]) + mm(gk_b, wqkv_ref[D : 2 * D]) + mm(gv_b, wqkv_ref[2 * D : 3 * D])
     g_in = r_o * g_norm - x_o * (r_o * r_o * r_o) * jnp.mean(x_o * g_norm, axis=-1, keepdims=True)
@@ -297,26 +303,47 @@
         py = rest // 4
         return px * inner + (rest - py * 4) * ny + dst * yb + py
 
-    out_ref[...] = mm(one_hot_rows(tokens, tokens, out_source), out).astype(BF16)
-
-
-def partial_kernel(recv_ref, out_ref, send_ref, *, width, n_gy, extra):
-    n_gx, tokens, _ = recv_ref.shape
-    both = recv_ref[...].reshape(n_gx * tokens, width + D)
-    partial = mm(both[:, 0:width], both[:, width : width + D], TN).astype(BF16)
-    rows = width // n_gy
+    moved = mm(one_hot_rows(tokens, tokens, out_source), out).astype(BF16)
     for d in range(n_gy):
-        send_ref[d, 0:rows] = partial[d * rows : (d + 1) * rows]
-        send_ref[d, rows : rows + extra] = out_ref[d * extra : (d + 1) * extra]
-
-
-def final_kernel(recv_ref, gw_ref, out_ref, *, rows, extra, factor):
-    n_gy = recv_ref.shape[0]
-    total = recv_ref[0, 0:rows].astype(F32)
-    for s in range(1, n_gy):
-        total = total + recv_ref[s, 0:rows].astype(F32)
+        out_ref[d] = moved[d * 8 * yb : (d + 1) * 8 * yb]
+
+
+def partial_kernel(*refs):
+    ins, (mine_ref, other_ref, both_ref) = refs[:-3], refs[-3:]
+    width = mine_ref.shape[0]
+    left = jnp.concatenate([ref[:, 0 : 2 * width] for ref in ins], axis=0)
+    right = jnp.concatenate([ref[:, 2 * width :] for ref in ins], axis=0)
+    partial = mm(left, right, TN)
+    both_ref[0] = partial[0:width]
+    both_ref[1] = partial[width:]
+    odd = lax.axis_index("gx") % 2
+    mine_ref[...] = both_ref[odd]
+    other_ref[...] = both_ref[1 - odd].astype(BF16)
+
+
+def scatter_kernel(mine_ref, other_ref, out_ref, keep_ref, *refs, n_gy):
+    sends, sum_ref = refs[:-1], refs[-1]
+    rows, extra = keep_ref.shape[0], out_ref.shape[1]
+    total = mine_ref[...] + other_ref[...].astype(F32)
+    for d in range(n_gy):
+        sum_ref[d] = total[d * rows : (d + 1) * rows]
+    gy = lax.axis_index("gy")
+    keep_ref[...] = sum_ref[gy]
+    for k in range(1, n_gy):
+        sends[k - 1][0:rows] = sum_ref[gy ^ k].astype(BF16)
+        sends[k - 1][rows : rows + extra] = out_ref[gy ^ k]
+
+
+def final_kernel(keep_ref, own_ref, *refs, n_gy, factor):
+    ins, (gw_ref, out_ref, got_ref) = refs[:-3], refs[-3:]
+    rows, extra = keep_ref.shape[0], own_ref.shape[1]
+    gy = lax.axis_index("gy")
+    total = keep_ref[...]
+    got_ref[gy] = own_ref[gy]
+    for k in range(1, n_gy):
+        total = total + ins[k - 1][0:rows].astype(F32)
+        got_ref[gy ^ k] = ins[k - 1][rows : rows + extra]
     gw_ref[...] = total * factor
-    got = jnp.concatenate([recv_ref[s, rows : rows + extra] for s in range(n_gy)], axis=0)
 
     def source(i):
         xy = i // (4 * n_gy)
@@ -324,14 +351,14 @@
         src = rest // 4
         return src * extra + xy * 4 + rest - src * 4
 
+    got = got_ref[...].reshape(n_gy * extra, D)
     out_ref[...] = mm(one_hot_rows(n_gy * extra, n_gy * extra, source), got).astype(BF16)
 
 
-def matchings(count, wrap):
+def matchings(count):
     first = [(i, i ^ 1) for i in range(count)]
-    ends = [(0, count - 1), (count - 1, 0)] if wrap else [(0, 0), (count - 1, count - 1)]
-    second = ends + [(i, i + 1) for i in range(1, count - 1, 2)]
-    second += [(i + 1, i) for i in range(1, count - 1, 2)]
+    second = [((i - 1) % count, i) for i in range(0, count, 2)]
+    second += [(t, s) for s, t in second]
     return first, second
 
 
@@ -359,35 +386,56 @@
     assert size_x == 2 and size_z == 4 and cotangent.shape[0] == 2
     assert cotangent.shape[2] == total_z and yb * n_gy == ny
     tokens = size_x * ny * size_z
-    gx1, gx2 = matchings(n_gx, True)
-    gy1, gy2 = matchings(n_gy, False)
+    gx1, gx2 = matchings(n_gx)
+    gy1, gy2 = matchings(n_gy)
+
+    def swapped(value, axis, k):
+        count = lax.axis_size(axis)
+        return lax.ppermute(value, axis, [(i, i ^ k) for i in range(count)])
 
     own = jnp.transpose(slab_tokens, (0, 2, 1, 3)).reshape(tokens, D)
-    cot = cotangent.reshape(2, yb * total_z, D)
-    x_payload = ((tokens + yb * total_z, D), BF16)
-    p1, p2 = call(pack_x_kernel, "pack_x", (own, cot), (x_payload, x_payload))
+    cot = cotangent.reshape(2 * yb * total_z, D)
+    window, edges = 12 * yb, 4 * ny
+    merged = n_gy == 4
+    sizes = [window + (edges if k == 1 or (merged and k == 3) else 0) for k in range(n_gy)]
+    if not merged:
+        sizes.append(edges)
+    packed = call(
+        lambda *refs: pack_z_kernel(*refs, ny=ny, n_gy=n_gy),
+        "pack_z",
+        (own, cot),
+        [((s, D), BF16) for s in sizes],
+    )
+    order = [1] + ([3, 2] if merged else list(range(2, n_gy)))
+    moved = {0: packed[0]}
+    for k in order:
+        moved[k] = swapped(packed[k], "gy", k)
+    if not merged:
+        moved[n_gy] = lax.ppermute(packed[n_gy], "gy", gy2)
+    x_payload = ((16 * ny + 6 * ny, D), BF16)
+    p1, p2, ext, cot_own = call(
+        lambda *refs: pack_x_kernel(*refs, ny=ny, n_gy=n_gy),
+        "pack_x",
+        (own,) + tuple(moved[k] for k in range(len(sizes))) + (w_qkv, w_out),
+        (x_payload, x_payload, ((16 * ny, D), BF16), ((2, 6 * ny, D), BF16)),
+    )
     m1 = lax.ppermute(p1, "gx", gx1)
     m2 = lax.ppermute(p2, "gx", gx2)
 
-    z_payload = ((12 * ny, D), BF16)
-    s1, s2, windows = call(
-        lambda *refs: pack_z_kernel(*refs, ny=ny, n_gx=n_gx, n_gy=n_gy),
-        "pack_z",
-        (own, m1, m2, cot),
-        (z_payload, z_payload, ((n_gy, 24 * yb, D), BF16)),
-    )
-    z1 = lax.ppermute(s1, "gy", gy1)
-    z2 = lax.ppermute(s2, "gy", gy2)
-    cot_rows = lax.all_to_all(windows, "gy", 0, 0, tiled=True).reshape(24 * ny, D)
-
     width = 4 * D // n_gx
-    send, out_rows, gin = call(
+    pairs = n_gx // 2
+    extra = tokens // n_gy
+    rows = width // n_gy
+    results = call(
         lambda *refs: main_kernel(*refs, ny=ny, n_gx=n_gx, n_gy=n_gy),
         "layer",
-        (logit_scale, own, m1, m2, z1, z2, cot_rows, w_qkv, w_out),
-        (((n_gx, tokens, width + D), BF16), ((tokens, D), BF16), ((tokens, D), BF16)),
+        (logit_scale, ext, m1, m2, cot_own, w_qkv, w_out),
+        [((tokens, 2 * width + D), BF16)] * pairs
+        + [((n_gy, extra, D), BF16), ((tokens, D), BF16)],
         scratch=(
             ((6, 8 * ny, D), BF16),
+            ((4, 6 * ny, D), BF16),
+            ((pairs, tokens, 2 * width + D), BF16),
             ((32 * ny, QUAD * 12 * ny), F32),
             ((tokens, D), F32),
             ((tokens, D), F32),
@@ -396,23 +444,31 @@
         ),
         smem=1,
     )
-
-    recv = lax.all_to_all(send, "gx", 0, 0, tiled=True)
-    extra = tokens // n_gy
-    rows = width // n_gy
-    (send2,) = call(
-        lambda *refs: partial_kernel(*refs, width=width, n_gy=n_gy, extra=extra),
+    sends, out_rows, gin = results[:pairs], results[pairs], results[pairs + 1]
+    arrived = [sends[0]] + [swapped(sends[k], "gx", 2 * k) for k in range(1, pairs)]
+    mine, other = call(
+        partial_kernel,
         "partial",
-        (recv, out_rows),
-        (((n_gy, rows + extra, D), BF16),),
-    )
-    recv2 = lax.all_to_all(send2, "gy", 0, 0, tiled=True)
+        arrived,
+        (((width, D), F32), ((width, D), BF16)),
+        scratch=(((2, width, D), F32),),
+    )
+    other = swapped(other, "gx", 1)
+    keep, *blocks = call(
+        lambda *refs: scatter_kernel(*refs, n_gy=n_gy),
+        "scatter",
+        (mine, other, out_rows),
+        [((rows, D), F32)] + [((rows + extra, D), BF16)] * (n_gy - 1),
+        scratch=(((n_gy, rows, D), F32),),
+    )
+    blocks = [swapped(blocks[k - 1], "gy", k) for k in range(1, n_gy)]
     factor = 1.0 / math.sqrt(total_x * ny * total_z)
     grad_weights, output = call(
-        lambda *refs: final_kernel(*refs, rows=rows, extra=extra, factor=factor),
+        lambda *refs: final_kernel(*refs, n_gy=n_gy, factor=factor),
         "final",
-        (recv2,),
+        [keep, out_rows] + blocks,
         (((rows, D), F32), ((n_gy * extra, D), BF16)),
+        scratch=(((n_gy, extra, D), BF16),),
     )
     return (
         output.reshape(2, yb, total_z, D),

time: 65.1 us -> 63.1 us (0.969)
  blocking collectives: 16.3 us -> 0 us
  local copies, waits for them, and re-layouts: 4.8 us -> 13.3 us
  waiting for transfers between devices: 16.4 us -> 21.8 us
  Pallas kernels: 9.75 us -> 10.6 us
    all_to_all x1 -> x0, blocking collectives: 16.3 us -> none  [on_device(): recv = lax.all_to_all(send, 'gx', 0, 0, tiled=True)]
    ppermute x2 -> x10, waiting for transfers between devices: 4.26 us -> 17.1 us  [swapped(): return lax.ppermute(value, axis, [(i, i ^ k) for i in range(count)])]
    ppermute x2 -> x10, starting transfers between devices: 3.56 us -> 13.6 us  [swapped(): return lax.ppermute(value, axis, [(i, i ^ k) for i in range(count)])]
    all_to_all x2 -> x0, waiting for transfers between devices: 9.36 us -> none  [the longest x1 9.07 us: on_device(): recv2 = lax.all_to_all(send2, 'gy', 0, 0, tiled=True)]
    all_to_all x2 -> x0, starting transfers between devices: 9.05 us -> none  [the longest x1 5.04 us: on_device(): lax.all_to_all(windows, 'gy', 0, 0, tiled=True).reshape(24 * ny, D)]
    unnamed x10 -> x24, local copies, waits for them, and re-layouts: 3.29 us -> 10.9 us
    ppermute x1, waiting for transfers between devices: 2.73 us -> 4.65 us  [on_device(): m2 = lax.ppermute(p2, 'gx', gx2)]
    ppermute x1, starting transfers between devices: 3.54 us -> 2.56 us  [on_device(): m2 = lax.ppermute(p2, 'gx', gx2)]
  transfers between devices with their start and end apart: 6 -> 12, of which waited for: 4 -> 7; matrix products, arithmetic and copies ran while one was open for 1% -> 2% of each run, Pallas kernels for 0% -> 0%
where the time goes in v2:
time: 63.1 us; the launch traced here: 62.5 us
  waiting for transfers between devices  21.8 us (35%)
  starting transfers between devices  16.1 us (26%)
  local copies, waits for them, and re-layouts  13.3 us (21%)
  Pallas kernels  10.6 us (17%)
  between operations  0.67 us (1%)
    ppermute x10, waiting for transfers between devices, swapped(): return lax.ppermute(value, axis, [(i, i ^ k) for i in range(count)])  17.1 us
    ppermute x10, starting transfers between devices, swapped(): return lax.ppermute(value, axis, [(i, i ^ k) for i in range(count)])  13.6 us
    unnamed x24, local copies, waits for them, and re-layouts  10.9 us
    pallas_call x6, Pallas kernels, call(): pl.pallas_call(kernel, name=name, out_shape=tuple((jax.ShapeDtypeStruct(s...  10.6 us
    ppermute x1, waiting for transfers between devices, on_device(): m2 = lax.ppermute(p2, 'gx', gx2)  4.65 us
    ppermute x1, starting transfers between devices, on_device(): m2 = lax.ppermute(p2, 'gx', gx2)  2.56 us
    reshape x1, local copies, waits for them, and re-layouts, on_device(): gin.reshape(2, ny, 4, D)  1.49 us
  transfers between devices with their start and end apart: 12, of which 7 were waited for; matrix products, arithmetic and copies ran while one was open for 2% of the time, Pallas kernels for 0%

profile of v2, /device:TPU:0, one launch (start us, length us, event | category | flops | bytes accessed | tf_op | source)
XLA Modules:
  0.0 62.5 jit_solution(9368779595898311353)
XLA Ops:
  0.6 0.9 %copy.8 = bf16[2,4,8,512]{3,2,1,0:T(8,128)(2,1)S(1)} copy(bf16[2,4,8,512]{3,1,2,0:T(4,128)(2,1)} %bitcast.7) | data formatting | bytes 131072 | tf_op jit(solution)/shard_map/transpose | solution.py:396
  1.5 0.0 copy-start.10
  1.5 0.8 %copy-done.10 = bf16[2,2,16,512]{3,2,1,0:T(8,128)(2,1)S(1)} copy-done((bf16[2,2,16,512]{3,2,1,0:T(8,128)(2,1)S(1)}, bf16[2,2,16,512]{3,2,1,0:T(8,128)(2,1)}, u32[]{:S(2)}) %copy-start.10) | copy-done | bytes 65560
  2.3 0.9 %pack_z.1 = (bf16[24,512]{1,0:T(8,128)(2,1)}, bf16[56,512]{1,0:T(8,128)(2,1)}, bf16[24,512]{1,0:T(8,128)(2,1)}, bf16[56,512]{1,0:T(8,128)(2,1)}) custom-call(bf16[64,512]{1,0:T(8,128)(2,1)S(1)} %bitcast.4, bf16[64,512]{1,0:T(8,128)(2,1)S(1)} %bitcast.6), custom_call_target="tpu_custom_call" | custom-call | tf_op jit(solution)/shard_map/pack_z/pallas_call | solution.py:370
  3.2 3.1 %collective-permute-start = (bf16[56,512]{1,0:T(8,128)(2,1)}, bf16[56,512]{1,0:T(8,128)(2,1)S(1)}, u32[]{:S(2)}, u32[]{:S(2)}) collective-permute-start(bf16[56,512]{1,0:T(8,128)(2,1)} %get-tuple-element.26), channel_id=1, source_target_pairs={{0,1},{1,0},{2,3},{3,2},{4,5},{5,4},{6,7},{7,6},{8,9},{9,8},{10,11... | collective-permute-start | bytes 172040 | tf_op jit(solution)/shard_map/ppermute | solution.py:394
  6.2 2.5 %collective-permute-start.2 = (bf16[56,512]{1,0:T(8,128)(2,1)}, bf16[56,512]{1,0:T(8,128)(2,1)S(1)}, u32[]{:S(2)}, u32[]{:S(2)}) collective-permute-start(bf16[56,512]{1,0:T(8,128)(2,1)} %get-tuple-element.28), channel_id=1, source_target_pairs={{0,3},{1,2},{2,1},{3,0},{4,7},{5,6},{6,5},{7,4},{8,11},{9,10},{10,... | collective-permute-start | bytes 172040 | tf_op jit(solution)/shard_map/ppermute | solution.py:394
  8.7 0.1 collective-permute-start.1
  8.8 5.1 %collective-permute-done.1.refs_3_ = bf16[24,512]{1,0:T(8,128)(2,1)S(1)} collective-permute-done((bf16[24,512]{1,0:T(8,128)(2,1)}, bf16[24,512]{1,0:T(8,128)(2,1)S(1)}, u32[]{:S(2)}, u32[]{:S(2)}) %collective-permute-start.1) | collective-permute-done | bytes 24608 | tf_op jit(solution)/shard_map/ppermute | solution.py:394
  13.9 0.0 collective-permute-done.refs_2_
  13.9 0.0 collective-permute-done.2.refs_4_
  13.9 0.0 copy-start
  13.9 1.4 %copy-done = bf16[1536,512]{1,0:T(8,128)(2,1)S(1)} copy-done((bf16[1536,512]{1,0:T(8,128)(2,1)S(1)}, bf16[1536,512]{1,0:T(8,128)(2,1)}, u32[]{:S(2)}) %copy-start) | copy-done | bytes 1572888
  15.3 0.0 copy-start.2
  15.3 1.0 %copy-done.2 = bf16[512,512]{1,0:T(8,128)(2,1)S(1)} copy-done((bf16[512,512]{1,0:T(8,128)(2,1)S(1)}, bf16[512,512]{1,0:T(8,128)(2,1)}, u32[]{:S(2)}) %copy-start.2) | copy-done | bytes 524312
  16.4 0.0 copy-start.11
  16.4 0.7 %copy-done.11 = bf16[24,512]{1,0:T(8,128)(2,1)S(1)} copy-done((bf16[24,512]{1,0:T(8,128)(2,1)S(1)}, bf16[24,512]{1,0:T(8,128)(2,1)}, u32[]{:S(2)}) %copy-start.11) | copy-done | bytes 24600
  17.1 0.0 copy-start.3
  17.1 1.0 %pack_x.1 = (bf16[176,512]{1,0:T(8,128)(2,1)}, bf16[176,512]{1,0:T(8,128)(2,1)}, bf16[128,512]{1,0:T(8,128)(2,1)}, bf16[2,48,512]{2,1,0:T(8,128)(2,1)}) custom-call(bf16[64,512]{1,0:T(8,128)(2,1)S(1)} %bitcast.5, bf16[24,512]{1,0:T(8,128)(2,1)S(1)} %copy-done.11, bf16[56,512]{1,0:T(8,128)(2,1)S(1)} %collective-permute-done.refs_2_, ...), custom_call_target="tpu_custom_call" | custom-call | tf_op jit(solution)/shard_map/pack_x/pallas_call | solution.py:370
  18.1 0.0 collective-permute-start.3
  18.1 2.6 %collective-permute-start.4 = (bf16[176,512]{1,0:T(8,128)(2,1)}, bf16[176,512]{1,0:T(8,128)(2,1)S(1)}, u32[]{:S(2)}, u32[]{:S(2)}) collective-permute-start(bf16[176,512]{1,0:T(8,128)(2,1)} %get-tuple-element.31), channel_id=1, source_target_pairs={{28,0},{4,8},{12,16},{20,24},{0,28},{8,4},{16,12},{24,20},{29,1},{... | collective-permute-start | bytes 540680 | tf_op jit(solution)/shard_map/ppermute | solution.py:423
  20.7 0.0 collective-permute-done.3.refs_2_
  20.7 4.7 %collective-permute-done.4.refs_3_ = bf16[176,512]{1,0:T(8,128)(2,1)S(1)} collective-permute-done((bf16[176,512]{1,0:T(8,128)(2,1)}, bf16[176,512]{1,0:T(8,128)(2,1)S(1)}, u32[]{:S(2)}, u32[]{:S(2)}) %collective-permute-start.4) | collective-permute-done | bytes 180256 | tf_op jit(solution)/shard_map/ppermute | solution.py:423
  25.3 0.0 copy-done.3
  25.3 0.0 copy-start.1
  25.3 1.4 %copy-done.1 = bf16[1536,512]{1,0:T(8,128)(2,1)S(1)} copy-done((bf16[1536,512]{1,0:T(8,128)(2,1)S(1)}, bf16[1536,512]{1,0:T(8,128)(2,1)}, u32[]{:S(2)}) %copy-start.1) | copy-done | bytes 1572888
  26.8 0.0 copy-start.7
  26.8 0.9 %copy-done.7 = bf16[128,512]{1,0:T(8,128)(2,1)S(1)} copy-done((bf16[128,512]{1,0:T(8,128)(2,1)S(1)}, bf16[128,512]{1,0:T(8,128)(2,1)}, u32[]{:S(2)}) %copy-start.7) | copy-done | bytes 131096
  27.7 0.0 copy-start.9
  27.7 0.9 %copy-done.9 = bf16[2,48,512]{2,1,0:T(8,128)(2,1)S(1)} copy-done((bf16[2,48,512]{2,1,0:T(8,128)(2,1)S(1)}, bf16[2,48,512]{2,1,0:T(8,128)(2,1)}, u32[]{:S(2)}) %copy-start.9) | copy-done | bytes 98328
  28.6 5.9 %layer.1 = (bf16[64,1024]{1,0:T(8,128)(2,1)}, bf16[64,1024]{1,0:T(8,128)(2,1)}, bf16[64,1024]{1,0:T(8,128)(2,1)}, bf16[64,1024]{1,0:T(8,128)(2,1)}, bf16[4,16,51...) custom-call(f32[8]{0:T(128)} %refs_0_.1, bf16[128,512]{1,0:T(8,128)(2,1)S(1)} %copy-done.7, ...), custom_call_target="tpu_custom_call" | custom-call | tf_op jit(solution)/shard_map/layer/pallas_call | solution.py:370
  34.4 0.0 collective-permute-start.5
  34.4 2.2 %collective-permute-start.6 = (bf16[64,1024]{1,0:T(8,128)(2,1)}, bf16[64,1024]{1,0:T(8,128)(2,1)S(1)}, u32[]{:S(2)}, u32[]{:S(2)}) collective-permute-start(bf16[64,1024]{1,0:T(8,128)(2,1)} %get-tuple-element.35), channel_id=1, source_target_pairs={{0,16},{4,20},{8,24},{12,28},{16,0},{20,4},{24,8},{28,12},{1,17},{... | collective-permute-start | bytes 393224 | tf_op jit(solution)/shard_map/ppermute | solution.py:394
  36.6 1.3 %collective-permute-start.7 = (bf16[64,1024]{1,0:T(8,128)(2,1)}, bf16[64,1024]{1,0:T(8,128)(2,1)S(1)}, u32[]{:S(2)}, u32[]{:S(2)}) collective-permute-start(bf16[64,1024]{1,0:T(8,128)(2,1)} %get-tuple-element.36), channel_id=1, source_target_pairs={{0,24},{4,28},{8,16},{12,20},{16,8},{20,12},{24,0},{28,4},{1,25},{... | collective-permute-start | bytes 393224 | tf_op jit(solution)/shard_map/ppermute | solution.py:394
  37.9 2.7 %collective-permute-done.5.refs_1_ = bf16[64,1024]{1,0:T(8,128)(2,1)S(1)} collective-permute-done((bf16[64,1024]{1,0:T(8,128)(2,1)}, bf16[64,1024]{1,0:T(8,128)(2,1)S(1)}, u32[]{:S(2)}, u32[]{:S(2)}) %collective-permute-start.5) | collective-permute-done | bytes 131104 | tf_op jit(solution)/shard_map/ppermute | solution.py:394
  40.6 2.3 %collective-permute-done.6.refs_2_ = bf16[64,1024]{1,0:T(8,128)(2,1)S(1)} collective-permute-done((bf16[64,1024]{1,0:T(8,128)(2,1)}, bf16[64,1024]{1,0:T(8,128)(2,1)S(1)}, u32[]{:S(2)}, u32[]{:S(2)}) %collective-permute-start.6) | collective-permute-done | bytes 131104 | tf_op jit(solution)/shard_map/ppermute | solution.py:394
  42.8 1.1 %collective-permute-done.7.refs_3_ = bf16[64,1024]{1,0:T(8,128)(2,1)S(1)} collective-permute-done((bf16[64,1024]{1,0:T(8,128)(2,1)}, bf16[64,1024]{1,0:T(8,128)(2,1)S(1)}, u32[]{:S(2)}, u32[]{:S(2)}) %collective-permute-start.7) | collective-permute-done | bytes 131104 | tf_op jit(solution)/shard_map/ppermute | solution.py:394
  43.9 0.0 copy-start.8
  43.9 0.9 %copy-done.8 = bf16[64,1024]{1,0:T(8,128)(2,1)S(1)} copy-done((bf16[64,1024]{1,0:T(8,128)(2,1)S(1)}, bf16[64,1024]{1,0:T(8,128)(2,1)}, u32[]{:S(2)}) %copy-start.8) | copy-done | bytes 131096
  44.8 1.3 %partial.1 = (f32[256,512]{1,0:T(8,128)}, bf16[256,512]{1,0:T(8,128)(2,1)}) custom-call(bf16[64,1024]{1,0:T(8,128)(2,1)S(1)} %copy-done.8, bf16[64,1024]{1,0:T(8,128)(2,1)S(1)} %collective-permute-done.5.refs_1_, bf16[64,1024]{1,0:T(8,128)(2,1)S(1)} %collective-permute-done.6.refs_2_, bf16[64,1024]{1,0:T(8,128)(2,1)S(1)} %collective-permute-done.7.refs_3_), custom_call_target="tpu_custom_call" | custom-call | tf_op jit(solution)/shard_map/partial/pallas_call | solution.py:370
  46.2 0.1 collective-permute-start.8
  46.2 1.7 %collective-permute-done.8.refs_1_ = bf16[256,512]{1,0:T(8,128)(2,1)S(1)} collective-permute-done((bf16[256,512]{1,0:T(8,128)(2,1)}, bf16[256,512]{1,0:T(8,128)(2,1)S(1)}, u32[]{:S(2)}, u32[]{:S(2)}) %collective-permute-start.8) | collective-permute-done | bytes 262176 | tf_op jit(solution)/shard_map/ppermute | solution.py:394
  47.9 0.0 copy-start.4
  47.9 1.0 %copy-done.4 = f32[256,512]{1,0:T(8,128)S(1)} copy-done((f32[256,512]{1,0:T(8,128)S(1)}, f32[256,512]{1,0:T(8,128)}, u32[]{:S(2)}) %copy-start.4) | copy-done | bytes 524312
  49.0 0.0 copy-start.5
  49.0 0.8 %copy-done.5 = bf16[4,16,512]{2,1,0:T(8,128)(2,1)S(1)} copy-done((bf16[4,16,512]{2,1,0:T(8,128)(2,1)S(1)}, bf16[4,16,512]{2,1,0:T(8,128)(2,1)}, u32[]{:S(2)}) %copy-start.5) | copy-done | bytes 65560
  49.8 0.8 %scatter.1 = (f32[64,512]{1,0:T(8,128)}, bf16[80,512]{1,0:T(8,128)(2,1)}, bf16[80,512]{1,0:T(8,128)(2,1)}, bf16[80,512]{1,0:T(8,128)(2,1)}) custom-call(f32[256,512]{1,0:T(8,128)S(1)} %copy-done.4, bf16[256,512]{1,0:T(8,128)(2,1)S(1)} %collective-permute-done.8.refs_1_, bf16[4,16,512]{2,1,0:T(8,128)(2,1)S(1)} %copy-done.5), custom_call_target="tpu_custom_call" | custom-call | tf_op jit(solution)/shard_map/scatter/pallas_call | solution.py:370
  50.6 0.5 collective-permute-start.9
  51.1 1.9 %collective-permute-start.10 = (bf16[80,512]{1,0:T(8,128)(2,1)}, bf16[80,512]{1,0:T(8,128)(2,1)S(1)}, u32[]{:S(2)}, u32[]{:S(2)}) collective-permute-start(bf16[80,512]{1,0:T(8,128)(2,1)} %get-tuple-element.42), channel_id=1, source_target_pairs={{0,2},{1,3},{2,0},{3,1},{4,6},{5,7},{6,4},{7,5},{8,10},{9,11},{10,... | collective-permute-start | bytes 245768 | tf_op jit(solution)/shard_map/ppermute | solution.py:394
  53.0 2.0 %collective-permute-start.11 = (bf16[80,512]{1,0:T(8,128)(2,1)}, bf16[80,512]{1,0:T(8,128)(2,1)S(1)}, u32[]{:S(2)}, u32[]{:S(2)}) collective-permute-start(bf16[80,512]{1,0:T(8,128)(2,1)} %get-tuple-element.43), channel_id=1, source_target_pairs={{0,3},{1,2},{2,1},{3,0},{4,7},{5,6},{6,5},{7,4},{8,11},{9,10},{10,... | collective-permute-start | bytes 245768 | tf_op jit(solution)/shard_map/ppermute | solution.py:394
  55.0 1.5 %reshape.21 = bf16[2,8,4,512]{3,2,1,0:T(4,128)(2,1)} reshape(bf16[64,512]{1,0:T(8,128)(2,1)} %get-tuple-element.45) | data formatting | bytes 131072 | tf_op jit(solution)/shard_map/reshape | solution.py:475
  56.5 0.0 collective-permute-done.9.refs_2_
  56.5 4.3 %collective-permute-done.10.refs_3_ = bf16[80,512]{1,0:T(8,128)(2,1)S(1)} collective-permute-done((bf16[80,512]{1,0:T(8,128)(2,1)}, bf16[80,512]{1,0:T(8,128)(2,1)S(1)}, u32[]{:S(2)}, u32[]{:S(2)}) %collective-permute-start.10) | collective-permute-done | bytes 81952 | tf_op jit(solution)/shard_map/ppermute | solution.py:394
  60.8 0.0 collective-permute-done.11.refs_4_
  60.8 0.0 copy-start.6
  60.8 0.9 %copy-done.6 = f32[64,512]{1,0:T(8,128)S(1)} copy-done((f32[64,512]{1,0:T(8,128)S(1)}, f32[64,512]{1,0:T(8,128)}, u32[]{:S(2)}) %copy-start.6) | copy-done | bytes 131096
  61.7 0.8 %final.1 = (f32[64,512]{1,0:T(8,128)}, bf16[64,512]{1,0:T(8,128)(2,1)}) custom-call(f32[64,512]{1,0:T(8,128)S(1)} %copy-done.6, bf16[4,16,512]{2,1,0:T(8,128)(2,1)S(1)} %copy-done.5, bf16[80,512]{1,0:T(8,128)(2,1)S(1)} %collective-permute-done.9.refs_2_, bf16[80,512]{1,0:T(8,128)(2,1)S(1)} %collective-permute-done.10.refs_3_, ...), custom_call_target="tpu_custom_call" | custom-call | tf_op jit(solution)/shard_map/final/pallas_call | solution.py:370
Async XLA Ops:
  1.5 0.8 %copy-start.10 = (bf16[2,2,16,512]{3,2,1,0:T(8,128)(2,1)S(1)}, bf16[2,2,16,512]{3,2,1,0:T(8,128)(2,1)}, u32[]{:S(2)}) copy-start(bf16[2,2,16,512]{3,2,1,0:T(8,128)(2,1)} %param.6) | copy-start | bytes 196612
  3.2 10.7 %collective-permute-start = (bf16[56,512]{1,0:T(8,128)(2,1)}, bf16[56,512]{1,0:T(8,128)(2,1)S(1)}, u32[]{:S(2)}, u32[]{:S(2)}) collective-permute-start(bf16[56,512]{1,0:T(8,128)(2,1)} %get-tuple-element.26), channel_id=1, source_target_pairs={{0,1},{1,0},{2,3},{3,2},{4,5},{5,4},{6,7},{7,6},{8,9},{9,8},{10,11... | collective-permute-start | bytes 172040 | tf_op jit(solution)/shard_map/ppermute | solution.py:394
  6.2 7.7 %collective-permute-start.2 = (bf16[56,512]{1,0:T(8,128)(2,1)}, bf16[56,512]{1,0:T(8,128)(2,1)S(1)}, u32[]{:S(2)}, u32[]{:S(2)}) collective-permute-start(bf16[56,512]{1,0:T(8,128)(2,1)} %get-tuple-element.28), channel_id=1, source_target_pairs={{0,3},{1,2},{2,1},{3,0},{4,7},{5,6},{6,5},{7,4},{8,11},{9,10},{10,... | collective-permute-start | bytes 172040 | tf_op jit(solution)/shard_map/ppermute | solution.py:394
  8.7 5.2 %collective-permute-start.1 = (bf16[24,512]{1,0:T(8,128)(2,1)}, bf16[24,512]{1,0:T(8,128)(2,1)S(1)}, u32[]{:S(2)}, u32[]{:S(2)}) collective-permute-start(bf16[24,512]{1,0:T(8,128)(2,1)} %get-tuple-element.27), channel_id=1, source_target_pairs={{0,2},{1,3},{2,0},{3,1},{4,6},{5,7},{6,4},{7,5},{8,10},{9,11},{10,... | collective-permute-start | bytes 73736 | tf_op jit(solution)/shard_map/ppermute | solution.py:394
  13.9 1.4 %copy-start = (bf16[1536,512]{1,0:T(8,128)(2,1)S(1)}, bf16[1536,512]{1,0:T(8,128)(2,1)}, u32[]{:S(2)}) copy-start(bf16[1536,512]{1,0:T(8,128)(2,1)} %refs_5_.3) | copy-start | bytes 4718596
  15.3 1.0 %copy-start.2 = (bf16[512,512]{1,0:T(8,128)(2,1)S(1)}, bf16[512,512]{1,0:T(8,128)(2,1)}, u32[]{:S(2)}) copy-start(bf16[512,512]{1,0:T(8,128)(2,1)} %refs_6_.3) | copy-start | bytes 1572868
  16.4 0.7 %copy-start.11 = (bf16[24,512]{1,0:T(8,128)(2,1)S(1)}, bf16[24,512]{1,0:T(8,128)(2,1)}, u32[]{:S(2)}) copy-start(bf16[24,512]{1,0:T(8,128)(2,1)} %get-tuple-element.25.refs_1_) | copy-start | bytes 73732
  17.1 8.2 %copy-start.3 = (bf16[512,512]{1,0:T(8,128)(2,1)S(1)}, bf16[512,512]{1,0:T(8,128)(2,1)}, u32[]{:S(2)}) copy-start(bf16[512,512]{1,0:T(8,128)(2,1)} %refs_6_.3) | copy-start | bytes 1572868
  18.1 2.6 %collective-permute-start.3 = (bf16[176,512]{1,0:T(8,128)(2,1)}, bf16[176,512]{1,0:T(8,128)(2,1)S(1)}, u32[]{:S(2)}, u32[]{:S(2)}) collective-permute-start(bf16[176,512]{1,0:T(8,128)(2,1)} %get-tuple-element.30), channel_id=1, source_target_pairs={{0,4},{4,0},{8,12},{12,8},{16,20},{20,16},{24,28},{28,24},{1,5},{5... | collective-permute-start | bytes 540680 | tf_op jit(solution)/shard_map/ppermute | solution.py:422
  18.1 7.2 %collective-permute-start.4 = (bf16[176,512]{1,0:T(8,128)(2,1)}, bf16[176,512]{1,0:T(8,128)(2,1)S(1)}, u32[]{:S(2)}, u32[]{:S(2)}) collective-permute-start(bf16[176,512]{1,0:T(8,128)(2,1)} %get-tuple-element.31), channel_id=1, source_target_pairs={{28,0},{4,8},{12,16},{20,24},{0,28},{8,4},{16,12},{24,20},{29,1},{... | collective-permute-start | bytes 540680 | tf_op jit(solution)/shard_map/ppermute | solution.py:423
  25.3 1.4 %copy-start.1 = (bf16[1536,512]{1,0:T(8,128)(2,1)S(1)}, bf16[1536,512]{1,0:T(8,128)(2,1)}, u32[]{:S(2)}) copy-start(bf16[1536,512]{1,0:T(8,128)(2,1)} %refs_5_.3) | copy-start | bytes 4718596
  26.8 0.9 %copy-start.7 = (bf16[128,512]{1,0:T(8,128)(2,1)S(1)}, bf16[128,512]{1,0:T(8,128)(2,1)}, u32[]{:S(2)}) copy-start(bf16[128,512]{1,0:T(8,128)(2,1)} %get-tuple-element.29.refs_1_) | copy-start | bytes 393220
  27.7 0.9 %copy-start.9 = (bf16[2,48,512]{2,1,0:T(8,128)(2,1)S(1)}, bf16[2,48,512]{2,1,0:T(8,128)(2,1)}, u32[]{:S(2)}) copy-start(bf16[2,48,512]{2,1,0:T(8,128)(2,1)} %get-tuple-element.32.refs_4_) | copy-start | bytes 294916
  34.4 6.1 %collective-permute-start.5 = (bf16[64,1024]{1,0:T(8,128)(2,1)}, bf16[64,1024]{1,0:T(8,128)(2,1)S(1)}, u32[]{:S(2)}, u32[]{:S(2)}) collective-permute-start(bf16[64,1024]{1,0:T(8,128)(2,1)} %get-tuple-element.34), channel_id=1, source_target_pairs={{0,8},{4,12},{8,0},{12,4},{16,24},{20,28},{24,16},{28,20},{1,9},{5... | collective-permute-start | bytes 393224 | tf_op jit(solution)/shard_map/ppermute | solution.py:394
  34.4 8.4 %collective-permute-start.6 = (bf16[64,1024]{1,0:T(8,128)(2,1)}, bf16[64,1024]{1,0:T(8,128)(2,1)S(1)}, u32[]{:S(2)}, u32[]{:S(2)}) collective-permute-start(bf16[64,1024]{1,0:T(8,128)(2,1)} %get-tuple-element.35), channel_id=1, source_target_pairs={{0,16},{4,20},{8,24},{12,28},{16,0},{20,4},{24,8},{28,12},{1,17},{... | collective-permute-start | bytes 393224 | tf_op jit(solution)/shard_map/ppermute | solution.py:394
  36.6 7.3 %collective-permute-start.7 = (bf16[64,1024]{1,0:T(8,128)(2,1)}, bf16[64,1024]{1,0:T(8,128)(2,1)S(1)}, u32[]{:S(2)}, u32[]{:S(2)}) collective-permute-start(bf16[64,1024]{1,0:T(8,128)(2,1)} %get-tuple-element.36), channel_id=1, source_target_pairs={{0,24},{4,28},{8,16},{12,20},{16,8},{20,12},{24,0},{28,4},{1,25},{... | collective-permute-start | bytes 393224 | tf_op jit(solution)/shard_map/ppermute | solution.py:394
  43.9 0.9 %copy-start.8 = (bf16[64,1024]{1,0:T(8,128)(2,1)S(1)}, bf16[64,1024]{1,0:T(8,128)(2,1)}, u32[]{:S(2)}) copy-start(bf16[64,1024]{1,0:T(8,128)(2,1)} %get-tuple-element.33.refs_0_) | copy-start | bytes 393220
  46.2 1.7 %collective-permute-start.8 = (bf16[256,512]{1,0:T(8,128)(2,1)}, bf16[256,512]{1,0:T(8,128)(2,1)S(1)}, u32[]{:S(2)}, u32[]{:S(2)}) collective-permute-start(bf16[256,512]{1,0:T(8,128)(2,1)} %get-tuple-element.38), channel_id=1, source_target_pairs={{0,4},{4,0},{8,12},{12,8},{16,20},{20,16},{24,28},{28,24},{1,5},{5... | collective-permute-start | bytes 786440 | tf_op jit(solution)/shard_map/ppermute | solution.py:394
  47.9 1.0 %copy-start.4 = (f32[256,512]{1,0:T(8,128)S(1)}, f32[256,512]{1,0:T(8,128)}, u32[]{:S(2)}) copy-start(f32[256,512]{1,0:T(8,128)} %get-tuple-element.37.refs_0_) | copy-start | bytes 1572868
  49.0 0.8 %copy-start.5 = (bf16[4,16,512]{2,1,0:T(8,128)(2,1)S(1)}, bf16[4,16,512]{2,1,0:T(8,128)(2,1)}, u32[]{:S(2)}) copy-start(bf16[4,16,512]{2,1,0:T(8,128)(2,1)} %get-tuple-element.39.refs_2_.refs_1_) | copy-start | bytes 196612
  50.6 5.9 %collective-permute-start.9 = (bf16[80,512]{1,0:T(8,128)(2,1)}, bf16[80,512]{1,0:T(8,128)(2,1)S(1)}, u32[]{:S(2)}, u32[]{:S(2)}) collective-permute-start(bf16[80,512]{1,0:T(8,128)(2,1)} %get-tuple-element.41), channel_id=1, source_target_pairs={{0,1},{1,0},{2,3},{3,2},{4,5},{5,4},{6,7},{7,6},{8,9},{9,8},{10,11... | collective-permute-start | bytes 245768 | tf_op jit(solution)/shard_map/ppermute | solution.py:394
  51.1 9.7 %collective-permute-start.10 = (bf16[80,512]{1,0:T(8,128)(2,1)}, bf16[80,512]{1,0:T(8,128)(2,1)S(1)}, u32[]{:S(2)}, u32[]{:S(2)}) collective-permute-start(bf16[80,512]{1,0:T(8,128)(2,1)} %get-tuple-element.42), channel_id=1, source_target_pairs={{0,2},{1,3},{2,0},{3,1},{4,6},{5,7},{6,4},{7,5},{8,10},{9,11},{10,... | collective-permute-start | bytes 245768 | tf_op jit(solution)/shard_map/ppermute | solution.py:394
  53.0 7.8 %collective-permute-start.11 = (bf16[80,512]{1,0:T(8,128)(2,1)}, bf16[80,512]{1,0:T(8,128)(2,1)S(1)}, u32[]{:S(2)}, u32[]{:S(2)}) collective-permute-start(bf16[80,512]{1,0:T(8,128)(2,1)} %get-tuple-element.43), channel_id=1, source_target_pairs={{0,3},{1,2},{2,1},{3,0},{4,7},{5,6},{6,5},{7,4},{8,11},{9,10},{10,... | collective-permute-start | bytes 245768 | tf_op jit(solution)/shard_map/ppermute | solution.py:394
  60.8 0.9 %copy-start.6 = (f32[64,512]{1,0:T(8,128)S(1)}, f32[64,512]{1,0:T(8,128)}, u32[]{:S(2)}) copy-start(f32[64,512]{1,0:T(8,128)} %get-tuple-element.40.refs_0_) | copy-start | bytes 393220

commit v3 on v2

--- a/solution.py
+++ b/solution.py
@@ -76,7 +76,7 @@
 
 
 def pack_x_kernel(own_ref, *refs, ny, n_gy):
-    ins, (w1_ref, w2_ref, m1_ref, m2_ref, ext_ref, cot_ref) = refs[:-6], refs[-6:]
+    ins, (m1_ref, m2_ref, ext_ref, cot_ref) = refs[:-4], refs[-4:]
     inner = 4 * ny
     plane = 8 * ny
     edge = 2 * ny
@@ -362,18 +362,23 @@
     return first, second
 
 
-def call(kernel, name, args, outs, scratch=(), smem=0):
+def call(kernel, name, args, outs, scratch=(), smem=0, results=0, limit=8):
     vmem = pl.BlockSpec(memory_space=pltpu.VMEM)
     args = list(args[:smem]) + [
         pltpu.with_memory_space_constraint(a, pltpu.VMEM) for a in args[smem:]
     ]
+    inner = len(outs) - results
     return pl.pallas_call(
         kernel,
         name=name,
-        out_shape=tuple(jax.ShapeDtypeStruct(s, t) for s, t in outs),
+        out_shape=tuple(
+            pltpu.VMEM(s, t) if i < inner else jax.ShapeDtypeStruct(s, t)
+            for i, (s, t) in enumerate(outs)
+        ),
         in_specs=[pl.BlockSpec(memory_space=pltpu.SMEM)] * smem + [vmem] * (len(args) - smem),
         out_specs=(vmem,) * len(outs),
         scratch_shapes=[pltpu.VMEM(s, t) for s, t in scratch],
+        compiler_params=pltpu.CompilerParams(vmem_limit_bytes=limit << 20),
     )(*args)
 
 
@@ -416,7 +421,7 @@
     p1, p2, ext, cot_own = call(
         lambda *refs: pack_x_kernel(*refs, ny=ny, n_gy=n_gy),
         "pack_x",
-        (own,) + tuple(moved[k] for k in range(len(sizes))) + (w_qkv, w_out),
+        (own,) + tuple(moved[k] for k in range(len(sizes))),
         (x_payload, x_payload, ((16 * ny, D), BF16), ((2, 6 * ny, D), BF16)),
     )
     m1 = lax.ppermute(p1, "gx", gx1)
@@ -443,6 +448,7 @@
             ((tokens, D), F32),
         ),
         smem=1,
+        limit=24,
     )
     sends, out_rows, gin = results[:pairs], results[pairs], results[pairs + 1]
     arrived = [sends[0]] + [swapped(sends[k], "gx", 2 * k) for k in range(1, pairs)]
@@ -452,6 +458,7 @@
         arrived,
         (((width, D), F32), ((width, D), BF16)),
         scratch=(((2, width, D), F32),),
+        limit=12,
     )
     other = swapped(other, "gx", 1)
     keep, *blocks = call(
@@ -469,6 +476,7 @@
         [keep, out_rows] + blocks,
         (((rows, D), F32), ((n_gy * extra, D), BF16)),
         scratch=(((n_gy, extra, D), BF16),),
+        results=2,
     )
     return (
         output.reshape(2, yb, total_z, D),

time: 63.1 us -> 51.2 us (0.81)
  local copies, waits for them, and re-layouts: 13.3 us -> 5.44 us
  Pallas kernels: 10.6 us -> 6.83 us
    unnamed x24 -> x8, local copies, waits for them, and re-layouts: 10.9 us -> 3.94 us
    pallas_call x6, Pallas kernels: 10.6 us -> 6.83 us  [call(): pl.pallas_call(kernel, name=name, out_shape=tuple((pltpu.VMEM(s, t) if i...]
    reshape x1, local copies, waits for them, and re-layouts: 1.49 us -> 0.65 us  [on_device(): gin.reshape(2, ny, 4, D)]
  transfers between devices with their start and end apart: 12 -> 12, of which waited for: 7 -> 8; matrix products, arithmetic and copies ran while one was open for 2% -> 1% of each run, Pallas kernels for 0% -> 0%
where the time goes in v3:
time: 51.2 us; the launch traced here: 51 us
  waiting for transfers between devices  21.6 us (42%)
  starting transfers between devices  16.4 us (32%)
  Pallas kernels  6.83 us (13%)
  local copies, waits for them, and re-layouts  5.44 us (11%)
  between operations  0.69 us (1%)
    ppermute x10, waiting for transfers between devices, swapped(): return lax.ppermute(value, axis, [(i, i ^ k) for i in range(count)])  17 us
    ppermute x10, starting transfers between devices, swapped(): return lax.ppermute(value, axis, [(i, i ^ k) for i in range(count)])  13.8 us
    pallas_call x6, Pallas kernels, call(): pl.pallas_call(kernel, name=name, out_shape=tuple((pltpu.VMEM(s, t) if i...  6.83 us
    ppermute x1, waiting for transfers between devices, on_device(): m2 = lax.ppermute(p2, 'gx', gx2)  4.59 us
    unnamed x8, local copies, waits for them, and re-layouts  3.94 us
    ppermute x1, starting transfers between devices, on_device(): m2 = lax.ppermute(p2, 'gx', gx2)  2.55 us
  transfers between devices with their start and end apart: 12, of which 8 were waited for; matrix products, arithmetic and copies ran while one was open for 1% of the time, Pallas kernels for 0%

profile of v3, /device:TPU:0, one launch (start us, length us, event | category | flops | bytes accessed | tf_op | source)
XLA Modules:
  0.0 51.0 jit_solution(1708762553714259169)
XLA Ops:
  0.6 0.9 %copy.8 = bf16[2,4,8,512]{3,2,1,0:T(8,128)(2,1)S(1)} copy(bf16[2,4,8,512]{3,1,2,0:T(4,128)(2,1)} %bitcast.7) | data formatting | bytes 131072 | tf_op jit(solution)/shard_map/transpose | solution.py:401
  1.5 0.0 copy-start.2
  1.5 0.8 %copy-done.2 = bf16[2,2,16,512]{3,2,1,0:T(8,128)(2,1)S(1)} copy-done((bf16[2,2,16,512]{3,2,1,0:T(8,128)(2,1)S(1)}, bf16[2,2,16,512]{3,2,1,0:T(8,128)(2,1)}, u32[]{:S(2)}) %copy-start.2) | copy-done | bytes 65560
  2.3 0.2 pack_z.1
  2.6 3.1 %collective-permute-start = (bf16[56,512]{1,0:T(8,128)(2,1)S(1)}, bf16[56,512]{1,0:T(8,128)(2,1)S(1)}, u32[]{:S(2)}, u32[]{:S(2)}) collective-permute-start(bf16[56,512]{1,0:T(8,128)(2,1)S(1)} %get-tuple-element.26), channel_id=1, source_target_pairs={{0,1},{1,0},{2,3},{3,2},{4,5},{5,4},{6,7},{7,6},{8,9},{9,8},{10,11... | collective-permute-start | bytes 172040 | tf_op jit(solution)/shard_map/ppermute | solution.py:399
  5.7 2.5 %collective-permute-start.2 = (bf16[56,512]{1,0:T(8,128)(2,1)S(1)}, bf16[56,512]{1,0:T(8,128)(2,1)S(1)}, u32[]{:S(2)}, u32[]{:S(2)}) collective-permute-start(bf16[56,512]{1,0:T(8,128)(2,1)S(1)} %get-tuple-element.28), channel_id=1, source_target_pairs={{0,3},{1,2},{2,1},{3,0},{4,7},{5,6},{6,5},{7,4},{8,11},{9,10},{10,... | collective-permute-start | bytes 172040 | tf_op jit(solution)/shard_map/ppermute | solution.py:399
  8.1 0.1 collective-permute-start.1
  8.2 4.9 %collective-permute-done.1.refs_3_ = bf16[24,512]{1,0:T(8,128)(2,1)S(1)} collective-permute-done((bf16[24,512]{1,0:T(8,128)(2,1)S(1)}, bf16[24,512]{1,0:T(8,128)(2,1)S(1)}, u32[]{:S(2)}, u32[]{:S(2)}) %collective-permute-start.1) | collective-permute-done | bytes 24608 | tf_op jit(solution)/shard_map/ppermute | solution.py:399
  13.1 0.0 collective-permute-done.refs_2_
  13.1 0.0 collective-permute-done.2.refs_4_
  13.1 0.2 pack_x.1
  13.3 0.1 collective-permute-start.3
  13.4 2.5 %collective-permute-start.4 = (bf16[176,512]{1,0:T(8,128)(2,1)S(1)}, bf16[176,512]{1,0:T(8,128)(2,1)S(1)}, u32[]{:S(2)}, u32[]{:S(2)}) collective-permute-start(bf16[176,512]{1,0:T(8,128)(2,1)S(1)} %get-tuple-element.31), channel_id=1, source_target_pairs={{28,0},{4,8},{12,16},{20,24},{0,28},{8,4},{16,12},{24,20},{29,1},{... | collective-permute-start | bytes 540680 | tf_op jit(solution)/shard_map/ppermute | solution.py:428
  16.0 0.0 collective-permute-done.3.refs_2_
  16.0 4.6 %collective-permute-done.4.refs_3_ = bf16[176,512]{1,0:T(8,128)(2,1)S(1)} collective-permute-done((bf16[176,512]{1,0:T(8,128)(2,1)S(1)}, bf16[176,512]{1,0:T(8,128)(2,1)S(1)}, u32[]{:S(2)}, u32[]{:S(2)}) %collective-permute-start.4) | collective-permute-done | bytes 180256 | tf_op jit(solution)/shard_map/ppermute | solution.py:428
  20.6 0.0 copy-start
  20.6 1.4 %copy-done = bf16[1536,512]{1,0:T(8,128)(2,1)S(1)} copy-done((bf16[1536,512]{1,0:T(8,128)(2,1)S(1)}, bf16[1536,512]{1,0:T(8,128)(2,1)}, u32[]{:S(2)}) %copy-start) | copy-done | bytes 1572888
  22.0 0.0 copy-start.1
  22.0 1.0 %copy-done.1 = bf16[512,512]{1,0:T(8,128)(2,1)S(1)} copy-done((bf16[512,512]{1,0:T(8,128)(2,1)S(1)}, bf16[512,512]{1,0:T(8,128)(2,1)}, u32[]{:S(2)}) %copy-start.1) | copy-done | bytes 524312
  23.0 0.0 copy-start.3
  23.0 0.7 %copy-done.3 = f32[8]{0:T(128)S(1)} copy-done((f32[8]{0:T(128)S(1)}, f32[8]{0:T(128)}, u32[]{:S(2)}) %copy-start.3) | copy-done | bytes 56
  23.7 5.1 %layer.1 = (bf16[64,1024]{1,0:T(8,128)(2,1)S(1)}, bf16[64,1024]{1,0:T(8,128)(2,1)S(1)}, bf16[64,1024]{1,0:T(8,128)(2,1)S(1)}, bf16[64,1024]{1,0:T(8,128)(2,1)S(1...) custom-call(f32[8]{0:T(128)S(1)} %copy-done.3, bf16[128,512]{1,0:T(8,128)(2,1)S(1)} %get-tuple-element.29.refs_1_, ...), custom_call_target="tpu_custom_call" | custom-call | tf_op jit(solution)/shard_map/layer/pallas_call | solution.py:371
  28.7 0.0 collective-permute-start.5
  28.8 2.2 %collective-permute-start.6 = (bf16[64,1024]{1,0:T(8,128)(2,1)S(1)}, bf16[64,1024]{1,0:T(8,128)(2,1)S(1)}, u32[]{:S(2)}, u32[]{:S(2)}) collective-permute-start(bf16[64,1024]{1,0:T(8,128)(2,1)S(1)} %get-tuple-element.35), channel_id=1, source_target_pairs={{0,16},{4,20},{8,24},{12,28},{16,0},{20,4},{24,8},{28,12},{1,17},{... | collective-permute-start | bytes 393224 | tf_op jit(solution)/shard_map/ppermute | solution.py:399
  31.0 1.3 %collective-permute-start.7 = (bf16[64,1024]{1,0:T(8,128)(2,1)S(1)}, bf16[64,1024]{1,0:T(8,128)(2,1)S(1)}, u32[]{:S(2)}, u32[]{:S(2)}) collective-permute-start(bf16[64,1024]{1,0:T(8,128)(2,1)S(1)} %get-tuple-element.36), channel_id=1, source_target_pairs={{0,24},{4,28},{8,16},{12,20},{16,8},{20,12},{24,0},{28,4},{1,25},{... | collective-permute-start | bytes 393224 | tf_op jit(solution)/shard_map/ppermute | solution.py:399
  32.3 2.4 %collective-permute-done.5.refs_1_ = bf16[64,1024]{1,0:T(8,128)(2,1)S(1)} collective-permute-done((bf16[64,1024]{1,0:T(8,128)(2,1)S(1)}, bf16[64,1024]{1,0:T(8,128)(2,1)S(1)}, u32[]{:S(2)}, u32[]{:S(2)}) %collective-permute-start.5) | collective-permute-done | bytes 131104 | tf_op jit(solution)/shard_map/ppermute | solution.py:399
  34.6 2.2 %collective-permute-done.6.refs_2_ = bf16[64,1024]{1,0:T(8,128)(2,1)S(1)} collective-permute-done((bf16[64,1024]{1,0:T(8,128)(2,1)S(1)}, bf16[64,1024]{1,0:T(8,128)(2,1)S(1)}, u32[]{:S(2)}, u32[]{:S(2)}) %collective-permute-start.6) | collective-permute-done | bytes 131104 | tf_op jit(solution)/shard_map/ppermute | solution.py:399
  36.8 1.1 %collective-permute-done.7.refs_3_ = bf16[64,1024]{1,0:T(8,128)(2,1)S(1)} collective-permute-done((bf16[64,1024]{1,0:T(8,128)(2,1)S(1)}, bf16[64,1024]{1,0:T(8,128)(2,1)S(1)}, u32[]{:S(2)}, u32[]{:S(2)}) %collective-permute-start.7) | collective-permute-done | bytes 131104 | tf_op jit(solution)/shard_map/ppermute | solution.py:399
  37.9 0.4 partial.1
  38.4 0.1 collective-permute-start.8
  38.5 1.5 %collective-permute-done.8.refs_1_ = bf16[256,512]{1,0:T(8,128)(2,1)S(1)} collective-permute-done((bf16[256,512]{1,0:T(8,128)(2,1)S(1)}, bf16[256,512]{1,0:T(8,128)(2,1)S(1)}, u32[]{:S(2)}, u32[]{:S(2)}) %collective-permute-start.8) | collective-permute-done | bytes 262176 | tf_op jit(solution)/shard_map/ppermute | solution.py:399
  40.0 0.1 scatter.1
  40.1 0.6 %collective-permute-start.9 = (bf16[80,512]{1,0:T(8,128)(2,1)S(1)}, bf16[80,512]{1,0:T(8,128)(2,1)S(1)}, u32[]{:S(2)}, u32[]{:S(2)}) collective-permute-start(bf16[80,512]{1,0:T(8,128)(2,1)S(1)} %get-tuple-element.41), channel_id=1, source_target_pairs={{0,1},{1,0},{2,3},{3,2},{4,5},{5,4},{6,7},{7,6},{8,9},{9,8},{10,11... | collective-permute-start | bytes 245768 | tf_op jit(solution)/shard_map/ppermute | solution.py:399
  40.7 1.9 %collective-permute-start.10 = (bf16[80,512]{1,0:T(8,128)(2,1)S(1)}, bf16[80,512]{1,0:T(8,128)(2,1)S(1)}, u32[]{:S(2)}, u32[]{:S(2)}) collective-permute-start(bf16[80,512]{1,0:T(8,128)(2,1)S(1)} %get-tuple-element.42), channel_id=1, source_target_pairs={{0,2},{1,3},{2,0},{3,1},{4,6},{5,7},{6,4},{7,5},{8,10},{9,11},{10,... | collective-permute-start | bytes 245768 | tf_op jit(solution)/shard_map/ppermute | solution.py:399
  42.6 2.0 %collective-permute-start.11 = (bf16[80,512]{1,0:T(8,128)(2,1)S(1)}, bf16[80,512]{1,0:T(8,128)(2,1)S(1)}, u32[]{:S(2)}, u32[]{:S(2)}) collective-permute-start(bf16[80,512]{1,0:T(8,128)(2,1)S(1)} %get-tuple-element.43), channel_id=1, source_target_pairs={{0,3},{1,2},{2,1},{3,0},{4,7},{5,6},{6,5},{7,4},{8,11},{9,10},{10,... | collective-permute-start | bytes 245768 | tf_op jit(solution)/shard_map/ppermute | solution.py:399
  44.5 0.6 %reshape.21 = bf16[2,8,4,512]{3,2,1,0:T(4,128)(2,1)} reshape(bf16[64,512]{1,0:T(8,128)(2,1)S(1)} %get-tuple-element.45) | data formatting | bytes 131072 | tf_op jit(solution)/shard_map/reshape | solution.py:483
  45.2 0.3 collective-permute-done.9.refs_2_
  45.5 4.6 %collective-permute-done.10.refs_3_ = bf16[80,512]{1,0:T(8,128)(2,1)S(1)} collective-permute-done((bf16[80,512]{1,0:T(8,128)(2,1)S(1)}, bf16[80,512]{1,0:T(8,128)(2,1)S(1)}, u32[]{:S(2)}, u32[]{:S(2)}) %collective-permute-start.10) | collective-permute-done | bytes 81952 | tf_op jit(solution)/shard_map/ppermute | solution.py:399
  50.1 0.0 collective-permute-done.11.refs_4_
  50.2 0.8 %final.1 = (f32[64,512]{1,0:T(8,128)}, bf16[64,512]{1,0:T(8,128)(2,1)}) custom-call(f32[64,512]{1,0:T(8,128)S(1)} %get-tuple-element.40.refs_0_, bf16[4,16,512]{2,1,0:T(8,128)(2,1)S(1)} %get-tuple-element.39.refs_2_.refs_1_, bf16[80,512]{1,0:T(8,128)(2,1)S(1)} %collective-permute-done.9.refs_2_, bf16[80,512]{1,0:T(8,128)(2,1)S(1)} %collective-permute-done.10.refs_3_, ...), custom_call_target="tpu_custom_call" | custom-call | tf_op jit(solution)/shard_map/final/pallas_call | solution.py:371
Async XLA Ops:
  1.5 0.8 %copy-start.2 = (bf16[2,2,16,512]{3,2,1,0:T(8,128)(2,1)S(1)}, bf16[2,2,16,512]{3,2,1,0:T(8,128)(2,1)}, u32[]{:S(2)}) copy-start(bf16[2,2,16,512]{3,2,1,0:T(8,128)(2,1)} %param.6) | copy-start | bytes 196612
  2.6 10.6 %collective-permute-start = (bf16[56,512]{1,0:T(8,128)(2,1)S(1)}, bf16[56,512]{1,0:T(8,128)(2,1)S(1)}, u32[]{:S(2)}, u32[]{:S(2)}) collective-permute-start(bf16[56,512]{1,0:T(8,128)(2,1)S(1)} %get-tuple-element.26), channel_id=1, source_target_pairs={{0,1},{1,0},{2,3},{3,2},{4,5},{5,4},{6,7},{7,6},{8,9},{9,8},{10,11... | collective-permute-start | bytes 172040 | tf_op jit(solution)/shard_map/ppermute | solution.py:399
  5.7 7.5 %collective-permute-start.2 = (bf16[56,512]{1,0:T(8,128)(2,1)S(1)}, bf16[56,512]{1,0:T(8,128)(2,1)S(1)}, u32[]{:S(2)}, u32[]{:S(2)}) collective-permute-start(bf16[56,512]{1,0:T(8,128)(2,1)S(1)} %get-tuple-element.28), channel_id=1, source_target_pairs={{0,3},{1,2},{2,1},{3,0},{4,7},{5,6},{6,5},{7,4},{8,11},{9,10},{10,... | collective-permute-start | bytes 172040 | tf_op jit(solution)/shard_map/ppermute | solution.py:399
  8.1 5.0 %collective-permute-start.1 = (bf16[24,512]{1,0:T(8,128)(2,1)S(1)}, bf16[24,512]{1,0:T(8,128)(2,1)S(1)}, u32[]{:S(2)}, u32[]{:S(2)}) collective-permute-start(bf16[24,512]{1,0:T(8,128)(2,1)S(1)} %get-tuple-element.27), channel_id=1, source_target_pairs={{0,2},{1,3},{2,0},{3,1},{4,6},{5,7},{6,4},{7,5},{8,10},{9,11},{10,... | collective-permute-start | bytes 73736 | tf_op jit(solution)/shard_map/ppermute | solution.py:399
  13.3 2.6 %collective-permute-start.3 = (bf16[176,512]{1,0:T(8,128)(2,1)S(1)}, bf16[176,512]{1,0:T(8,128)(2,1)S(1)}, u32[]{:S(2)}, u32[]{:S(2)}) collective-permute-start(bf16[176,512]{1,0:T(8,128)(2,1)S(1)} %get-tuple-element.30), channel_id=1, source_target_pairs={{0,4},{4,0},{8,12},{12,8},{16,20},{20,16},{24,28},{28,24},{1,5},{5... | collective-permute-start | bytes 540680 | tf_op jit(solution)/shard_map/ppermute | solution.py:427
  13.4 7.1 %collective-permute-start.4 = (bf16[176,512]{1,0:T(8,128)(2,1)S(1)}, bf16[176,512]{1,0:T(8,128)(2,1)S(1)}, u32[]{:S(2)}, u32[]{:S(2)}) collective-permute-start(bf16[176,512]{1,0:T(8,128)(2,1)S(1)} %get-tuple-element.31), channel_id=1, source_target_pairs={{28,0},{4,8},{12,16},{20,24},{0,28},{8,4},{16,12},{24,20},{29,1},{... | collective-permute-start | bytes 540680 | tf_op jit(solution)/shard_map/ppermute | solution.py:428
  20.6 1.4 %copy-start = (bf16[1536,512]{1,0:T(8,128)(2,1)S(1)}, bf16[1536,512]{1,0:T(8,128)(2,1)}, u32[]{:S(2)}) copy-start(bf16[1536,512]{1,0:T(8,128)(2,1)} %refs_5_.1) | copy-start | bytes 4718596
  22.0 1.0 %copy-start.1 = (bf16[512,512]{1,0:T(8,128)(2,1)S(1)}, bf16[512,512]{1,0:T(8,128)(2,1)}, u32[]{:S(2)}) copy-start(bf16[512,512]{1,0:T(8,128)(2,1)} %refs_6_.1) | copy-start | bytes 1572868
  23.0 0.7 %copy-start.3 = (f32[8]{0:T(128)S(1)}, f32[8]{0:T(128)}, u32[]{:S(2)}) copy-start(f32[8]{0:T(128)} %refs_0_.1) | copy-start | bytes 100
  28.7 5.9 %collective-permute-start.5 = (bf16[64,1024]{1,0:T(8,128)(2,1)S(1)}, bf16[64,1024]{1,0:T(8,128)(2,1)S(1)}, u32[]{:S(2)}, u32[]{:S(2)}) collective-permute-start(bf16[64,1024]{1,0:T(8,128)(2,1)S(1)} %get-tuple-element.34), channel_id=1, source_target_pairs={{0,8},{4,12},{8,0},{12,4},{16,24},{20,28},{24,16},{28,20},{1,9},{5... | collective-permute-start | bytes 393224 | tf_op jit(solution)/shard_map/ppermute | solution.py:399
  28.8 8.0 %collective-permute-start.6 = (bf16[64,1024]{1,0:T(8,128)(2,1)S(1)}, bf16[64,1024]{1,0:T(8,128)(2,1)S(1)}, u32[]{:S(2)}, u32[]{:S(2)}) collective-permute-start(bf16[64,1024]{1,0:T(8,128)(2,1)S(1)} %get-tuple-element.35), channel_id=1, source_target_pairs={{0,16},{4,20},{8,24},{12,28},{16,0},{20,4},{24,8},{28,12},{1,17},{... | collective-permute-start | bytes 393224 | tf_op jit(solution)/shard_map/ppermute | solution.py:399
  31.0 6.9 %collective-permute-start.7 = (bf16[64,1024]{1,0:T(8,128)(2,1)S(1)}, bf16[64,1024]{1,0:T(8,128)(2,1)S(1)}, u32[]{:S(2)}, u32[]{:S(2)}) collective-permute-start(bf16[64,1024]{1,0:T(8,128)(2,1)S(1)} %get-tuple-element.36), channel_id=1, source_target_pairs={{0,24},{4,28},{8,16},{12,20},{16,8},{20,12},{24,0},{28,4},{1,25},{... | collective-permute-start | bytes 393224 | tf_op jit(solution)/shard_map/ppermute | solution.py:399
  38.4 1.6 %collective-permute-start.8 = (bf16[256,512]{1,0:T(8,128)(2,1)S(1)}, bf16[256,512]{1,0:T(8,128)(2,1)S(1)}, u32[]{:S(2)}, u32[]{:S(2)}) collective-permute-start(bf16[256,512]{1,0:T(8,128)(2,1)S(1)} %get-tuple-element.38), channel_id=1, source_target_pairs={{0,4},{4,0},{8,12},{12,8},{16,20},{20,16},{24,28},{28,24},{1,5},{5... | collective-permute-start | bytes 786440 | tf_op jit(solution)/shard_map/ppermute | solution.py:399
  40.1 5.4 %collective-permute-start.9 = (bf16[80,512]{1,0:T(8,128)(2,1)S(1)}, bf16[80,512]{1,0:T(8,128)(2,1)S(1)}, u32[]{:S(2)}, u32[]{:S(2)}) collective-permute-start(bf16[80,512]{1,0:T(8,128)(2,1)S(1)} %get-tuple-element.41), channel_id=1, source_target_pairs={{0,1},{1,0},{2,3},{3,2},{4,5},{5,4},{6,7},{7,6},{8,9},{9,8},{10,11... | collective-permute-start | bytes 245768 | tf_op jit(solution)/shard_map/ppermute | solution.py:399
  40.7 9.5 %collective-permute-start.10 = (bf16[80,512]{1,0:T(8,128)(2,1)S(1)}, bf16[80,512]{1,0:T(8,128)(2,1)S(1)}, u32[]{:S(2)}, u32[]{:S(2)}) collective-permute-start(bf16[80,512]{1,0:T(8,128)(2,1)S(1)} %get-tuple-element.42), channel_id=1, source_target_pairs={{0,2},{1,3},{2,0},{3,1},{4,6},{5,7},{6,4},{7,5},{8,10},{9,11},{10,... | collective-permute-start | bytes 245768 | tf_op jit(solution)/shard_map/ppermute | solution.py:399
  42.6 7.6 %collective-permute-start.11 = (bf16[80,512]{1,0:T(8,128)(2,1)S(1)}, bf16[80,512]{1,0:T(8,128)(2,1)S(1)}, u32[]{:S(2)}, u32[]{:S(2)}) collective-permute-start(bf16[80,512]{1,0:T(8,128)(2,1)S(1)} %get-tuple-element.43), channel_id=1, source_target_pairs={{0,3},{1,2},{2,1},{3,0},{4,7},{5,6},{6,5},{7,4},{8,11},{9,10},{10,... | collective-permute-start | bytes 245768 | tf_op jit(solution)/shard_map/ppermute | solution.py:399

commit v4 on v3

v4 whole, which is shorter than its diff:
```python
import math

import jax
import jax.numpy as jnp
from jax import lax
from jax.experimental import pallas as pl
from jax.experimental.pallas import tpu as pltpu
from jax.sharding import PartitionSpec as P

D = 512
HEADS = 8
HEAD_DIM = 64
QUAD = 4
LANES = QUAD * HEAD_DIM
EPSILON = 1e-06
NEGATIVE = -1e30
F32 = jnp.float32
BF16 = jnp.bfloat16

NN = (((1,), (0,)), ((), ()))
NT = (((1,), (1,)), ((), ()))
TN = (((0,), (0,)), ((), ()))


def mm(a, b, dims=NN):
    return lax.dot_general(a, b, dims, preferred_element_type=F32)


def iota(shape, dim):
    return lax.broadcasted_iota(jnp.int32, shape, dim)


def head_sums(values, ones):
    high = values.astype(BF16)
    low = (values - high.astype(F32)).astype(BF16)
    return jnp.concatenate(
        [
            mm(high[:, g : g + LANES], ones) + mm(low[:, g : g + LANES], ones)
            for g in range(0, D, LANES)
        ],
        axis=1,
    )


def one_hot_rows(count, columns, source_of):
    return jnp.where(source_of(iota((count, 1), 0)) == iota((1, columns), 1), 1.0, 0.0).astype(BF16)


def pack_z_kernel(slab_hbm, cot_hbm, own_ref, *refs, ny, n_gy):
    inner = 4 * ny
    edge = 2 * ny
    yb = ny // n_gy
    total_z = 4 * n_gy
    window = 12 * yb
    gy = lax.axis_index("gy")
    odd = gy % 2
    outs, (slab_ref, cot_ref, sem_ref) = refs[:-3], refs[-3:]
    slab_copy = pltpu.make_async_copy(slab_hbm, slab_ref, sem_ref.at[0])
    cot_copy = pltpu.make_async_copy(cot_hbm, cot_ref, sem_ref.at[1])
    slab_copy.start()
    cot_copy.start()

    def own_source(i):
        row = i // ny
        px = row // 4
        return (px * ny + i - row * ny) * 4 + row - px * 4

    def source(i):
        k = i // window
        rest = i - k * window
        px = rest // (6 * yb)
        rest = rest - px * (6 * yb)
        pz = rest // yb
        z = 4 * (gy ^ k) - 1 + pz
        return jnp.where((z >= 0) & (z < total_z), (px * yb + rest - pz * yb) * total_z + z, -1)

    moves = one_hot_rows(2 * inner, 2 * inner, own_source)
    windows = one_hot_rows(n_gy * window, 2 * yb * total_z, source)
    slab_copy.wait()
    rows = jnp.concatenate(
        [slab_ref[p, y].astype(F32) for p in range(2) for y in range(ny)], axis=0
    )
    own_ref[...] = mm(moves, rows.astype(BF16)).astype(BF16)
    cot_copy.wait()
    win = mm(windows, cot_ref[...]).astype(BF16)
    for k in range(n_gy):
        outs[k][0:window] = win[k * window : (k + 1) * window]
    last = 3 if n_gy == 4 else n_gy
    base = window if n_gy == 4 else 0
    for ref, start, off in ((outs[1], window, 1 - odd), (outs[last], base, odd)):
        for p in range(2):
            at = pl.multiple_of(p * inner + off * edge, edge)
            ref[start + p * edge : start + (p + 1) * edge] = own_ref[pl.ds(at, edge)]


def pack_x_kernel(own_ref, *refs, ny, n_gy):
    ins, (m1_ref, m2_ref, ext_ref, cot_ref) = refs[:-4], refs[-4:]
    inner = 4 * ny
    plane = 8 * ny
    edge = 2 * ny
    qplane = 6 * ny
    yb = ny // n_gy
    window = 12 * yb
    gx = lax.axis_index("gx")
    gy = lax.axis_index("gy")
    odd = gx % 2
    odd_z = gy % 2
    last = 3 if n_gy == 4 else n_gy
    base = window if n_gy == 4 else 0
    for p in range(2):
        ext_ref[p * plane + edge : p * plane + edge + inner] = own_ref[p * inner : (p + 1) * inner]
        for ref, start, top in ((ins[1], window, 1 - odd_z), (ins[last], base, odd_z)):
            at = pl.multiple_of(p * plane + top * qplane, edge)
            ext_ref[pl.ds(at, edge)] = ref[start + p * edge : start + (p + 1) * edge]
    got = jnp.concatenate([ins[k][0:window].astype(F32) for k in range(n_gy)], axis=0).astype(BF16)

    def source(i):
        row = i // ny
        y = i - row * ny
        src = y // yb
        return ((src ^ gy) * 12 + row) * yb + y - src * yb

    cot = mm(one_hot_rows(2 * qplane, n_gy * window, source), got).astype(BF16)
    cot_ref[0] = cot[0:qplane]
    cot_ref[1] = cot[qplane : 2 * qplane]
    for ref, p in ((m1_ref, 1 - odd), (m2_ref, odd)):
        ref[0 : 2 * plane] = ext_ref[...]
        ref[2 * plane :] = cot_ref[p]


def rms_scale(x):
    return lax.rsqrt(jnp.mean(x * x, axis=-1, keepdims=True) + EPSILON)


def head_ones():
    same = iota((LANES, 1), 0) // HEAD_DIM == iota((1, LANES), 1) // HEAD_DIM
    return jnp.where(same, 1.0, 0.0).astype(BF16)


def head_scale(values, ones):
    return lax.rsqrt(head_sums(values * values, ones) * (1.0 / HEAD_DIM) + EPSILON)


def head_back(values, scale, grad, ones):
    mean = head_sums(values * grad, ones) * (1.0 / HEAD_DIM)
    return (scale * grad - values * (scale * scale * scale) * mean).astype(BF16)


def side_queries(n_ref, own_cot, side_cot, high, ny):
    own, side = n_ref[2 + high], n_ref[1 - high]
    rows = jnp.concatenate(
        [own[2 * ny : 6 * ny], own[ny : 2 * ny], own[6 * ny : 7 * ny], side[ny : 7 * ny]], axis=0
    )
    cots = jnp.concatenate(
        [own_cot[ny : 5 * ny], own_cot[0:ny], own_cot[5 * ny : 6 * ny], side_cot], axis=0
    )
    return rows.astype(BF16), cots.astype(BF16)


def side_attention(
    scale, q, ub, kb, vb, high, ones, bias_ref, gq_ref, att_ref, dq_ref, dk_ref, dv_ref,
    *, ny, n_gx, n_gy,
):
    plane = 8 * ny
    inner = 4 * ny
    edge = 2 * ny
    block = 12 * ny
    total_x, total_z = 2 * n_gx, 4 * n_gy
    gx = lax.axis_index("gx")
    gy = lax.axis_index("gy")
    rq = head_scale(q, ones)
    qb = (q * rq * scale).astype(BF16)

    lane = iota((1, QUAD * block), 1)
    is_own = lane < QUAD * inner
    t_own = lane % inner
    t_oth = (lane - QUAD * inner) % (8 * ny)
    in_edge = t_oth < 2 * ny
    qz = jnp.where(
        is_own,
        2 + t_own // ny,
        jnp.where(in_edge, jnp.where(t_oth < ny, 1, 6), 1 + (t_oth - 2 * ny) // ny),
    )
    qy = lane % ny
    qx = jnp.where(is_own | in_edge, high, 3 * high - 1)
    kj = iota((4 * plane, 1), 0)
    kp = kj // plane
    kr = kj - kp * plane
    kz = kr // ny
    ky = kr - kz * ny
    kx = jnp.where(kp < 2, kp + 4 * high - 2, kp - 2)
    gz = gy * 4 - 2 + kz
    gxk = gx * 2 + kx
    k_ok = (gz >= 0) & (gz < total_z) & (gxk >= 0) & (gxk < total_x)
    ok = (jnp.abs(kz - qz) <= 1) & (jnp.abs(ky - qy) <= 1) & (jnp.abs(kx - qx) <= 1) & k_ok
    bias_ref[...] = jnp.where(ok, 0.0, NEGATIVE)

    lane_head = iota((1, LANES), 1) // HEAD_DIM
    mask = [jnp.where(lane_head == j, 1.0, 0.0).astype(BF16) for j in range(QUAD)]

    def own_keys(values):
        return jnp.concatenate(
            [values[(2 + p) * plane + edge : (2 + p) * plane + edge + inner] for p in range(2)],
            axis=0,
        )

    for g in range(0, D, LANES):
        lanes = slice(g, g + LANES)
        kq, vq = kb[:, lanes], vb[:, lanes]

        def stacked(values):
            return jnp.concatenate(
                [values[0:inner, lanes] * m for m in mask]
                + [values[inner:block, lanes] * m for m in mask],
                axis=0,
            )

        qs = stacked(qb)
        us = stacked(ub)
        s = mm(kq, qs, NT) + bias_ref[...]
        w = jnp.exp(s - jnp.max(s, axis=0, keepdims=True))
        w = w * (1.0 / jnp.sum(w, axis=0, keepdims=True))
        dp = mm(vq, us, NT)
        ds = w * (dp - jnp.sum(w * dp, axis=0, keepdims=True))
        wb = w.astype(BF16)
        dsb = ds.astype(BF16)
        o_all = mm(wb[:, 0 : QUAD * inner], vq, TN)
        dq_all = mm(dsb[:, 0 : QUAD * inner], kq, TN)
        att = o_all[0:inner]
        dq = dq_all[0:inner]
        for j in range(1, QUAD):
            att = jnp.where(lane_head == j, o_all[j * inner : (j + 1) * inner], att)
            dq = jnp.where(lane_head == j, dq_all[j * inner : (j + 1) * inner], dq)
        att_ref[:, lanes] = att.astype(BF16)
        dq_ref[:, lanes] = dq
        dk_ref[:, lanes] = mm(own_keys(dsb), qs)
        dv_ref[:, lanes] = mm(own_keys(wb), us)
    gq_ref[...] = head_back(q[0:inner], rq[0:inner], dq_ref[...] * scale, ones)


def near_kernel(
    ext_ref, m_ref, cot_ref, wqkv_hbm, wout_hbm, ls_hbm,
    wqkv_ref, wout_ref, scale_ref, kb_ref, vb_ref, k_ref, rk_ref, gq_ref, att_ref, dk_ref, dv_ref,
    n_ref, bias_ref, dq_ref, ls_ref, sem_ref,
    *, ny, n_gx, n_gy,
):
    copies = [
        pltpu.make_async_copy(wqkv_hbm.at[pl.ds(i * D, D)], wqkv_ref.at[pl.ds(i * D, D)], sem_ref.at[i])
        for i in range(3)
    ]
    copies.append(pltpu.make_async_copy(wout_hbm, wout_ref, sem_ref.at[3]))
    copies.append(pltpu.make_async_copy(ls_hbm, ls_ref, sem_ref.at[4]))
    for i in (1, 2, 0, 3, 4):
        copies[i].start()
    plane = 8 * ny
    high = 1 - lax.axis_index("gx") % 2
    for i, src in enumerate((m_ref, ext_ref)):
        x = src[0 : 2 * plane].astype(F32)
        n = x * rms_scale(x)
        n_ref[2 * i] = n[0:plane]
        n_ref[2 * i + 1] = n[plane:]
    ones = head_ones()
    normed = n_ref[...].reshape(4 * plane, D).astype(BF16)
    copies[1].wait()
    k = mm(normed, wqkv_ref[D : 2 * D], NT)
    rk = head_scale(k, ones)
    kb = (k * rk).astype(BF16)
    copies[2].wait()
    vb = mm(normed, wqkv_ref[2 * D : 3 * D], NT).astype(BF16)
    kb_ref[...] = kb[2 * plane :]
    vb_ref[...] = vb[2 * plane :]
    for p in range(2):
        at = (2 + p) * plane + 2 * ny
        k_ref[p * 4 * ny : (p + 1) * 4 * ny] = k[at : at + 4 * ny]
        rk_ref[p * 4 * ny : (p + 1) * 4 * ny] = rk[at : at + 4 * ny]
    side_cot = m_ref[2 * plane :].astype(F32)
    rows, cots = side_queries(n_ref, cot_ref[high].astype(F32), side_cot, high, ny)
    copies[0].wait()
    q = mm(rows, wqkv_ref[0:D], NT)
    copies[3].wait()
    copies[4].wait()
    head = iota((1, D), 1) // HEAD_DIM
    scale = jnp.zeros((1, D), F32)
    for h in range(HEADS):
        scale = jnp.where(head == h, ls_ref[h] * (1.0 / HEAD_DIM), scale)
    scale_ref[...] = scale
    ub = mm(cots, wout_ref[...]).astype(BF16)
    side_attention(
        scale, q, ub, kb, vb, high, ones, bias_ref, gq_ref, att_ref, dq_ref, dk_ref, dv_ref,
        ny=ny, n_gx=n_gx, n_gy=n_gy,
    )


def far_kernel(*refs, ny, n_gx, n_gy):
    pairs = n_gx // 2
    ext_ref, m_ref, cot_ref, wqkv_ref, wout_ref, scale_ref, kb_ref, vb_ref, k_ref, rk_ref = refs[:10]
    scale = scale_ref[...]
    gq1_ref, att1_ref, dk1_ref, dv1_ref = refs[10:14]
    send_refs = refs[14 : 14 + pairs]
    g_ref, a_ref = refs[14 + pairs : 16 + pairs]
    n_ref, bias_ref, dq_ref, gq_ref, att_ref, dk_ref, dv_ref, full_ref, b_ref = refs[16 + pairs :]
    plane = 8 * ny
    inner = 4 * ny
    gx = lax.axis_index("gx")
    high = gx % 2
    for i, src in enumerate((m_ref, ext_ref)):
        x = src[0 : 2 * plane].astype(F32)
        n = x * rms_scale(x)
        n_ref[2 * i] = n[0:plane]
        n_ref[2 * i + 1] = n[plane:]
    ones = head_ones()
    normed = n_ref[0:2].reshape(2 * plane, D).astype(BF16)
    k = mm(normed, wqkv_ref[D : 2 * D], NT)
    kb = jnp.concatenate([(k * head_scale(k, ones)).astype(BF16), kb_ref[...]], axis=0)
    v = mm(normed, wqkv_ref[2 * D : 3 * D], NT)
    vb = jnp.concatenate([v.astype(BF16), vb_ref[...]], axis=0)
    inside = jnp.where((gx > 0) & (gx < n_gx - 1), 1.0, 0.0)
    side_cot = m_ref[2 * plane :].astype(F32) * inside
    rows, cots = side_queries(n_ref, cot_ref[high].astype(F32), side_cot, high, ny)
    q = mm(rows, wqkv_ref[0:D], NT)
    ub = mm(cots, wout_ref[...]).astype(BF16)
    side_attention(
        scale, q, ub, kb, vb, high, ones, bias_ref, gq_ref, att_ref, dq_ref, dk_ref, dv_ref,
        ny=ny, n_gx=n_gx, n_gy=n_gy,
    )
    dk = dk1_ref[...] + dk_ref[...]
    gk_b = head_back(k_ref[...], rk_ref[...], dk, ones)
    gv_b = (dv1_ref[...] + dv_ref[...]).astype(BF16)
    b_ref[0, 1 - high] = gq1_ref[...]
    b_ref[0, high] = gq_ref[...]
    b_ref[1, 1 - high] = att1_ref[...]
    b_ref[1, high] = att_ref[...]
    gq_b = b_ref[0].reshape(2 * inner, D)
    att_b = b_ref[1].reshape(2 * inner, D)
    cot_b = jnp.concatenate(
        [cot_ref[p].astype(F32)[ny : 5 * ny] for p in range(2)], axis=0
    ).astype(BF16)
    normed_b = jnp.concatenate([n_ref[2 + p][2 * ny : 6 * ny] for p in range(2)], axis=0).astype(BF16)

    width = 8 * D // n_gx
    per = D // width
    for d in range(pairs):
        part = (gq_b, gk_b, gv_b, cot_b)[d // per]
        off = (d % per) * width
        full_ref[d, :, 0:width] = part[:, off : off + width]
        full_ref[d, :, width : width + D] = normed_b if d < 3 * per else att_b
    for k in range(pairs):
        send_refs[k][...] = full_ref[(gx // 2) ^ k]
    for i, part in enumerate((gq_b, gk_b, gv_b)):
        g_ref[i] = part
    a_ref[...] = att_b


def token_kernel(ext_ref, cot_ref, g_ref, a_ref, wqkv_ref, wout_ref, out_ref, gin_ref, *, ny, n_gy):
    plane = 8 * ny
    inner = 4 * ny
    tokens = 2 * inner
    yb = ny // n_gy
    x = jnp.concatenate(
        [ext_ref[p * plane + 2 * ny : p * plane + 6 * ny].astype(F32) for p in range(2)], axis=0
    )
    r = rms_scale(x)
    cot = jnp.concatenate([cot_ref[p].astype(F32)[ny : 5 * ny] for p in range(2)], axis=0)
    g_norm = mm(g_ref[0], wqkv_ref[0:D])
    for i in range(1, 3):
        g_norm = g_norm + mm(g_ref[i], wqkv_ref[i * D : (i + 1) * D])
    g_in = r * g_norm - x * (r * r * r) * jnp.mean(x * g_norm, axis=-1, keepdims=True)
    gin = (cot + g_in).astype(BF16)

    def gin_source(i):
        px = i // inner
        rest = i - px * inner
        py = rest // 4
        return px * inner + (rest - py * 4) * ny + py

    gin_ref[...] = mm(one_hot_rows(tokens, tokens, gin_source), gin).astype(BF16)

    out = (x + mm(a_ref[...], wout_ref[...], NT)).astype(BF16)

    def out_source(i):
        dst = i // (8 * yb)
        rest = i - dst * (8 * yb)
        px = rest // (4 * yb)
        rest = rest - px * (4 * yb)
        py = rest // 4
        return px * inner + (rest - py * 4) * ny + dst * yb + py

    moved = mm(one_hot_rows(tokens, tokens, out_source), out).astype(BF16)
    for d in range(n_gy):
        out_ref[d] = moved[d * 8 * yb : (d + 1) * 8 * yb]


def partial_kernel(*refs):
    ins, (mine_ref, other_ref, both_ref) = refs[:-3], refs[-3:]
    width = mine_ref.shape[0]
    left = jnp.concatenate([ref[:, 0 : 2 * width] for ref in ins], axis=0)
    right = jnp.concatenate([ref[:, 2 * width :] for ref in ins], axis=0)
    partial = mm(left, right, TN)
    both_ref[0] = partial[0:width]
    both_ref[1] = partial[width:]
    odd = lax.axis_index("gx") % 2
    mine_ref[...] = both_ref[odd]
    other_ref[...] = both_ref[1 - odd].astype(BF16)


def scatter_kernel(mine_ref, other_ref, out_ref, keep_ref, *refs, n_gy):
    sends, sum_ref = refs[:-1], refs[-1]
    rows, extra = keep_ref.shape[0], out_ref.shape[1]
    total = mine_ref[...] + other_ref[...].astype(F32)
    for d in range(n_gy):
        sum_ref[d] = total[d * rows : (d + 1) * rows]
    gy = lax.axis_index("gy")
    keep_ref[...] = sum_ref[gy]
    for k in range(1, n_gy):
        sends[k - 1][0:rows] = sum_ref[gy ^ k].astype(BF16)
        sends[k - 1][rows : rows + extra] = out_ref[gy ^ k]


def final_kernel(keep_ref, own_ref, *refs, n_gy, factor):
    ins, (gw_ref, out_ref, got_ref) = refs[:-3], refs[-3:]
    rows, extra = keep_ref.shape[0], own_ref.shape[1]
    gy = lax.axis_index("gy")
    total = keep_ref[...]
    got_ref[gy] = own_ref[gy]
    for k in range(1, n_gy):
        total = total + ins[k - 1][0:rows].astype(F32)
        got_ref[gy ^ k] = ins[k - 1][rows : rows + extra]
    gw_ref[...] = total * factor

    def source(i):
        xy = i // (4 * n_gy)
        rest = i - xy * (4 * n_gy)
        src = rest // 4
        return src * extra + xy * 4 + rest - src * 4

    got = got_ref[...].reshape(n_gy * extra, D)
    out_ref[...] = mm(one_hot_rows(n_gy * extra, n_gy * extra, source), got).astype(BF16)


def matchings(count):
    first = [(i, i ^ 1) for i in range(count)]
    second = [((i - 1) % count, i) for i in range(0, count, 2)]
    second += [(t, s) for s, t in second]
    return first, second


def call(
    kernel, name, args, outs, scratch=(), scalars=0, semaphores=0, outside=0, results=0, limit=8
):
    vmem = pl.BlockSpec(memory_space=pltpu.VMEM)
    inner = len(args) - outside
    args = list(args)
    for i in range(len(args)):
        space = pltpu.VMEM if i < inner else pltpu.HBM
        args[i] = pltpu.with_memory_space_constraint(args[i], space)
    kept = len(outs) - results
    scratches = [pltpu.VMEM(s, t) for s, t in scratch]
    if scalars:
        scratches.append(pltpu.SMEM((scalars,), F32))
    if semaphores:
        scratches.append(pltpu.SemaphoreType.DMA((semaphores,)))
    return pl.pallas_call(
        kernel,
        name=name,
        out_shape=tuple(
            pltpu.VMEM(s, t) if i < kept else jax.ShapeDtypeStruct(s, t)
            for i, (s, t) in enumerate(outs)
        ),
        in_specs=[vmem] * inner
        + [pl.BlockSpec(memory_space=pltpu.HBM)] * outside,
        out_specs=(vmem,) * len(outs),
        scratch_shapes=scratches,
        compiler_params=pltpu.CompilerParams(vmem_limit_bytes=limit << 20),
    )(*args)


def on_device(slab_tokens, cotangent, w_qkv, w_out, logit_scale):
    size_x, ny, size_z, _ = slab_tokens.shape
    n_gx = lax.axis_size("gx")
    n_gy = lax.axis_size("gy")
    yb = cotangent.shape[1]
    total_x, total_z = size_x * n_gx, size_z * n_gy
    assert size_x == 2 and size_z == 4 and cotangent.shape[0] == 2
    assert cotangent.shape[2] == total_z and yb * n_gy == ny
    tokens = size_x * ny * size_z
    gx1, gx2 = matchings(n_gx)
    gy1, gy2 = matchings(n_gy)

    def swapped(value, axis, k):
        count = lax.axis_size(axis)
        return lax.ppermute(value, axis, [(i, i ^ k) for i in range(count)])

    cot = cotangent.reshape(2 * yb * total_z, D)
    window, edges = 12 * yb, 4 * ny
    merged = n_gy == 4
    sizes = [window + (edges if k == 1 or (merged and k == 3) else 0) for k in range(n_gy)]
    if not merged:
        sizes.append(edges)
    own, *packed = call(
        lambda *refs: pack_z_kernel(*refs, ny=ny, n_gy=n_gy),
        "pack_z",
        (slab_tokens, cot),
        [((tokens, D), BF16)] + [((s, D), BF16) for s in sizes],
        scratch=(((2, ny, 4, D), BF16), ((2 * yb * total_z, D), BF16)),
        semaphores=2,
        outside=2,
    )
    order = [1] + ([3, 2] if merged else list(range(2, n_gy)))
    moved = {0: packed[0]}
    for k in order:
        moved[k] = swapped(packed[k], "gy", k)
    if not merged:
        moved[n_gy] = lax.ppermute(packed[n_gy], "gy", gy2)
    x_payload = ((16 * ny + 6 * ny, D), BF16)
    p1, p2, ext, cot_own = call(
        lambda *refs: pack_x_kernel(*refs, ny=ny, n_gy=n_gy),
        "pack_x",
        (own,) + tuple(moved[k] for k in range(len(sizes))),
        (x_payload, x_payload, ((16 * ny, D), BF16), ((2, 6 * ny, D), BF16)),
    )
    m1 = lax.ppermute(p1, "gx", gx1)
    m2 = lax.ppermute(p2, "gx", gx2)

    width = 4 * D // n_gx
    pairs = n_gx // 2
    extra = tokens // n_gy
    rows = width // n_gy
    dims = dict(ny=ny, n_gx=n_gx, n_gy=n_gy)
    half = tokens // 2
    near = call(
        lambda *refs: near_kernel(*refs, **dims),
        "near",
        (ext, m1, cot_own, w_qkv, w_out, logit_scale),
        (
            ((3 * D, D), BF16),
            ((D, D), BF16),
            ((1, D), F32),
            ((16 * ny, D), BF16),
            ((16 * ny, D), BF16),
            ((tokens, D), F32),
            ((tokens, D), F32),
            ((half, D), BF16),
            ((half, D), BF16),
            ((tokens, D), F32),
            ((tokens, D), F32),
        ),
        scratch=(
            ((4, 8 * ny, D), F32),
            ((32 * ny, QUAD * 12 * ny), F32),
            ((half, D), F32),
        ),
        scalars=HEADS,
        semaphores=5,
        outside=3,
        limit=24,
    )
    wq, wo = near[:2]
    *sends, grads, att = call(
        lambda *refs: far_kernel(*refs, **dims),
        "far",
        (ext, m2, cot_own, wq, wo) + tuple(near[2:]),
        [((tokens, 2 * width + D), BF16)] * pairs + [((3, tokens, D), BF16), ((tokens, D), BF16)],
        scratch=(
            ((4, 8 * ny, D), F32),
            ((32 * ny, QUAD * 12 * ny), F32),
            ((half, D), F32),
            ((half, D), BF16),
            ((half, D), BF16),
            ((tokens, D), F32),
            ((tokens, D), F32),
            ((pairs, tokens, 2 * width + D), BF16),
            ((2, 2, half, D), BF16),
        ),
        limit=24,
    )
    out_rows, gin = call(
        lambda *refs: token_kernel(*refs, ny=ny, n_gy=n_gy),
        "token",
        (ext, cot_own, grads, att, wq, wo),
        (((n_gy, extra, D), BF16), ((tokens, D), BF16)),
    )
    arrived = [sends[0]] + [swapped(sends[k], "gx", 2 * k) for k in range(1, pairs)]
    mine, other = call(
        partial_kernel,
        "partial",
        arrived,
        (((width, D), F32), ((width, D), BF16)),
        scratch=(((2, width, D), F32),),
        limit=12,
    )
    other = swapped(other, "gx", 1)
    keep, *blocks = call(
        lambda *refs: scatter_kernel(*refs, n_gy=n_gy),
        "scatter",
        (mine, other, out_rows),
        [((rows, D), F32)] + [((rows + extra, D), BF16)] * (n_gy - 1),
        scratch=(((n_gy, rows, D), F32),),
    )
    blocks = [swapped(blocks[k - 1], "gy", k) for k in range(1, n_gy)]
    factor = 1.0 / math.sqrt(total_x * ny * total_z)
    grad_weights, output = call(
        lambda *refs: final_kernel(*refs, n_gy=n_gy, factor=factor),
        "final",
        [keep, out_rows] + blocks,
        (((rows, D), F32), ((n_gy * extra, D), BF16)),
        scratch=(((n_gy, extra, D), BF16),),
        results=2,
    )
    return (
        output.reshape(2, yb, total_z, D),
        gin.reshape(2, ny, 4, D),
        grad_weights,
    )


def solution(mesh):
    return jax.shard_map(
        on_device,
        mesh=mesh,
        in_specs=(P("gx", None, "gy", None), P("gx", "gy", None, None), P(), P(), P()),
        out_specs=(P("gx", "gy", None, None), P("gx", None, "gy", None), P(("gx", "gy"), None)),
        check_vma=False,
    )
```

time: 51.2 us -> 44.9 us (0.88)
  waiting for transfers between devices: 21.6 us -> 16.4 us
  local copies, waits for them, and re-layouts: 5.44 us -> 0.65 us
  Pallas kernels: 6.83 us -> 10.5 us
    ppermute x1, waiting for transfers between devices: 4.59 us -> 0.37 us  [on_device(): m2 = lax.ppermute(p2, 'gx', gx2)]
    unnamed x8 -> x0, local copies, waits for them, and re-layouts: 3.94 us -> none
    pallas_call x6 -> x8, Pallas kernels: 6.83 us -> 10.5 us  [call(): pl.pallas_call(kernel, name=name, out_shape=tuple((pltpu.VMEM(s, t) if i...]
    ppermute x10, waiting for transfers between devices: 17 us -> 16.1 us  [swapped(): return lax.ppermute(value, axis, [(i, i ^ k) for i in range(count)])]
    transpose x1 -> x0, local copies, waits for them, and re-layouts: 0.86 us -> none  [on_device(): own = jnp.transpose(slab_tokens, (0, 2, 1, 3)).reshape(tokens, D)]
  transfers between devices with their start and end apart: 12 -> 12, of which waited for: 8 -> 8; matrix products, arithmetic and copies ran while one was open for 1% -> 1% of each run, Pallas kernels for 0% -> 11%
where the time goes in v4:
time: 44.9 us; the launch traced here: 44.8 us
  starting transfers between devices  16.5 us (37%)
  waiting for transfers between devices  16.4 us (37%)
  Pallas kernels  10.5 us (23%)
  between operations  0.7 us (2%)
  local copies, waits for them, and re-layouts  0.65 us (1%)
    ppermute x10, waiting for transfers between devices, swapped(): return lax.ppermute(value, axis, [(i, i ^ k) for i in range(count)])  16.1 us
    ppermute x10, starting transfers between devices, swapped(): return lax.ppermute(value, axis, [(i, i ^ k) for i in range(count)])  13.8 us
    pallas_call x8, Pallas kernels, call(): pl.pallas_call(kernel, name=name, out_shape=tuple((pltpu.VMEM(s, t) if i...  10.5 us
    ppermute x1, starting transfers between devices, on_device(): m2 = lax.ppermute(p2, 'gx', gx2)  2.55 us
  transfers between devices with their start and end apart: 12, of which 8 were waited for; matrix products, arithmetic and copies ran while one was open for 1% of the time, Pallas kernels for 11%

profile of v4, /device:TPU:0, one launch (start us, length us, event | category | flops | bytes accessed | tf_op | source)
XLA Modules:
  0.0 44.8 jit_solution(11292459747513131163)
XLA Ops:
  0.6 1.2 %pack_z.1 = (bf16[64,512]{1,0:T(8,128)(2,1)S(1)}, bf16[24,512]{1,0:T(8,128)(2,1)S(1)}, bf16[56,512]{1,0:T(8,128)(2,1)S(1)}, bf16[24,512]{1,0:T(8,128)(2,1)S(1)}, bf16[56,512]{1,0:T(8,128)(2,1)S(1)}) custom-call(bf16[2,8,4,512]{3,2,1,0:T(4,128)(2,1)} %refs_0_.1, bf16[64,512]{1,0:T(8,128)(2,1)} %bitcast.2), custom_call_target="tpu_custom_call" | custom-call | tf_op jit(solution)/shard_map/pack_z/pallas_call | solution.py:462
  1.8 3.1 %collective-permute-start = (bf16[56,512]{1,0:T(8,128)(2,1)S(1)}, bf16[56,512]{1,0:T(8,128)(2,1)S(1)}, u32[]{:S(2)}, u32[]{:S(2)}) collective-permute-start(bf16[56,512]{1,0:T(8,128)(2,1)S(1)} %get-tuple-element.41), channel_id=1, source_target_pairs={{0,1},{1,0},{2,3},{3,2},{4,5},{5,4},{6,7},{7,6},{8,9},{9,8},{10,11... | collective-permute-start | bytes 172040 | tf_op jit(solution)/shard_map/ppermute | solution.py:491
  4.9 2.5 %collective-permute-start.2 = (bf16[56,512]{1,0:T(8,128)(2,1)S(1)}, bf16[56,512]{1,0:T(8,128)(2,1)S(1)}, u32[]{:S(2)}, u32[]{:S(2)}) collective-permute-start(bf16[56,512]{1,0:T(8,128)(2,1)S(1)} %get-tuple-element.43), channel_id=1, source_target_pairs={{0,3},{1,2},{2,1},{3,0},{4,7},{5,6},{6,5},{7,4},{8,11},{9,10},{10,... | collective-permute-start | bytes 172040 | tf_op jit(solution)/shard_map/ppermute | solution.py:491
  7.4 0.1 collective-permute-start.1
  7.5 4.9 %collective-permute-done.1.refs_3_ = bf16[24,512]{1,0:T(8,128)(2,1)S(1)} collective-permute-done((bf16[24,512]{1,0:T(8,128)(2,1)S(1)}, bf16[24,512]{1,0:T(8,128)(2,1)S(1)}, u32[]{:S(2)}, u32[]{:S(2)}) %collective-permute-start.1) | collective-permute-done | bytes 24608 | tf_op jit(solution)/shard_map/ppermute | solution.py:491
  12.4 0.0 collective-permute-done.refs_2_
  12.4 0.0 collective-permute-done.2.refs_4_
  12.4 0.2 pack_x.1
  12.6 0.1 collective-permute-start.4
  12.7 2.5 %collective-permute-start.3 = (bf16[176,512]{1,0:T(8,128)(2,1)S(1)}, bf16[176,512]{1,0:T(8,128)(2,1)S(1)}, u32[]{:S(2)}, u32[]{:S(2)}) collective-permute-start(bf16[176,512]{1,0:T(8,128)(2,1)S(1)} %get-tuple-element.45), channel_id=1, source_target_pairs={{28,0},{4,8},{12,16},{20,24},{0,28},{8,4},{16,12},{24,20},{29,1},{... | collective-permute-start | bytes 540680 | tf_op jit(solution)/shard_map/ppermute | solution.py:522
  15.2 0.0 collective-permute-done.4.refs_1_
  15.2 4.2 %near.1 = (bf16[1536,512]{1,0:T(8,128)(2,1)S(1)}, bf16[512,512]{1,0:T(8,128)(2,1)S(1)}, f32[1,512]{1,0:T(1,128)S(1)}, bf16[128,512]{1,0:T(8,128)(2,1)S(1)}, bf16...) custom-call(bf16[128,512]{1,0:T(8,128)(2,1)S(1)} %get-tuple-element., ...), custom_call_target="tpu_custom_call" | custom-call | tf_op jit(solution)/shard_map/near/pallas_call | solution.py:462
  19.5 0.4 collective-permute-done.3.refs_1_
  19.8 2.7 %far.1 = (bf16[64,1024]{1,0:T(8,128)(2,1)S(1)}, bf16[64,1024]{1,0:T(8,128)(2,1)S(1)}, bf16[64,1024]{1,0:T(8,128)(2,1)S(1)}, bf16[64,1024]{1,0:T(8,128)(2,1)S(1)}...) custom-call(bf16[128,512]{1,0:T(8,128)(2,1)S(1)} %get-tuple-element.44.refs_0_, ...), custom_call_target="tpu_custom_call" | custom-call | tf_op jit(solution)/shard_map/far/pallas_call | solution.py:462
  22.5 0.1 collective-permute-start.5
  22.6 2.2 %collective-permute-start.6 = (bf16[64,1024]{1,0:T(8,128)(2,1)S(1)}, bf16[64,1024]{1,0:T(8,128)(2,1)S(1)}, u32[]{:S(2)}, u32[]{:S(2)}) collective-permute-start(bf16[64,1024]{1,0:T(8,128)(2,1)S(1)} %get-tuple-element.61), channel_id=1, source_target_pairs={{0,16},{4,20},{8,24},{12,28},{16,0},{20,4},{24,8},{28,12},{1,17},{... | collective-permute-start | bytes 393224 | tf_op jit(solution)/shard_map/ppermute | solution.py:491
  24.8 1.3 %collective-permute-start.7 = (bf16[64,1024]{1,0:T(8,128)(2,1)S(1)}, bf16[64,1024]{1,0:T(8,128)(2,1)S(1)}, u32[]{:S(2)}, u32[]{:S(2)}) collective-permute-start(bf16[64,1024]{1,0:T(8,128)(2,1)S(1)} %get-tuple-element.62), channel_id=1, source_target_pairs={{0,24},{4,28},{8,16},{12,20},{16,8},{20,12},{24,0},{28,4},{1,25},{... | collective-permute-start | bytes 393224 | tf_op jit(solution)/shard_map/ppermute | solution.py:491
  26.1 2.4 %collective-permute-done.5.refs_1_ = bf16[64,1024]{1,0:T(8,128)(2,1)S(1)} collective-permute-done((bf16[64,1024]{1,0:T(8,128)(2,1)S(1)}, bf16[64,1024]{1,0:T(8,128)(2,1)S(1)}, u32[]{:S(2)}, u32[]{:S(2)}) %collective-permute-start.5) | collective-permute-done | bytes 131104 | tf_op jit(solution)/shard_map/ppermute | solution.py:491
  28.4 2.2 %collective-permute-done.6.refs_2_ = bf16[64,1024]{1,0:T(8,128)(2,1)S(1)} collective-permute-done((bf16[64,1024]{1,0:T(8,128)(2,1)S(1)}, bf16[64,1024]{1,0:T(8,128)(2,1)S(1)}, u32[]{:S(2)}, u32[]{:S(2)}) %collective-permute-start.6) | collective-permute-done | bytes 131104 | tf_op jit(solution)/shard_map/ppermute | solution.py:491
  30.6 1.1 %collective-permute-done.7.refs_3_ = bf16[64,1024]{1,0:T(8,128)(2,1)S(1)} collective-permute-done((bf16[64,1024]{1,0:T(8,128)(2,1)S(1)}, bf16[64,1024]{1,0:T(8,128)(2,1)S(1)}, u32[]{:S(2)}, u32[]{:S(2)}) %collective-permute-start.7) | collective-permute-done | bytes 131104 | tf_op jit(solution)/shard_map/ppermute | solution.py:491
  31.7 0.4 partial.1
  32.2 0.1 collective-permute-start.8
  32.3 0.9 %token_.1 = (bf16[4,16,512]{2,1,0:T(8,128)(2,1)S(1)}, bf16[64,512]{1,0:T(8,128)(2,1)S(1)}) custom-call(bf16[128,512]{1,0:T(8,128)(2,1)S(1)} %get-tuple-element.44.refs_0_, bf16[2,48,512]{2,1,0:T(8,128)(2,1)S(1)} %get-tuple-element.46.refs_2_.refs_1_, bf16[3,64,512]{2,1,0:T(8,128)(2,1)S(1)} %get-tuple-element.65.refs_2_, ...), custom_call_target="tpu_custom_call" | custom-call | tf_op jit(solution)/shard_map/token/pallas_call | solution.py:462
  33.2 0.6 %collective-permute-done.8.refs_1_ = bf16[256,512]{1,0:T(8,128)(2,1)S(1)} collective-permute-done((bf16[256,512]{1,0:T(8,128)(2,1)S(1)}, bf16[256,512]{1,0:T(8,128)(2,1)S(1)}, u32[]{:S(2)}, u32[]{:S(2)}) %collective-permute-start.8) | collective-permute-done | bytes 262176 | tf_op jit(solution)/shard_map/ppermute | solution.py:491
  33.8 0.1 scatter.1
  33.9 0.6 %collective-permute-start.9 = (bf16[80,512]{1,0:T(8,128)(2,1)S(1)}, bf16[80,512]{1,0:T(8,128)(2,1)S(1)}, u32[]{:S(2)}, u32[]{:S(2)}) collective-permute-start(bf16[80,512]{1,0:T(8,128)(2,1)S(1)} %get-tuple-element.69), channel_id=1, source_target_pairs={{0,1},{1,0},{2,3},{3,2},{4,5},{5,4},{6,7},{7,6},{8,9},{9,8},{10,11... | collective-permute-start | bytes 245768 | tf_op jit(solution)/shard_map/ppermute | solution.py:491
  34.5 1.9 %collective-permute-start.10 = (bf16[80,512]{1,0:T(8,128)(2,1)S(1)}, bf16[80,512]{1,0:T(8,128)(2,1)S(1)}, u32[]{:S(2)}, u32[]{:S(2)}) collective-permute-start(bf16[80,512]{1,0:T(8,128)(2,1)S(1)} %get-tuple-element.70), channel_id=1, source_target_pairs={{0,2},{1,3},{2,0},{3,1},{4,6},{5,7},{6,4},{7,5},{8,10},{9,11},{10,... | collective-permute-start | bytes 245768 | tf_op jit(solution)/shard_map/ppermute | solution.py:491
  36.4 2.0 %collective-permute-start.11 = (bf16[80,512]{1,0:T(8,128)(2,1)S(1)}, bf16[80,512]{1,0:T(8,128)(2,1)S(1)}, u32[]{:S(2)}, u32[]{:S(2)}) collective-permute-start(bf16[80,512]{1,0:T(8,128)(2,1)S(1)} %get-tuple-element.71), channel_id=1, source_target_pairs={{0,3},{1,2},{2,1},{3,0},{4,7},{5,6},{6,5},{7,4},{8,11},{9,10},{10,... | collective-permute-start | bytes 245768 | tf_op jit(solution)/shard_map/ppermute | solution.py:491
  38.3 0.6 %reshape.17 = bf16[2,8,4,512]{3,2,1,0:T(4,128)(2,1)} reshape(bf16[64,512]{1,0:T(8,128)(2,1)S(1)} %get-tuple-element.73) | data formatting | bytes 131072 | tf_op jit(solution)/shard_map/reshape | solution.py:611
  39.0 0.3 collective-permute-done.9.refs_2_
  39.3 4.6 %collective-permute-done.10.refs_3_ = bf16[80,512]{1,0:T(8,128)(2,1)S(1)} collective-permute-done((bf16[80,512]{1,0:T(8,128)(2,1)S(1)}, bf16[80,512]{1,0:T(8,128)(2,1)S(1)}, u32[]{:S(2)}, u32[]{:S(2)}) %collective-permute-start.10) | collective-permute-done | bytes 81952 | tf_op jit(solution)/shard_map/ppermute | solution.py:491
  43.9 0.0 collective-permute-done.11.refs_4_
  43.9 0.8 %final.1 = (f32[64,512]{1,0:T(8,128)}, bf16[64,512]{1,0:T(8,128)(2,1)}) custom-call(f32[64,512]{1,0:T(8,128)S(1)} %get-tuple-element.68.refs_0_, bf16[4,16,512]{2,1,0:T(8,128)(2,1)S(1)} %get-tuple-element.67.refs_2_.refs_1_, bf16[80,512]{1,0:T(8,128)(2,1)S(1)} %collective-permute-done.9.refs_2_, bf16[80,512]{1,0:T(8,128)(2,1)S(1)} %collective-permute-done.10.refs_3_, ...), custom_call_target="tpu_custom_call" | custom-call | tf_op jit(solution)/shard_map/final/pallas_call | solution.py:462
Async XLA Ops:
  1.8 10.6 %collective-permute-start = (bf16[56,512]{1,0:T(8,128)(2,1)S(1)}, bf16[56,512]{1,0:T(8,128)(2,1)S(1)}, u32[]{:S(2)}, u32[]{:S(2)}) collective-permute-start(bf16[56,512]{1,0:T(8,128)(2,1)S(1)} %get-tuple-element.41), channel_id=1, source_target_pairs={{0,1},{1,0},{2,3},{3,2},{4,5},{5,4},{6,7},{7,6},{8,9},{9,8},{10,11... | collective-permute-start | bytes 172040 | tf_op jit(solution)/shard_map/ppermute | solution.py:491
  4.9 7.5 %collective-permute-start.2 = (bf16[56,512]{1,0:T(8,128)(2,1)S(1)}, bf16[56,512]{1,0:T(8,128)(2,1)S(1)}, u32[]{:S(2)}, u32[]{:S(2)}) collective-permute-start(bf16[56,512]{1,0:T(8,128)(2,1)S(1)} %get-tuple-element.43), channel_id=1, source_target_pairs={{0,3},{1,2},{2,1},{3,0},{4,7},{5,6},{6,5},{7,4},{8,11},{9,10},{10,... | collective-permute-start | bytes 172040 | tf_op jit(solution)/shard_map/ppermute | solution.py:491
  7.4 5.0 %collective-permute-start.1 = (bf16[24,512]{1,0:T(8,128)(2,1)S(1)}, bf16[24,512]{1,0:T(8,128)(2,1)S(1)}, u32[]{:S(2)}, u32[]{:S(2)}) collective-permute-start(bf16[24,512]{1,0:T(8,128)(2,1)S(1)} %get-tuple-element.42), channel_id=1, source_target_pairs={{0,2},{1,3},{2,0},{3,1},{4,6},{5,7},{6,4},{7,5},{8,10},{9,11},{10,... | collective-permute-start | bytes 73736 | tf_op jit(solution)/shard_map/ppermute | solution.py:491
  12.6 2.6 %collective-permute-start.4 = (bf16[176,512]{1,0:T(8,128)(2,1)S(1)}, bf16[176,512]{1,0:T(8,128)(2,1)S(1)}, u32[]{:S(2)}, u32[]{:S(2)}) collective-permute-start(bf16[176,512]{1,0:T(8,128)(2,1)S(1)} %get-tuple-element.47), channel_id=1, source_target_pairs={{0,4},{4,0},{8,12},{12,8},{16,20},{20,16},{24,28},{28,24},{1,5},{5... | collective-permute-start | bytes 540680 | tf_op jit(solution)/shard_map/ppermute | solution.py:521
  12.7 7.1 %collective-permute-start.3 = (bf16[176,512]{1,0:T(8,128)(2,1)S(1)}, bf16[176,512]{1,0:T(8,128)(2,1)S(1)}, u32[]{:S(2)}, u32[]{:S(2)}) collective-permute-start(bf16[176,512]{1,0:T(8,128)(2,1)S(1)} %get-tuple-element.45), channel_id=1, source_target_pairs={{28,0},{4,8},{12,16},{20,24},{0,28},{8,4},{16,12},{24,20},{29,1},{... | collective-permute-start | bytes 540680 | tf_op jit(solution)/shard_map/ppermute | solution.py:522
  22.5 5.9 %collective-permute-start.5 = (bf16[64,1024]{1,0:T(8,128)(2,1)S(1)}, bf16[64,1024]{1,0:T(8,128)(2,1)S(1)}, u32[]{:S(2)}, u32[]{:S(2)}) collective-permute-start(bf16[64,1024]{1,0:T(8,128)(2,1)S(1)} %get-tuple-element.60), channel_id=1, source_target_pairs={{0,8},{4,12},{8,0},{12,4},{16,24},{20,28},{24,16},{28,20},{1,9},{5... | collective-permute-start | bytes 393224 | tf_op jit(solution)/shard_map/ppermute | solution.py:491
  22.6 8.0 %collective-permute-start.6 = (bf16[64,1024]{1,0:T(8,128)(2,1)S(1)}, bf16[64,1024]{1,0:T(8,128)(2,1)S(1)}, u32[]{:S(2)}, u32[]{:S(2)}) collective-permute-start(bf16[64,1024]{1,0:T(8,128)(2,1)S(1)} %get-tuple-element.61), channel_id=1, source_target_pairs={{0,16},{4,20},{8,24},{12,28},{16,0},{20,4},{24,8},{28,12},{1,17},{... | collective-permute-start | bytes 393224 | tf_op jit(solution)/shard_map/ppermute | solution.py:491
  24.8 6.9 %collective-permute-start.7 = (bf16[64,1024]{1,0:T(8,128)(2,1)S(1)}, bf16[64,1024]{1,0:T(8,128)(2,1)S(1)}, u32[]{:S(2)}, u32[]{:S(2)}) collective-permute-start(bf16[64,1024]{1,0:T(8,128)(2,1)S(1)} %get-tuple-element.62), channel_id=1, source_target_pairs={{0,24},{4,28},{8,16},{12,20},{16,8},{20,12},{24,0},{28,4},{1,25},{... | collective-permute-start | bytes 393224 | tf_op jit(solution)/shard_map/ppermute | solution.py:491
  32.2 1.6 %collective-permute-start.8 = (bf16[256,512]{1,0:T(8,128)(2,1)S(1)}, bf16[256,512]{1,0:T(8,128)(2,1)S(1)}, u32[]{:S(2)}, u32[]{:S(2)}) collective-permute-start(bf16[256,512]{1,0:T(8,128)(2,1)S(1)} %get-tuple-element.64), channel_id=1, source_target_pairs={{0,4},{4,0},{8,12},{12,8},{16,20},{20,16},{24,28},{28,24},{1,5},{5... | collective-permute-start | bytes 786440 | tf_op jit(solution)/shard_map/ppermute | solution.py:491
  33.9 5.4 %collective-permute-start.9 = (bf16[80,512]{1,0:T(8,128)(2,1)S(1)}, bf16[80,512]{1,0:T(8,128)(2,1)S(1)}, u32[]{:S(2)}, u32[]{:S(2)}) collective-permute-start(bf16[80,512]{1,0:T(8,128)(2,1)S(1)} %get-tuple-element.69), channel_id=1, source_target_pairs={{0,1},{1,0},{2,3},{3,2},{4,5},{5,4},{6,7},{7,6},{8,9},{9,8},{10,11... | collective-permute-start | bytes 245768 | tf_op jit(solution)/shard_map/ppermute | solution.py:491
  34.5 9.5 %collective-permute-start.10 = (bf16[80,512]{1,0:T(8,128)(2,1)S(1)}, bf16[80,512]{1,0:T(8,128)(2,1)S(1)}, u32[]{:S(2)}, u32[]{:S(2)}) collective-permute-start(bf16[80,512]{1,0:T(8,128)(2,1)S(1)} %get-tuple-element.70), channel_id=1, source_target_pairs={{0,2},{1,3},{2,0},{3,1},{4,6},{5,7},{6,4},{7,5},{8,10},{9,11},{10,... | collective-permute-start | bytes 245768 | tf_op jit(solution)/shard_map/ppermute | solution.py:491
  36.4 7.6 %collective-permute-start.11 = (bf16[80,512]{1,0:T(8,128)(2,1)S(1)}, bf16[80,512]{1,0:T(8,128)(2,1)S(1)}, u32[]{:S(2)}, u32[]{:S(2)}) collective-permute-start(bf16[80,512]{1,0:T(8,128)(2,1)S(1)} %get-tuple-element.71), channel_id=1, source_target_pairs={{0,3},{1,2},{2,1},{3,0},{4,7},{5,6},{6,5},{7,4},{8,11},{9,10},{10,... | collective-permute-start | bytes 245768 | tf_op jit(solution)/shard_map/ppermute | solution.py:491
